TPU v7x, 32 devices: a whole 2x2x4 slice. The times are simulated.
32 devices in a mesh: dp: 4 (over x, core), tm: 8 (over z, y).
Axes of the slice: x: 2, y: 2, z: 4, core: 2. Of those that a mesh axis runs over, the one named last changes fastest.
Arguments:
- latent: float32 [4, 64, 4096], P('dp', None, 'tm'), may hold values from -40 to 40
- target: float32 [4, 8192], P('dp', 'tm'), may hold values from -20 to 20
- up_kernel: float32 [4, 32, 64], replicated, may hold values from -0.5 to 0.5
- inner_kernel: float32 [3, 16, 32], replicated, may hold values from -0.625 to 0.625
- outer_kernel: float32 [32, 16], replicated, may hold values from -1.5 to 1.5
- out_kernel: float32 [7, 32], replicated, may hold values from -0.375 to 0.375
Outputs:
- latent_grad: float32 [4, 64, 4096], P('dp', None, 'tm')
- up_update: float32 [4, 32, 64], replicated
- inner_update: float32 [3, 16, 32], replicated
- outer_update: float32 [32, 16], replicated
- out_update: float32 [7, 32], replicated
All inputs are finite; a program needn't handle non-finite values.
Results may differ from a plain program's by a relative error of at most 0.0003.
Values sent between devices are 32-bit elements; how exact they have to be, the bound alone decides.
No kernel may reach another device: no remote copies, remote signals or barrier semaphores. Data moves between devices by JAX's collectives and lax.ppermute only.
A program may use at most 64 MiB of HBM per device.

v0:
```python
import jax
import jax.numpy as jnp
from jax import lax
from jax.sharding import PartitionSpec as P

MELS = 64
WIN_COARSE = 1024
WIN_FINE = 256


LOSS_WEIGHTS = (0.25, 0.5, 0.5)


def padded_2(cells, sides, width):
    for axis, dim in sides:
        count = lax.axis_size(axis)
        ends = count - 1
        head = lax.slice_in_dim(cells, 0, width, axis=dim)
        tail = lax.slice_in_dim(cells, cells.shape[dim] - width, cells.shape[dim], axis=dim)
        cells = jnp.concatenate(
            [
                lax.ppermute(tail, axis, [(i, (i + 1) % count) for i in range(ends)]),
                cells,
                lax.ppermute(head, axis, [((i + 1) % count, i) for i in range(ends)]),
            ],
            axis=dim,
        )
    return cells


def from_behind(x, axis, by):
    peers = lax.axis_size(axis)
    pairs = [(i, i + by) for i in range(peers) if 0 <= i + by < peers]
    return lax.ppermute(x, axis, pairs)


def product(form, left, right):
    return jnp.einsum(
        form, left, right, precision=lax.Precision.HIGHEST, preferred_element_type=jnp.float32
    )


def mel_bank(window, mel_count):
    half_window = window // 2
    top_mel = 2595.0 * jnp.log10(1.0 + 12000.0 / 700.0)
    points = (jnp.arange(mel_count + 1, dtype=jnp.float32) + 1.0) / (mel_count + 2.0) * top_mel
    centers = 700.0 * (jnp.power(10.0, points / 2595.0) - 1.0) / 12000.0 * half_window
    spacing = jnp.maximum(centers[1:] - centers[:-1], 1.0)
    places = jnp.arange(half_window, dtype=jnp.float32)[:, None]
    return jnp.maximum(0.0, 1.0 - jnp.abs(places - centers[None, :mel_count]) / spacing[None, :])


def dft_table(window):
    half_window = window // 2
    sample = jnp.arange(window, dtype=jnp.int32)[:, None]
    freq_index = jnp.arange(half_window, dtype=jnp.int32)[None, :]
    angles = (sample * freq_index % window).astype(jnp.float32) * (2.0 * jnp.pi / window)
    hann_taper = 0.5 - 0.5 * jnp.cos(sample.astype(jnp.float32) * (2.0 * jnp.pi / window))
    return jnp.concatenate([hann_taper * jnp.cos(angles), -hann_taper * jnp.sin(angles)], axis=1)


def framed(signal, window, frame_count):
    hop_size = window // 4
    blocks = signal.reshape(signal.shape[:-1] + (frame_count + 3, hop_size))
    return jnp.concatenate(
        [blocks[..., offset : offset + frame_count, :] for offset in range(4)], axis=-1
    )


def mel_energy(signal, window, frame_count):
    frames = framed(signal, window, frame_count)
    spectra = product("...nf,fk->...nk", frames, dft_table(window))
    half_window = window // 2
    energy = spectra[..., :half_window] ** 2 + spectra[..., half_window:] ** 2
    return product("...nk,km->...nm", energy, mel_bank(window, MELS))


def spectral_loss(signal, target_mel, window, frame_count):
    level = jnp.sqrt(mel_energy(signal, window, frame_count) + 1.0)
    return jnp.sum((level - jnp.sqrt(target_mel + 1.0)) ** 2)


def elu_slope(values):
    return jnp.where(values > 0, 1.0, jnp.exp(jnp.minimum(values, 0.0)))


def apply_mask(values, mask):
    return values * mask


def upsample_forward(values, kernel, stride, previous):
    lagged = jnp.concatenate([previous, values[:, :, :-1]], axis=2)
    phases = product("pij,bjm->bimp", kernel[:stride], values) + product(
        "pij,bjm->bimp", kernel[stride:], lagged
    )
    return (phases.reshape(phases.shape[0], phases.shape[1], -1), lagged)


def taps_forward(padded, kernel, length):
    summed = product("oi,bil->bol", kernel[0], padded[:, :, :length])
    for offset in range(1, kernel.shape[0]):
        summed = summed + product(
            "oi,bil->bol", kernel[offset], padded[:, :, offset : offset + length]
        )
    return summed


def decode_forward(activated, weights, movers, clip_mask):
    up_kernel, inner_kernel, outer_kernel, out_kernel = weights
    lend_frame, border_inner, border_output = movers
    upper, lagged = upsample_forward(activated, up_kernel, 2, lend_frame(activated[:, :, -1:]))
    upper = apply_mask(upper, clip_mask)
    padded_inner = border_inner(jax.nn.elu(upper))
    inner_out = taps_forward(padded_inner, inner_kernel, upper.shape[2])
    hidden = jax.nn.elu(inner_out)
    mixed = apply_mask(upper + product("oi,bil->bol", outer_kernel, hidden), clip_mask)
    padded_output = border_output(jax.nn.elu(mixed))
    waveform = taps_forward(padded_output, out_kernel[:, None, :], upper.shape[2])[:, 0, :]
    return (waveform, (upper, lagged, padded_inner, inner_out, hidden, mixed, padded_output))


def taps_backward(grad_out, padded, kernel, length, keep):
    tap_count = kernel.shape[0]
    row_grad = apply_mask(grad_out, keep)
    kernel_rows = jnp.stack(
        [
            product("nbol,bil->nboi", row_grad, padded[:, :, offset : offset + length])
            for offset in range(tap_count)
        ],
        axis=2,
    )
    spread = jnp.zeros(grad_out.shape[:2] + (kernel.shape[2], length + tap_count - 1), jnp.float32)
    for offset in range(tap_count):
        moved = product("oi,nbol->nbil", kernel[offset], grad_out)
        spread = spread + jnp.pad(moved, ((0, 0), (0, 0), (0, 0), (offset, tap_count - 1 - offset)))
    return (kernel_rows, spread)


def rims_backward(spread, rim_width):
    interior = spread[..., rim_width:-rim_width]
    return interior


def residual_backward(
    grad_mixed, upper, padded, inner_out, hidden, inner_kernel, outer_kernel, keep
):
    length = upper.shape[-1]
    outer_rows = product("nbol,bil->nboi", apply_mask(grad_mixed, keep), hidden)
    grad_inner = product("oi,nbol->nbil", outer_kernel, grad_mixed) * elu_slope(inner_out)
    inner_rows, spread = taps_backward(grad_inner, padded, inner_kernel, length, keep)
    grad_rectified = rims_backward(spread, 1)
    return (grad_mixed + grad_rectified * elu_slope(upper), inner_rows, outer_rows)


def upsample_backward(grad_upper, values, lagged, kernel, stride, keep):
    phase_shape = grad_upper.shape[:3] + (values.shape[-1], stride)
    grad_phase = grad_upper.reshape(phase_shape)
    row_phase = apply_mask(grad_upper, keep).reshape(phase_shape)
    first_rows = product("nbimp,bjm->nbpij", row_phase, values)
    second_rows = product("nbimp,bjm->nbpij", row_phase, lagged)
    grad_values = product("pij,nbimp->nbjm", kernel[:stride], grad_phase)
    grad_lagged = product("pij,nbimp->nbjm", kernel[stride:], grad_phase)
    arrived = jnp.zeros_like(grad_lagged[..., :1])
    grad_values = grad_values + jnp.concatenate([grad_lagged[..., 1:], arrived], axis=-1)
    return (grad_values, jnp.concatenate([first_rows, second_rows], axis=2))


def local(latent, target, up_kernel, inner_kernel, outer_kernel, out_kernel):
    weights = (up_kernel, inner_kernel, outer_kernel, out_kernel)
    clips_here = target.shape[0]
    samples = target.shape[1]
    frames_here = latent.shape[2]
    latent_in = padded_2(latent, (("tm", 2),), 4)
    start_frame = 4
    margin = 8

    def lend_frame(edge):
        return jnp.zeros_like(edge)

    def border_inner(values):
        return jnp.pad(values, ((0, 0), (0, 0), (1, 1)))

    def border_output(values):
        return jnp.pad(values, ((0, 0), (0, 0), (3, 3)))

    shard_index = lax.axis_index("tm")
    shard_total = lax.axis_size("tm")
    wide_length = samples + 2 * margin
    local_places = jnp.arange(wide_length, dtype=jnp.int32)
    clip_places = samples * shard_index - margin + local_places
    clip_mask = ((clip_places >= 0) & (clip_places < samples * shard_total)).astype(jnp.float32)
    keep_rows = ((local_places >= margin) & (local_places < margin + samples)).astype(jnp.float32)
    activated = jax.nn.elu(latent_in)
    wave_all, saved = decode_forward(
        activated, weights, (lend_frame, border_inner, border_output), clip_mask
    )
    upper, lagged, padded_inner, inner_out, hidden, mixed, padded_output = saved
    waveform = wave_all[:, margin : margin + samples]
    tail_length = 3 * WIN_COARSE // 4
    wave_next, target_next = from_behind(
        (waveform[:, :tail_length], target[:, :tail_length]), "tm", -1
    )
    long_wave = jnp.concatenate([waveform, wave_next], axis=1)
    long_target = jnp.concatenate([target, target_next], axis=1)
    gradients = [2.0 * (waveform - target)]
    tails = []
    for window in (WIN_COARSE, WIN_FINE):
        hop_size = window // 4
        frame_count = samples // hop_size
        span = samples + 3 * hop_size
        target_mel = mel_energy(long_target[:, :span], window, frame_count)

        def scale_loss(signal):
            return spectral_loss(signal, target_mel, window, frame_count)

        local_grad = jax.grad(scale_loss)(long_wave[:, :span])
        gradients.append(local_grad[:, :samples])
        tails.append(jnp.pad(local_grad[:, samples:], ((0, 0), (0, tail_length - 3 * hop_size))))
    coarse_in, fine_in = from_behind((tails[0], tails[1]), "tm", 1)
    gradients[1] = gradients[1] + jnp.pad(coarse_in, ((0, 0), (0, samples - tail_length)))
    gradients[2] = gradients[2] + jnp.pad(fine_in, ((0, 0), (0, samples - tail_length)))
    squares = jnp.stack([jnp.sum(member * member, axis=1) for member in gradients], axis=1)
    squares = lax.psum(squares, "tm")
    total_samples = samples * lax.axis_size("tm")
    grad_scale = jnp.asarray(LOSS_WEIGHTS, jnp.float32)[None, :] / jnp.sqrt(
        squares / total_samples + 1e-06
    )
    streams = (
        gradients[0] * grad_scale[:, 0, None]
        + gradients[1] * grad_scale[:, 1, None]
        + gradients[2] * grad_scale[:, 2, None]
    )[None]
    row_weights = jnp.ones((1, clips_here), jnp.float32)
    streams_wide = padded_2(streams, (("tm", 2),), 8)
    wave_length = mixed.shape[2]
    out_taps = out_kernel[:, None, :]
    kernel_rows_out, spread_out = taps_backward(
        streams_wide[:, :, None, :], padded_output, out_taps, wave_length, keep_rows
    )
    out_rows = kernel_rows_out[:, :, :, 0, :]
    grad_final = rims_backward(spread_out, 3)
    grad_mixed = apply_mask(grad_final * elu_slope(mixed), clip_mask)
    grad_upper, inner_rows, outer_rows = residual_backward(
        grad_mixed, upper, padded_inner, inner_out, hidden, inner_kernel, outer_kernel, keep_rows
    )
    grad_activated, up_rows = upsample_backward(
        apply_mask(grad_upper, clip_mask), activated, lagged, up_kernel, 2, keep_rows
    )
    grad_latent_rows = grad_activated[..., start_frame : start_frame + frames_here] * elu_slope(
        latent
    )
    latent_grad = product("nb,nbcm->bcm", row_weights, grad_latent_rows)
    local_totals = [
        product("nb,nb...->...", row_weights, member)
        for member in (up_rows, inner_rows, outer_rows, out_rows)
    ]
    param_count = sum((member.size for member in local_totals))
    summed = lax.psum(
        (local_totals[0], local_totals[1], local_totals[2], local_totals[3]), ("dp", "tm")
    )
    squares_all = sum((jnp.sum(member * member) for member in summed))
    factor = jnp.minimum(1.0, 1.0 / jnp.sqrt(squares_all / param_count + 1e-06))
    updates = [member * factor for member in summed]
    return (latent_grad, updates[0], updates[1], updates[2], updates[3])


def solution(mesh):
    placed = (P("dp", None, "tm"), P("dp", "tm"), P(), P(), P(), P())
    return jax.shard_map(
        local,
        mesh=mesh,
        in_specs=placed,
        out_specs=(P("dp", None, "tm"), P(), P(), P(), P()),
        check_vma=False,
    )
```

profile of v0, /device:TPU:0, one launch (start us, length us, event | category | flops | bytes accessed | tf_op | source)
XLA Modules:
  0.0 188.2 jit_solution(7671481007626582187)
XLA Ops:
  4.1 5.5 %collective-permute-start = (f32[1,64,4]{2,1,0:T(8,128)S(1)}, f32[1,64,4]{2,1,0:T(8,128)S(1)}, u32[]{:S(2)}, u32[]{:S(2)}) collective-permute-start(f32[1,64,4]{2,1,0:T(8,128)S(1)} %get-tuple-element.15), channel_id=1, source_target_pairs={{0,1},{1,2},{2,3},{3,4},{4,5},{5,6},{6,7},{8,9},{9,10},{10,11},{11... | collective-permute-start | bytes 3080 | tf_op jit(solution)/shard_map/ppermute | solution.py:22
  9.6 1.3 collective-permute-start.1
  12.3 1.6 slice_bitcast_fusion.6
  15.1 9.4 %sine_multiply_fusion = (f32[1024,512]{1,0:T(8,128)S(1)}, f32[1024,512]{1,0:T(8,128)}) fusion(f32[1024]{0:T(1024)S(1)} %fusion.218, f32[1024]{0:T(1024)S(1)} %multiply_subtract_fusion), kind=kLoop, calls=%fused_computation.21 | loop fusion | flops 8388608 | bytes 4202496 | tf_op jit(solution)/shard_map/jvp()/mul | solution.py:59
  31.4 1.3 compare_select_fusion.9
  39.6 2.0 %multiply_reduce_fusion.6 = (f32[]{:T(128)}, f32[1,1024]{1,0:T(1,128)}, f32[1,1792]{1,0:T(1,128)S(1)}) fusion(f32[1,1024]{1,0:T(1,128)} %param.8, f32[1,1040]{1,0:T(1,128)S(1)} %squeeze.11), kind=kLoop, calls=%fused_computation.340 | loop fusion | flops 4094 | bytes 16388 | tf_op jit(solution)/shard_map/reduce_sum | solution.py:222
  45.4 1.3 reduce.11
  48.0 1.4 reshape.970
  51.1 4.3 %fusion.15 = f32[1,4,1024]{2,1,0:T(4,128)} fusion(f32[1024,512]{1,0:T(8,128)S(1)} %get-tuple-element.77, f32[1024,512]{1,0:T(8,128)} %get-tuple-element.78, f32[1,4,256]{2,1,0:T(4,128)S(1)} %get-tuple-element.45, f32[1,4,256]{2,1,0:T(4,128)S(1)} %get-tuple-element.46, f32[1,4,256]{2,1,0:T(4,128)S(1)} %get-tuple-element.47, ...), kind=kOutput, calls=%fused_computation.33 | convolution fusion | flops 51392512 | bytes 4227072 | tf_op jit(solution)/shard_map/...nf,fk->...nk/dot_general | solution.py:38
  56.3 1.3 maximum_reduce_fusion
  57.6 1.3 reshape.959
  58.9 1.3 fusion.210
  60.2 1.4 reshape.967
  61.6 1.4 fusion.285
  69.7 1.4 reshape.974
  71.7 6.2 %collective-permute-start.5 = (f32[1,768]{1,0:T(1,128)S(1)}, f32[1,768]{1,0:T(1,128)S(1)}, u32[]{:S(2)}, u32[]{:S(2)}) collective-permute-start(f32[1,768]{1,0:T(1,128)S(1)} %pad.112), channel_id=1, source_target_pairs={{0,1},{1,2},{2,3},{3,4},{4,5},{5,6},{6,7},{8,9},{9,10},{10,11},{11... | collective-permute-start | bytes 9224 | tf_op jit(solution)/shard_map/ppermute | solution.py:34
  78.0 3.7 %fusion.14 = f32[1,4,1024]{2,1,0:T(4,128)S(1)} fusion(f32[1024,512]{1,0:T(8,128)S(1)} %get-tuple-element.77, f32[1024,512]{1,0:T(8,128)} %get-tuple-element.78, f32[1,4,256]{2,1,0:T(4,128)} %get-tuple-element.49, f32[1,4,256]{2,1,0:T(4,128)} %get-tuple-element.50, f32[1,4,256]{2,1,0:T(4,128)} %get-tuple-element.51, f32[1,4,256]{2,1,0:T(4,128)} %get-tuple-element.48), kind=kOutput, calls=%fused_computation.32 | convolution fusion | flops 51392512 | bytes 4227072 | tf_op jit(solution)/shard_map/jvp(...nf,fk->...nk)/dot_general | solution.py:38
  83.3 3.5 %fusion.16 = f32[1,4,1024]{2,1,0:T(4,128)S(1)} fusion(f32[1024,512]{1,0:T(8,128)S(1)} %get-tuple-element.77, f32[1024,512]{1,0:T(8,128)S(1)} %copy-done.1, f32[1,4,512]{2,1,0:T(4,128)S(1)} %get-tuple-element.18, f32[1,4,512]{2,1,0:T(4,128)S(1)} %get-tuple-element.17), kind=kOutput, calls=%fused_computation.34 | convolution fusion | flops 51384320 | bytes 4227072 | tf_op jit(solution)/shard_map/transpose(jvp(...nf,fk->...nk))/dot_general | solution.py:38
  86.9 5.0 %collective-permute-start.4 = (f32[1,768]{1,0:T(1,128)S(1)}, f32[1,768]{1,0:T(1,128)S(1)}, u32[]{:S(2)}, u32[]{:S(2)}) collective-permute-start(f32[1,768]{1,0:T(1,128)S(1)} %slice.347), channel_id=1, source_target_pairs={{0,1},{1,2},{2,3},{3,4},{4,5},{5,6},{6,7},{8,9},{9,10},{10,11},{11... | collective-permute-start | bytes 9224 | tf_op jit(solution)/shard_map/ppermute | solution.py:34
  93.8 2.0 %pad_maximum_fusion.16 = f32[1,3]{1,0:T(1,128)S(1)} fusion(f32[1,1]{1,0:T(1,128)} %bitcast.63, f32[1,1]{1,0:T(1,128)} %bitcast.53, f32[1,1]{1,0:T(1,128)} %bitcast.43), kind=kLoop, calls=%fused_computation.344 | loop fusion | flops 6 | bytes 24 | tf_op jit(solution)/shard_map/stack | solution.py:222
  96.0 22.0 %psum.35 = f32[1,3]{1,0:T(1,128)S(1)} all-reduce(f32[1,3]{1,0:T(1,128)S(1)} %pad_maximum_fusion.16), channel_id=1, replica_groups=mesh['dp'=4,'tm'=8] {'tm'}, use_global_device_ids=true, to_apply=%region_3.4 | all-reduce | flops 3 | bytes 24 | tf_op jit(solution)/shard_map/psum | solution.py:223
  119.8 2.1 %add_bitcast_fusion.1 = f32[1,1,1024]{2,1,0:T(1,128)S(1)} fusion(f32[1,1024]{1,0:T(1,128)S(1)} %get-tuple-element.14, f32[1,1024]{1,0:T(1,128)S(1)} %get-tuple-element.12, f32[]{:T(128)} %bitcast.66, f32[]{:T(128)} %bitcast.65, f32[]{:T(128)} %bitcast.64, f32[1,1024]{1,0:T(1,128)} %param.8, f32[1,1040]{1,0:T(1,128)} %copy-done.14), kind=kLoop, calls=%fused_computation.336 | loop fusion | flops 6144 | bytes 20492 | tf_op jit(solution)/shard_map/broadcast_in_dim | solution.py:228
  123.3 4.5 %collective-permute-start.6 = (f32[1,1,8]{2,1,0:T(1,128)S(1)}, f32[1,1,8]{2,1,0:T(1,128)S(1)}, u32[]{:S(2)}, u32[]{:S(2)}) collective-permute-start(f32[1,1,8]{2,1,0:T(1,128)S(1)} %get-tuple-element.62), channel_id=1, source_target_pairs={{0,1},{1,2},{2,3},{3,4},{4,5},{5,6},{6,7},{8,9},{9,10},{10,11},{11... | collective-permute-start | bytes 104 | tf_op jit(solution)/shard_map/ppermute | solution.py:22
  136.8 41.8 %all-reduce.29 = (f32[4,32,64]{2,1,0:T(8,128)S(1)}, f32[3,16,32]{2,1,0:T(8,128)S(1)}, f32[32,16]{0,1:T(8,128)S(1)}, f32[7,32]{1,0:T(8,128)S(1)}) all-reduce(f32[4,32,64]{2,1,0:T(8,128)S(1)} %maximum_bitcast_fusion, f32[3,16,32]{2,1,0:T(8,128)S(1)} %maximum_bitcast_fusion.1, ...), channel_id=1, replica_groups=mesh['dp'=4,'tm'=8] {'dp','tm'}, use_global_device_ids=true, to_apply=%region_4.5 | all-reduce | flops 10464 | bytes 83712 | tf_op jit(solution)/shard_map/psum | solution.py:258
  (165 shorter events, 56.6 us)
Async XLA Ops:
  0.6 30.8 %copy-start = (f32[32,16]{0,1:T(8,128)S(1)}, f32[32,16]{0,1:T(8,128)}, u32[]{:S(2)}) copy-start(f32[32,16]{0,1:T(8,128)} %param.11) | copy-start | bytes 6148
  1.9 41.6 %collective-permute-start.3 = (f32[1,768]{1,0:T(1,128)}, f32[1,768]{1,0:T(1,128)}, u32[]{:S(2)}, u32[]{:S(2)}) collective-permute-start(f32[1,768]{1,0:T(1,128)} %slice.296), channel_id=1, source_target_pairs={{1,0},{2,1},{3,2},{4,3},{5,4},{6,5},{7,6},{9,8},{10,9},{11,10},{12... | collective-permute-start | bytes 9224 | tf_op jit(solution)/shard_map/ppermute | solution.py:34
  4.1 20.5 %collective-permute-start = (f32[1,64,4]{2,1,0:T(8,128)S(1)}, f32[1,64,4]{2,1,0:T(8,128)S(1)}, u32[]{:S(2)}, u32[]{:S(2)}) collective-permute-start(f32[1,64,4]{2,1,0:T(8,128)S(1)} %get-tuple-element.15), channel_id=1, source_target_pairs={{0,1},{1,2},{2,3},{3,4},{4,5},{5,6},{6,7},{8,9},{9,10},{10,11},{11... | collective-permute-start | bytes 3080 | tf_op jit(solution)/shard_map/ppermute | solution.py:22
  9.6 15.0 %collective-permute-start.1 = (f32[1,64,4]{2,1,0:T(8,128)S(1)}, f32[1,64,4]{2,1,0:T(8,128)S(1)}, u32[]{:S(2)}, u32[]{:S(2)}) collective-permute-start(f32[1,64,4]{2,1,0:T(8,128)S(1)} %get-tuple-element.16), channel_id=1, source_target_pairs={{1,0},{2,1},{3,2},{4,3},{5,4},{6,5},{7,6},{9,8},{10,9},{11,10},{12... | collective-permute-start | bytes 3080 | tf_op jit(solution)/shard_map/ppermute | solution.py:24
  15.1 9.5 %copy-start.7 = (f32[1,64,512]{2,1,0:T(8,128)S(1)}, f32[1,64,512]{2,1,0:T(8,128)}, u32[]{:S(2)}) copy-start(f32[1,64,512]{2,1,0:T(8,128)} %param.7) | copy-start | bytes 393220
  15.1 9.5 %copy-start.11 = (f32[4,32,64]{2,1,0:T(8,128)S(1)}, f32[4,32,64]{2,1,0:T(8,128)}, u32[]{:S(2)}) copy-start(f32[4,32,64]{2,1,0:T(8,128)} %param.9) | copy-start | bytes 98308
  32.7 5.9 %copy-start.9 = (f32[1,32,1040]{2,1,0:T(8,128)}, f32[1,32,1040]{2,1,0:T(8,128)S(1)}, u32[]{:S(2)}) copy-start(f32[1,32,1040]{2,1,0:T(8,128)S(1)} %get-tuple-element.74) | copy-start | bytes 399364
  42.3 14.1 %collective-permute-start.2 = (f32[1,768]{1,0:T(1,128)}, f32[1,768]{1,0:T(1,128)}, u32[]{:S(2)}, u32[]{:S(2)}) collective-permute-start(f32[1,768]{1,0:T(1,128)} %slice.333), channel_id=1, source_target_pairs={{1,0},{2,1},{3,2},{4,3},{5,4},{6,5},{7,6},{9,8},{10,9},{11,10},{12... | collective-permute-start | bytes 9224 | tf_op jit(solution)/shard_map/ppermute | solution.py:34
  51.1 4.3 %copy-start.2 = (f32[256,128]{1,0:T(8,128)S(1)}, f32[256,128]{1,0:T(8,128)}, u32[]{:S(2)}) copy-start(f32[256,128]{1,0:T(8,128)} %get-tuple-element.75) | copy-start | bytes 393220
  51.1 4.3 %copy-start.3 = (f32[256,128]{1,0:T(8,128)S(1)}, f32[256,128]{1,0:T(8,128)}, u32[]{:S(2)}) copy-start(f32[256,128]{1,0:T(8,128)} %get-tuple-element.76) | copy-start | bytes 393220
  51.1 5.2 %copy-start.16 = (f32[1,1024]{1,0:T(1,128)S(1)}, f32[1,1024]{1,0:T(1,128)}, u32[]{:S(2)}) copy-start(f32[1,1024]{1,0:T(1,128)} %get-tuple-element.53) | copy-start | bytes 12292
  71.7 20.1 %collective-permute-start.5 = (f32[1,768]{1,0:T(1,128)S(1)}, f32[1,768]{1,0:T(1,128)S(1)}, u32[]{:S(2)}, u32[]{:S(2)}) collective-permute-start(f32[1,768]{1,0:T(1,128)S(1)} %pad.112), channel_id=1, source_target_pairs={{0,1},{1,2},{2,3},{3,4},{4,5},{5,6},{6,7},{8,9},{9,10},{10,11},{11... | collective-permute-start | bytes 9224 | tf_op jit(solution)/shard_map/ppermute | solution.py:34
  78.0 3.7 %copy-start.23 = (f32[64]{0:T(128)S(1)}, f32[64]{0:T(128)}, u32[]{:S(2)}) copy-start(f32[64]{0:T(128)} %get-tuple-element.67) | copy-start | bytes 772
  78.0 3.7 %copy-start.24 = (f32[64]{0:T(128)S(1)}, f32[64]{0:T(128)}, u32[]{:S(2)}) copy-start(f32[64]{0:T(128)} %get-tuple-element.68) | copy-start | bytes 772
  78.0 4.1 %copy-start.22 = (f32[1,4,1024]{2,1,0:T(4,128)S(1)}, f32[1,4,1024]{2,1,0:T(4,128)}, u32[]{:S(2)}) copy-start(f32[1,4,1024]{2,1,0:T(4,128)} %fusion.15) | copy-start | bytes 49156
  83.3 8.6 %copy-start.21 = (f32[1,1216]{1,0:T(1,128)S(1)}, f32[1,1216]{1,0:T(1,128)}, u32[]{:S(2)}) copy-start(f32[1,1216]{1,0:T(1,128)} %reshape.974) | copy-start | bytes 14596
  86.8 43.6 %copy-start.10 = (f32[1,32,1040]{2,1,0:T(8,128)S(1)}, f32[1,32,1040]{2,1,0:T(8,128)}, u32[]{:S(2)}) copy-start(f32[1,32,1040]{2,1,0:T(8,128)} %copy-done.9) | copy-start | bytes 399364
  86.9 6.3 %collective-permute-start.4 = (f32[1,768]{1,0:T(1,128)S(1)}, f32[1,768]{1,0:T(1,128)S(1)}, u32[]{:S(2)}, u32[]{:S(2)}) collective-permute-start(f32[1,768]{1,0:T(1,128)S(1)} %slice.347), channel_id=1, source_target_pairs={{0,1},{1,2},{2,3},{3,4},{4,5},{5,6},{6,7},{8,9},{9,10},{10,11},{11... | collective-permute-start | bytes 9224 | tf_op jit(solution)/shard_map/ppermute | solution.py:34
  122.0 5.8 %collective-permute-start.7 = (f32[1,1,8]{2,1,0:T(1,128)S(1)}, f32[1,1,8]{2,1,0:T(1,128)S(1)}, u32[]{:S(2)}, u32[]{:S(2)}) collective-permute-start(f32[1,1,8]{2,1,0:T(1,128)S(1)} %get-tuple-element.61), channel_id=1, source_target_pairs={{1,0},{2,1},{3,2},{4,3},{5,4},{6,5},{7,6},{9,8},{10,9},{11,10},{12... | collective-permute-start | bytes 104 | tf_op jit(solution)/shard_map/ppermute | solution.py:24
  123.3 5.8 %collective-permute-start.6 = (f32[1,1,8]{2,1,0:T(1,128)S(1)}, f32[1,1,8]{2,1,0:T(1,128)S(1)}, u32[]{:S(2)}, u32[]{:S(2)}) collective-permute-start(f32[1,1,8]{2,1,0:T(1,128)S(1)} %get-tuple-element.62), channel_id=1, source_target_pairs={{0,1},{1,2},{2,3},{3,4},{4,5},{5,6},{6,7},{8,9},{9,10},{10,11},{11... | collective-permute-start | bytes 104 | tf_op jit(solution)/shard_map/ppermute | solution.py:22
  129.2 3.1 %copy-start.13 = (f32[3,16,32]{2,1,0:T(8,128)S(1)}, f32[3,16,32]{2,1,0:T(8,128)}, u32[]{:S(2)}) copy-start(f32[3,16,32]{2,1,0:T(8,128)} %param.10) | copy-start | bytes 18436
  131.2 2.7 %copy-start.5 = (f32[1,64,519]{2,1,0:T(8,128)S(1)}, f32[1,64,519]{2,1,0:T(8,128)}, u32[]{:S(2)}) copy-start(f32[1,64,519]{2,1,0:T(8,128)} %copy-done.4) | copy-start | bytes 398596
  131.7 2.7 %copy-start.8 = (f32[1,64,512]{2,1,0:T(8,128)S(1)}, f32[1,64,512]{2,1,0:T(8,128)}, u32[]{:S(2)}) copy-start(f32[1,64,512]{2,1,0:T(8,128)} %param.7) | copy-start | bytes 393220
  134.0 52.6 %copy-start.12 = (f32[4,32,64]{2,1,0:T(8,128)S(1)}, f32[4,32,64]{2,1,0:T(8,128)}, u32[]{:S(2)}) copy-start(f32[4,32,64]{2,1,0:T(8,128)} %param.9) | copy-start | bytes 98308
  (9 other events, 14.2 us)
where the time goes:
time: 190 us; the launch traced here: 188 us
  blocking collectives  63.8 us (34%)
  matrix products  37.6 us (20%)
  other arithmetic  31.8 us (17%)
  starting transfers between devices  26.4 us (14%)
  local copies, waits for them, and re-layouts  22 us (12%)
  between operations  4.65 us (2%)
  waiting for transfers between devices  1.95 us (1%)
    psum x1, blocking collectives, local(): lax.psum((local_totals[0], local_totals[1], local_totals[2], local_totals...  41.8 us
    dot_general x44, matrix products, product(): jnp.einsum(form, left, right, precision=lax.Precision.HIGHEST, preferred_...  37.6 us
    psum x1, blocking collectives, local(): squares = lax.psum(squares, 'tm')  22 us
    ppermute x4, starting transfers between devices, from_behind(): return lax.ppermute(x, axis, pairs)  13.8 us
    mul x2, other arithmetic, dft_table(): -hann_taper * jnp.sin(angles)  10.7 us
    ppermute x2, starting transfers between devices, padded_2(): lax.ppermute(tail, axis, [(i, (i + 1) % count) for i in range(ends)])  10.1 us
    reshape x5, local copies, waits for them, and re-layouts, framed(): blocks = signal.reshape(signal.shape[:-1] + (frame_count + 3, hop_size))  6.68 us
    slice x4, local copies, waits for them, and re-layouts, framed(): blocks[..., offset:offset + frame_count, :]  4.01 us
  transfers between devices with their start and end apart: 8, of which 2 were waited for; matrix products, arithmetic and copies ran while one was open for 28% of the time, Pallas kernels for 0%

commit v1 on v0

v1 whole, which is shorter than its diff:
```python
import jax
import jax.numpy as jnp
import numpy as np
from jax import lax
from jax.experimental import pallas as pl
from jax.experimental.pallas import tpu as pltpu
from jax.sharding import PartitionSpec as P

MELS = 64
WIN_COARSE = 1024
WIN_FINE = 256
LOSS_WEIGHTS = (0.25, 0.5, 0.5)
LANES = 128
BLOCK = 2 * LANES
STREAMS = 3
F32 = jnp.float32
BF16 = jnp.bfloat16
VMEM = pltpu.MemorySpace.VMEM


def hi_lo(table):
    high = table.astype(np.float32).astype(BF16)
    low = (table - high.astype(np.float64)).astype(np.float32).astype(BF16)
    return high, low


def mel_table(window):
    half = window // 2
    top = 2595.0 * np.log10(1.0 + 12000.0 / 700.0)
    points = (np.arange(MELS + 1) + 1.0) / (MELS + 2.0) * top
    centers = 700.0 * (10.0 ** (points / 2595.0) - 1.0) / 12000.0 * half
    spacing = np.maximum(centers[1:] - centers[:-1], 1.0)
    places = np.arange(half)[:, None]
    return np.maximum(0.0, 1.0 - np.abs(places - centers[None, :MELS]) / spacing[None, :])


def tables():
    order = np.concatenate([np.arange(0, BLOCK, 2), np.arange(1, BLOCK, 2)])
    p = np.arange(LANES)
    cos, sin = [], []
    for rho in range(4):
        angle = 2.0 * np.pi / WIN_COARSE * ((order[:, None] * (4 * p + rho)[None, :]) % WIN_COARSE)
        cos.append(np.cos(angle))
        sin.append(np.sin(angle))
    even = np.concatenate(
        [np.concatenate([cos[0], -sin[0]], 1), np.concatenate([cos[2], -sin[2]], 1)], 0
    )
    odd = np.concatenate(
        [
            np.concatenate([cos[1], -sin[1], cos[3], -sin[3]], 1),
            np.concatenate([-sin[1], -cos[1], sin[3], cos[3]], 1),
        ],
        0,
    )
    angle = 2.0 * np.pi / WIN_FINE * ((order[:, None] * p[None, :]) % WIN_FINE)
    taper = 0.5 - 0.5 * np.cos(2.0 * np.pi / WIN_FINE * order)[:, None]
    fine = np.concatenate([taper * np.cos(angle), -taper * np.sin(angle)], 1)
    coarse_mel = mel_table(WIN_COARSE)
    coarse_mel = np.concatenate([coarse_mel[rho::4] for rho in (0, 2, 1, 3)], 0)
    fine_mel = mel_table(WIN_FINE)
    hann = 0.5 - 0.5 * np.cos(2.0 * np.pi / WIN_COARSE * np.arange(WIN_COARSE))
    hann = hann.reshape(4, BLOCK)[:, order].astype(np.float32)
    hann = np.concatenate([hann, np.zeros_like(hann)], 0)
    deal = np.zeros((BLOCK, BLOCK), np.float32)
    deal[order, np.arange(BLOCK)] = 1.0
    out = [hann, deal.astype(BF16)]
    for table in (even, odd, fine, coarse_mel, fine_mel):
        out += list(hi_lo(table))
    return out


def split(x):
    high = x.astype(BF16)
    return high, (x - high.astype(F32)).astype(BF16)


def stacked(x):
    high = x.astype(BF16).astype(F32)
    return jnp.concatenate([high, x - high], axis=0).astype(BF16)


def dot(left, right, transposed=False):
    dims = (((1,), (1 if transposed else 0,)), ((), ()))
    return lax.dot_general(left, right, dims, preferred_element_type=F32)


def dot3(left, right_high, right_low, transposed=False):
    rows = left.shape[0]
    both = stacked(left)
    first = dot(both, right_high, transposed)
    second = dot(left.astype(BF16), right_low, transposed)
    return first[:rows] + first[rows:] + second


def dot3x(left, right, transposed=False):
    return dot3(left, *split(right), transposed)


def elu_pair(x):
    slope = jnp.exp(jnp.minimum(x, 0.0))
    return jnp.where(x > 0, x, slope - 1.0), slope


def moved(x, by):
    return pltpu.roll(x, by % x.shape[1], 1)


def main_kernel(sizes, *refs):
    (own_ref, first_ref, second_ref, up_ref, inner_ref, outer_ref, out_ref) = refs[:7]
    (hann_ref, deal_ref, even_h, even_l, odd_h, odd_l, fine_h, fine_l) = refs[7:15]
    (cmel_h, cmel_l, fmel_h, fmel_l) = refs[15:19]
    payload_ref, grads_ref = refs[19:21]
    (lat, act, slope_a, a_h, a_l, slope_u, e_h, e_l, slope_c, h_h, h_l, slope_m, g_h, g_l) = refs[21:35]
    (square, wup, kfwd, wblock, shifted, wave_b, targ_b, lanes_b) = refs[35:43]
    channels, half, hidden, frames = sizes
    wide = 3 * frames
    own_blocks = frames // LANES
    index = lax.axis_index("tm")
    count = lax.axis_size("tm")
    odd_place = lax.rem(index, 2) == 1

    first, second = first_ref[...], second_ref[...]
    left_buf = jnp.where(odd_place, first, second)
    right_buf = jnp.where(odd_place, second, first)
    lat[:, 0:frames] = left_buf[:channels]
    lat[:, frames : 2 * frames] = own_ref[0:channels, :]
    lat[:, 2 * frames :] = right_buf[:channels]
    per_row = frames // BLOCK
    for side, rows in enumerate((left_buf, own_ref[...], right_buf)):
        for row in range(2):
            for piece in range(per_row):
                targ_b[pl.ds(side * own_blocks + row * per_row + piece, 1), :] = rows[
                    channels + row : channels + row + 1, piece * BLOCK : (piece + 1) * BLOCK
                ]

    place = lax.broadcasted_iota(jnp.int32, (1, wide), 1) + (index - 1) * frames
    mask = ((place >= 0) & (place < count * frames)).astype(F32)

    for r in range(2):
        wup[r * half : (r + 1) * half, 0:channels] = up_ref[r]
        wup[r * half : (r + 1) * half, channels : 2 * channels] = up_ref[r + 2]
    kfwd[...] = jnp.zeros_like(kfwd)
    square[...] = jnp.zeros_like(square)
    for j in range(3):
        kfwd[0:hidden, j * half : (j + 1) * half] = inner_ref[j]
        kfwd[hidden : 2 * hidden, (j + 1) * half : (j + 2) * half] = inner_ref[j]
        square[(2 - j) * hidden : (3 - j) * hidden, 0:half] = inner_ref[j]
        square[(3 - j) * hidden : (4 - j) * hidden, half : 2 * half] = inner_ref[j]
    back_inner = jnp.transpose(square[...])[0 : 2 * half, 0 : 4 * hidden]
    square[...] = jnp.zeros_like(square)
    square[0:half, 0:hidden] = outer_ref[...]
    square[half : 2 * half, hidden : 2 * hidden] = outer_ref[...]
    outer_fwd = square[0 : 2 * half, 0 : 2 * hidden]
    outer_back = jnp.transpose(square[...])[0 : 2 * hidden, 0 : 2 * half]
    square[...] = jnp.zeros_like(square)
    square[1:8, 0:half] = out_ref[...]
    square[0:7, half : 2 * half] = out_ref[...]
    out_fwd = square[0:8, 0 : 2 * half]
    out_back = jnp.transpose(square[...])[0 : 2 * half, 0:8]
    square[...] = jnp.zeros_like(square)
    for r in range(4):
        square[r * half : (r + 1) * half, 0:channels] = up_ref[r]
    up_back = jnp.transpose(square[...])[0:channels, :]

    activated, slope = elu_pair(lat[...])
    slope_a[...] = slope
    high, low = split(activated)
    a_h[0:channels], a_l[0:channels] = high, low
    high, low = split(moved(activated, 1))
    a_h[channels:], a_l[channels:] = high, low
    upper = dot3(wup[...], a_h[...], a_l[...]) * mask
    rect, slope = elu_pair(upper)
    act[...] = upper
    slope_u[...] = slope
    before, after = moved(rect[half:], 1), moved(rect[:half], -1)
    for at, piece in enumerate((before, rect, after)):
        rows = piece.shape[0]
        start = (0, half, 3 * half)[at]
        high, low = split(piece)
        e_h[start : start + rows], e_l[start : start + rows] = high, low
    inner_out = dot3(kfwd[...], e_h[...], e_l[...])
    hid, slope = elu_pair(inner_out)
    slope_c[...] = slope
    high, low = split(hid)
    h_h[...], h_l[...] = high, low
    mixed = (act[...] + dot3(outer_fwd, h_h[...], h_l[...])) * mask
    rect, slope = elu_pair(mixed)
    slope_m[...] = slope
    high, low = split(rect)
    g_h[...], g_l[...] = high, low
    taps = dot3(out_fwd, g_h[...], g_l[...])
    plus1, plus2, minus1, minus2 = (moved(taps, by) for by in (1, 2, -1, -2))
    wave = [
        (plus2[0:1] + plus1[2:3] + taps[4:5] + minus1[6:7]) * mask,
        (plus1[1:2] + taps[3:4] + minus1[5:6] + minus2[7:8]) * mask,
    ]

    for b in range(3 * own_blocks):
        for r in range(2):
            wave_b[b : b + 1, r * LANES : (r + 1) * LANES] = wave[r][:, b * LANES : (b + 1) * LANES]
    whole = targ_b[...]
    high = whole.astype(BF16)
    rest = whole - high.astype(F32)
    middle = rest.astype(BF16)
    last = (rest - middle.astype(F32)).astype(BF16)
    deal = deal_ref[...]
    targ_b[...] = dot(high, deal) + dot(middle, deal) + dot(last, deal)

    row_count = own_blocks + 4
    start = own_blocks - 3
    parts = []
    for j in range(4):
        rows = jnp.concatenate(
            [wave_b[pl.ds(start + j, row_count), :], targ_b[pl.ds(start + j, row_count), :]], 0
        )
        parts.append(rows * hann_ref[j : j + 1, :])
    even_sum, odd_sum = parts[0] + parts[2], parts[1] + parts[3]
    turned = jnp.concatenate([parts[0] - parts[2], parts[1] - parts[3]], axis=1)
    spec0 = dot3(even_sum + odd_sum, even_h[0:BLOCK], even_l[0:BLOCK])
    spec2 = dot3(even_sum - odd_sum, even_h[BLOCK:], even_l[BLOCK:])
    spec1 = dot3(turned, odd_h[...], odd_l[...])
    real = jnp.concatenate(
        [spec0[:, :LANES], spec2[:, :LANES], spec1[:, :LANES], spec1[:, BLOCK : BLOCK + LANES]], 1
    )
    imag = jnp.concatenate(
        [spec0[:, LANES:], spec2[:, LANES:], spec1[:, LANES:BLOCK], spec1[:, BLOCK + LANES :]], 1
    )
    mel = dot3(real * real + imag * imag, cmel_h[...], cmel_l[...])
    level = jnp.sqrt(mel + 1.0)
    level_wave = level[:row_count]
    frame = lax.broadcasted_iota(jnp.int32, (row_count, MELS), 0) + index * own_blocks - 3
    slope = jnp.where(frame >= 0, (level_wave - level[row_count:]) / level_wave, 0.0)
    push = 2.0 * dot3(slope, cmel_h[...], cmel_l[...], True)
    real, imag = real[:row_count] * push, imag[:row_count] * push
    back0 = dot3(
        jnp.concatenate([real[:, :LANES], imag[:, :LANES]], 1), even_h[0:BLOCK], even_l[0:BLOCK], True
    )
    back2 = dot3(
        jnp.concatenate([real[:, LANES:BLOCK], imag[:, LANES:BLOCK]], 1),
        even_h[BLOCK:],
        even_l[BLOCK:],
        True,
    )
    back1 = dot3(
        jnp.concatenate(
            [
                real[:, BLOCK : BLOCK + LANES],
                imag[:, BLOCK : BLOCK + LANES],
                real[:, BLOCK + LANES :],
                imag[:, BLOCK + LANES :],
            ],
            1,
        ),
        odd_h[...],
        odd_l[...],
        True,
    )
    plus, minus = back0 + back2, back0 - back2
    backs = [
        plus + back1[:, :BLOCK],
        minus + back1[:, BLOCK:],
        plus - back1[:, :BLOCK],
        minus - back1[:, BLOCK:],
    ]
    coarse = jnp.zeros((own_blocks, BLOCK), F32)
    for j in range(4):
        coarse = coarse + (backs[j] * hann_ref[j : j + 1, :])[3 - j : 3 - j + own_blocks]

    hop = LANES // 4
    lane = lax.broadcasted_iota(jnp.int32, (1, LANES), 1)
    start = own_blocks - 1
    for which, source in enumerate((wave_b, targ_b)):
        for s in range(4):
            base = (which * 4 + s) * row_count
            for r in range(2):
                here = source[pl.ds(start, row_count), r * LANES : (r + 1) * LANES]
                if s:
                    there = source[pl.ds(start + 1, row_count), r * LANES : (r + 1) * LANES]
                    here = jnp.where(
                        lane < LANES - s * hop,
                        pltpu.roll(here, LANES - s * hop, 1),
                        pltpu.roll(there, LANES - s * hop, 1),
                    )
                shifted[base : base + row_count, r * LANES : (r + 1) * LANES] = here
    spec = dot3(shifted[...], fine_h[...], fine_l[...])
    real, imag = spec[:, :LANES], spec[:, LANES:]
    mel = dot3(real * real + imag * imag, fmel_h[...], fmel_l[...])
    level = jnp.sqrt(mel + 1.0)
    fine_rows = 4 * row_count
    level_wave = level[:fine_rows]
    row = lax.broadcasted_iota(jnp.int32, (fine_rows, MELS), 0)
    frame = (lax.rem(row, row_count) - 1 + index * own_blocks) * 4 + row // row_count
    slope = jnp.where(frame >= 0, (level_wave - level[fine_rows:]) / level_wave, 0.0)
    push = 2.0 * dot3(slope, fmel_h[...], fmel_l[...], True)
    back = dot3(
        jnp.concatenate([real[:fine_rows] * push, imag[:fine_rows] * push], 1),
        fine_h[...],
        fine_l[...],
        True,
    )
    fine = []
    for r in range(2):
        total = jnp.zeros((own_blocks, LANES), F32)
        for s in range(4):
            piece = back[s * row_count : (s + 1) * row_count, r * LANES : (r + 1) * LANES]
            if s:
                piece = pltpu.roll(piece, s * hop, 1)
                total = total + jnp.where(
                    lane >= s * hop, piece[1 : 1 + own_blocks], piece[0:own_blocks]
                )
            else:
                total = total + piece[1 : 1 + own_blocks]
        fine.append(total)
    fine = jnp.concatenate(fine, axis=1)

    own_rows = pl.ds(own_blocks, own_blocks)
    timed = 2.0 * (wave_b[own_rows, :] - targ_b[own_rows, :])

    window = frames + 2 * LANES
    at = slice(frames - LANES, 2 * frames + LANES)
    mask = mask[:, at]
    totals = []
    edges = []
    for i, stream in enumerate((timed, coarse, fine)):
        totals.append(jnp.sum(stream * stream))
        lanes_b[i] = jnp.zeros((8, window), F32)
        for b in range(own_blocks):
            for r in range(2):
                lanes_b[i, r : r + 1, (b + 1) * LANES : (b + 2) * LANES] = stream[
                    b : b + 1, r * LANES : (r + 1) * LANES
                ]
        evens, odds = lanes_b[i, 0:1, :], lanes_b[i, 1:2, :]
        for k in range(8):
            source = odds if k % 2 else evens
            lanes_b[i, k : k + 1, :] = moved(source, -((4 - k) // 2))
        view = lanes_b[i]
        grad_mixed = dot3x(out_back, view) * slope_m[:, at] * mask
        mixed_h, mixed_l = split(grad_mixed)
        grad_inner = dot3(outer_back, mixed_h, mixed_l) * slope_c[:, at]
        spread = jnp.concatenate(
            [moved(grad_inner[hidden:], 1), grad_inner, moved(grad_inner[:hidden], -1)], 0
        )
        grad_upper = (grad_mixed + dot3x(back_inner, spread) * slope_u[:, at]) * mask
        both = jnp.concatenate([grad_upper, moved(grad_upper, -1)], 0)
        grads = dot3x(up_back, both) * slope_a[:, at] * mask
        grads_ref[i * channels : (i + 1) * channels, :] = grads[:, LANES : LANES + frames]
        before = jnp.transpose(grads[:, 0:LANES])[LANES - 8 :]
        after = jnp.transpose(grads[:, LANES + frames :])[:8]
        edges.append(jnp.concatenate([before, after], axis=1))
        payload_ref[i * 2 * half : (i + 1) * 2 * half, :] = dot3(
            grad_upper, a_h[:, at], a_l[:, at], True
        )
        kern = dot3(grad_inner, e_h[:, at], e_l[:, at], True)
        base = STREAMS * 2 * half + i * hidden
        payload_ref[base : base + hidden, 0 : 3 * half] = (
            kern[:hidden, : 3 * half] + kern[hidden:, half:]
        )
        mix = dot(h_h[:, at], mixed_h, True) + dot(h_l[:, at], mixed_h, True) + dot(h_h[:, at], mixed_l, True)
        payload_ref[base : base + hidden, 3 * half : 4 * half] = (
            mix[:hidden, :half] + mix[hidden:, half:]
        )
        taps = dot3(view, g_h[:, at], g_l[:, at], True)
        wblock[0:7, i * half : (i + 1) * half] = taps[1:8, :half] + taps[0:7, half:]
    base = STREAMS * (2 * half + hidden)
    lane = lax.broadcasted_iota(jnp.int32, (1, half), 1)
    sums = jnp.where(lane == 0, totals[0], jnp.where(lane == 1, totals[1], totals[2]))
    wblock[7:8, :] = jnp.zeros((1, 4 * half), F32)
    wblock[0:7, STREAMS * half :] = jnp.zeros((7, half), F32)
    wblock[7:8, STREAMS * half :] = sums
    payload_ref[base : base + 8, :] = wblock[...]
    payload_ref[base + 8 :, :] = jnp.concatenate(edges, axis=0)


def combine_kernel(sizes, mine_ref, theirs_ref, weights_ref, aux_ref):
    half, hidden, samples = sizes
    rows = STREAMS * (2 * half + hidden)
    total = mine_ref[0 : rows + 8, :] + theirs_ref[0 : rows + 8, :]
    line = total[rows + 7 : rows + 8, :]
    lane = lax.broadcasted_iota(jnp.int32, line.shape, 1) - STREAMS * half
    wanted = jnp.where(lane == 0, LOSS_WEIGHTS[0], jnp.where(lane == 1, LOSS_WEIGHTS[1], LOSS_WEIGHTS[2]))
    line = wanted / jnp.sqrt(line / samples + 1e-06)
    scale = [
        jnp.sum(jnp.where(lane == i, line, 0.0), axis=1, keepdims=True) for i in range(STREAMS)
    ]
    up = sum(total[i * 2 * half : (i + 1) * 2 * half] * scale[i] for i in range(STREAMS))
    base = STREAMS * 2 * half
    inner = sum(total[base + i * hidden : base + (i + 1) * hidden] * scale[i] for i in range(STREAMS))
    last = total[rows : rows + 8]
    out = sum(
        (pltpu.roll(last, (4 - i) * half % (4 * half), 1) if i else last) * scale[i]
        for i in range(STREAMS)
    )
    place = lax.broadcasted_iota(jnp.int32, out.shape, 0)
    lane = lax.broadcasted_iota(jnp.int32, out.shape, 1)
    weights_ref[0 : 2 * half, :] = up
    weights_ref[2 * half : 2 * half + hidden, :] = inner
    weights_ref[2 * half + hidden :, :] = jnp.where((place < 7) & (lane < half), out, 0.0)
    index = lax.axis_index("tm")
    step = lax.axis_size("tm") // 2
    low = lax.rem(index, step)
    edge_lane = lax.broadcasted_iota(jnp.int32, (1, LANES), 1)
    swap = ((low == 0) & (edge_lane >= LANES // 2)) | ((low == step - 1) & (edge_lane < LANES // 2))
    edges = jnp.where(swap, theirs_ref[rows + 8 :, :], mine_ref[rows + 8 :, :])
    aux_ref[0:8, :] = sum(edges[8 * i : 8 * i + 8] * scale[i] for i in range(STREAMS))
    for i in range(STREAMS):
        aux_ref[8 + i : 9 + i, :] = jnp.broadcast_to(scale[i], (1, LANES))


def latent_kernel(channels, grads_ref, aux_ref, square, grad_ref):
    frames = grads_ref.shape[1]
    total = sum(
        grads_ref[i * channels : (i + 1) * channels, :] * aux_ref[8 + i : 9 + i, 0:1]
        for i in range(STREAMS)
    )
    grad_ref[0] = total
    square[...] = jnp.zeros_like(square)
    square[0:8, 0:channels] = aux_ref[0:8, channels:]
    square[LANES - 8 :, channels:] = aux_ref[0:8, 0:channels]
    turned = jnp.transpose(square[...])
    grad_ref[0, :, 0:LANES] = grad_ref[0, :, 0:LANES] + turned[0:channels]
    grad_ref[0, :, frames - LANES :] = grad_ref[0, :, frames - LANES :] + turned[channels:]


def final_kernel(sizes, mine_ref, theirs_ref, up_ref, inner_ref, outer_ref, out_ref, square):
    channels, half, hidden, params = sizes
    total = mine_ref[...] + theirs_ref[...]
    squares = jnp.sum(total * total)
    factor = jnp.minimum(1.0, 1.0 / jnp.sqrt(jnp.full((1, 1), squares / params + 1e-06, F32)))
    total = total * factor
    for r in range(2):
        up_ref[r] = total[r * half : (r + 1) * half, 0:channels]
        up_ref[r + 2] = total[r * half : (r + 1) * half, channels:]
    inner = total[2 * half : 2 * half + hidden]
    for j in range(3):
        inner_ref[j] = inner[:, j * half : (j + 1) * half]
    square[...] = jnp.zeros_like(square)
    square[0:hidden, :] = inner
    outer_ref[...] = jnp.transpose(square[...])[3 * half :, 0:hidden]
    out_ref[...] = total[2 * half + hidden : 2 * half + hidden + 7, 0:half]


def in_vmem(count):
    return [pl.BlockSpec(memory_space=VMEM)] * count


def local(latent, target, up_kernel, inner_kernel, outer_kernel, out_kernel):
    assert latent.shape[0] == 1
    channels, frames = latent.shape[1:]
    half, hidden = outer_kernel.shape
    wide = 3 * frames
    window = frames + 2 * LANES
    blocks = frames // LANES
    count = lax.axis_size("tm")
    samples = target.shape[1] * count
    params = sum(x.size for x in (up_kernel, inner_kernel, outer_kernel, out_kernel))

    own = jnp.concatenate([latent[0], target.reshape(2, frames)], axis=0)
    pairs = [(i, i ^ 1) for i in range(count) if i ^ 1 < count]
    first = lax.ppermute(own, "tm", pairs)
    pairs = [(i, i + 1 if i % 2 else i - 1) for i in range(count)]
    second = lax.ppermute(own, "tm", [(a, b) for a, b in pairs if 0 <= b < count])

    constants = tables()
    rows = STREAMS * (2 * half + hidden)
    scratch = [
        pltpu.VMEM((channels, wide), F32),
        pltpu.VMEM((2 * half, wide), F32),
        pltpu.VMEM((channels, wide), F32),
        pltpu.VMEM((2 * channels, wide), BF16),
        pltpu.VMEM((2 * channels, wide), BF16),
        pltpu.VMEM((2 * half, wide), F32),
        pltpu.VMEM((4 * half, wide), BF16),
        pltpu.VMEM((4 * half, wide), BF16),
        pltpu.VMEM((2 * hidden, wide), F32),
        pltpu.VMEM((2 * hidden, wide), BF16),
        pltpu.VMEM((2 * hidden, wide), BF16),
        pltpu.VMEM((2 * half, wide), F32),
        pltpu.VMEM((2 * half, wide), BF16),
        pltpu.VMEM((2 * half, wide), BF16),
        pltpu.VMEM((LANES, LANES), F32),
        pltpu.VMEM((2 * half, 2 * channels), F32),
        pltpu.VMEM((2 * hidden, 4 * half), F32),
        pltpu.VMEM((8, 4 * half), F32),
        pltpu.VMEM((8 * (blocks + 4), BLOCK), F32),
        pltpu.VMEM((3 * blocks, BLOCK), F32),
        pltpu.VMEM((3 * blocks, BLOCK), F32),
        pltpu.VMEM((STREAMS, 8, window), F32),
    ]
    sizes = (channels, half, hidden, frames)
    payload, grads = pl.pallas_call(
        lambda *refs: main_kernel(sizes, *refs),
        out_shape=(
            jax.ShapeDtypeStruct((rows + 8 + 8 * STREAMS, LANES), F32),
            jax.ShapeDtypeStruct((STREAMS * channels, frames), F32),
        ),
        in_specs=in_vmem(7 + len(constants)),
        out_specs=tuple(in_vmem(2)),
        scratch_shapes=scratch,
        name="decode_and_losses",
    )(own, first, second, up_kernel, inner_kernel, outer_kernel, out_kernel, *constants)

    index = lax.axis_index("tm")
    line = lax.broadcasted_iota(jnp.int32, payload.shape, 0)
    lane = lax.broadcasted_iota(jnp.int32, payload.shape, 1)
    step = 1
    while True:
        theirs = lax.ppermute(payload, "tm", [(i, i ^ step) for i in range(count)])
        if 2 * step == count:
            break
        low = index % step
        swap = ((low == 0) & (lane >= LANES // 2)) | ((low == step - 1) & (lane < LANES // 2))
        payload = jnp.where(
            line < rows + 8, payload + theirs, jnp.where(swap, theirs, payload)
        )
        step *= 2

    weights, aux = pl.pallas_call(
        lambda *refs: combine_kernel((half, hidden, samples), *refs),
        out_shape=(
            jax.ShapeDtypeStruct((2 * half + hidden + 8, LANES), F32),
            jax.ShapeDtypeStruct((16, LANES), F32),
        ),
        in_specs=in_vmem(2),
        out_specs=tuple(in_vmem(2)),
        name="combine",
    )(payload, theirs)
    latent_grad = pl.pallas_call(
        lambda grads_ref, aux_ref, out, square: latent_kernel(channels, grads_ref, aux_ref, square, out),
        out_shape=jax.ShapeDtypeStruct(latent.shape, F32),
        in_specs=in_vmem(2),
        out_specs=in_vmem(1)[0],
        scratch_shapes=[pltpu.VMEM((LANES, LANES), F32)],
        name="latent",
    )(grads, aux)

    count = lax.axis_size("dp")
    step = 1
    while True:
        theirs = lax.ppermute(weights, "dp", [(i, i ^ step) for i in range(count)])
        if 2 * step == count:
            break
        weights = weights + theirs
        step *= 2
    updates = pl.pallas_call(
        lambda *refs: final_kernel((channels, half, hidden, params), *refs),
        out_shape=tuple(
            jax.ShapeDtypeStruct(x.shape, F32)
            for x in (up_kernel, inner_kernel, outer_kernel, out_kernel)
        ),
        in_specs=in_vmem(2),
        out_specs=tuple(in_vmem(4)),
        scratch_shapes=[pltpu.VMEM((LANES, LANES), F32)],
        name="final",
    )(weights, theirs)
    return (latent_grad, *updates)


def solution(mesh):
    for axis in ("dp", "tm"):
        size = mesh.shape[axis]
        assert size > 1 and size & (size - 1) == 0
    placed = (P("dp", None, "tm"), P("dp", "tm"), P(), P(), P(), P())
    return jax.shard_map(
        local,
        mesh=mesh,
        in_specs=placed,
        out_specs=(P("dp", None, "tm"), P(), P(), P(), P()),
        check_vma=False,
    )
```

time: 190 us -> 56.8 us (0.30)
  blocking collectives: 63.8 us -> 0 us
  matrix products: 37.6 us -> 0 us
  other arithmetic: 31.8 us -> 4.19 us
  local copies, waits for them, and re-layouts: 22 us -> 5.21 us
  Pallas kernels: 0 us -> 14.4 us
  waiting for transfers between devices: 1.95 us -> 15.4 us
  starting transfers between devices: 26.4 us -> 16.5 us
  between operations: 4.65 us -> 0.72 us
    psum x2 -> x0, blocking collectives: 63.8 us -> none  [the longest x1 41.8 us: local(): lax.psum((local_totals[0], local_totals[1], local_totals[2], local_totals...]
    dot_general x44 -> x0, matrix products: 37.6 us -> none  [product(): jnp.einsum(form, left, right, precision=lax.Precision.HIGHEST, preferred_...]
    pallas_call x0 -> x4, Pallas kernels: none -> 14.4 us  [the longest x1 9.15 us: local(): pl.pallas_call(lambda *refs: main_kernel(sizes, *refs), out_shape=(jax.Sh...]
    mul x10 -> x0, other arithmetic: 13.6 us -> none  [the longest x2 10.7 us: dft_table(): -hann_taper * jnp.sin(angles)]
    ppermute x8 -> x7, waiting for transfers between devices: 1.95 us -> 15.4 us  [the longest x3 10.8 us: local(): theirs = lax.ppermute(payload, 'tm', [(i, i ^ step) for i in range(count)])]
    ppermute x8 -> x7, starting transfers between devices: 26.4 us -> 16.5 us  [the longest x3 11.3 us: local(): theirs = lax.ppermute(payload, 'tm', [(i, i ^ step) for i in range(count)])]
    slice x13 -> x0, local copies, waits for them, and re-layouts: 8.86 us -> none  [the longest x4 4.01 us: framed(): blocks[..., offset:offset + frame_count, :]]
    reshape x7 -> x1, local copies, waits for them, and re-layouts: 7.07 us -> 0.01 us  [local(): own = jnp.concatenate([latent[0], target.reshape(2, frames)], axis=0)]
  transfers between devices with their start and end apart: 8 -> 7, of which waited for: 2 -> 6; matrix products, arithmetic and copies ran while one was open for 28% -> 1% of each run, Pallas kernels for 0% -> 3%
where the time goes in v1:
time: 56.8 us; the launch traced here: 56.4 us
  starting transfers between devices  16.5 us (29%)
  waiting for transfers between devices  15.4 us (27%)
  Pallas kernels  14.4 us (25%)
  local copies, waits for them, and re-layouts  5.21 us (9%)
  other arithmetic  4.19 us (7%)
  between operations  0.72 us (1%)
    ppermute x3, starting transfers between devices, local(): theirs = lax.ppermute(payload, 'tm', [(i, i ^ step) for i in range(count)])  11.3 us
    ppermute x3, waiting for transfers between devices, local(): theirs = lax.ppermute(payload, 'tm', [(i, i ^ step) for i in range(count)])  10.8 us
    pallas_call x1, Pallas kernels, local(): pl.pallas_call(lambda *refs: main_kernel(sizes, *refs), out_shape=(jax.Sh...  9.15 us
    unnamed x19, local copies, waits for them, and re-layouts  5.2 us
    ppermute x1, starting transfers between devices, local(): first = lax.ppermute(own, 'tm', pairs)  3.06 us
    ppermute x1, waiting for transfers between devices, local(): first = lax.ppermute(own, 'tm', pairs)  2.49 us
    ppermute x2, waiting for transfers between devices, local(): theirs = lax.ppermute(weights, 'dp', [(i, i ^ step) for i in range(count)])  2.15 us
    pallas_call x1, Pallas kernels, local(): pl.pallas_call(lambda grads_ref, aux_ref, out, square: latent_kernel(chan...  1.83 us
  transfers between devices with their start and end apart: 7, of which 6 were waited for; matrix products, arithmetic and copies ran while one was open for 1% of the time, Pallas kernels for 3%

profile of v1, /device:TPU:0, one launch (start us, length us, event | category | flops | bytes accessed | tf_op | source)
XLA Modules:
  0.0 56.4 jit_solution(8458085624797197897)
XLA Ops:
  1.1 1.3 %reduce.3 = f32[1024]{0:T(1024)S(1)} reduce(f32[1,1024]{1,0:T(1,128)} %param.19, f32[]{:T(128)} %broadcast.32), dimensions={0}, to_apply=%param.19.reduce_sub_computation.3 | reduce | bytes 8196 | tf_op args[1]
  2.5 0.9 %pad_maximum_fusion.refs_0_ = f32[66,512]{1,0:T(8,128)S(1)} fusion(f32[2,512]{1,0:T(2,128)S(1)} %reshape.13, f32[64,512]{1,0:T(8,128)} %bitcast.1), kind=kLoop, calls=%fused_computation | loop fusion | flops 33792 | bytes 270336 | tf_op jit(solution)/shard_map/concatenate | solution.py:457
  3.5 3.1 %collective-permute-start = (f32[66,512]{1,0:T(8,128)S(1)}, f32[66,512]{1,0:T(8,128)S(1)}, u32[]{:S(2)}, u32[]{:S(2)}) collective-permute-start(f32[66,512]{1,0:T(8,128)S(1)} %pad_maximum_fusion.refs_0_), channel_id=1, source_target_pairs={{0,1},{1,0},{2,3},{3,2},{4,5},{5,4},{6,7},{7,6},{8,9},{9,8},{10,11... | collective-permute-start | bytes 405512 | tf_op jit(solution)/shard_map/ppermute | solution.py:459
  6.5 0.7 %collective-permute-start.1 = (f32[66,512]{1,0:T(8,128)S(1)}, f32[66,512]{1,0:T(8,128)S(1)}, u32[]{:S(2)}, u32[]{:S(2)}) collective-permute-start(f32[66,512]{1,0:T(8,128)S(1)} %pad_maximum_fusion.refs_0_), channel_id=1, source_target_pairs={{1,2},{2,1},{3,4},{4,3},{5,6},{6,5},{9,10},{10,9},{11,12},{12,11},... | collective-permute-start | bytes 405512 | tf_op jit(solution)/shard_map/ppermute | solution.py:461
  7.2 0.7 %copy.23.refs_5_ = f32[32,16]{1,0:T(8,128)} copy(f32[32,16]{0,1:T(8,128)S(1)} %copy-done.7) | data formatting | bytes 4096 | tf_op args[4]
  7.9 2.5 %collective-permute-done.refs_1_ = f32[66,512]{1,0:T(8,128)S(1)} collective-permute-done((f32[66,512]{1,0:T(8,128)S(1)}, f32[66,512]{1,0:T(8,128)S(1)}, u32[]{:S(2)}, u32[]{:S(2)}) %collective-permute-start) | collective-permute-done | bytes 135200 | tf_op jit(solution)/shard_map/ppermute | solution.py:459
  11.0 0.7 %copy-done.4 = f32[66,512]{1,0:T(8,128)} copy-done((f32[66,512]{1,0:T(8,128)}, f32[66,512]{1,0:T(8,128)S(1)}, u32[]{:S(2)}) %copy-start.4) | copy-done | bytes 135192
  11.7 9.2 %decode_and_losses.1 = (f32[272,128]{1,0:T(8,128)}, f32[192,512]{1,0:T(8,128)}) custom-call(f32[66,512]{1,0:T(8,128)} %copy-done, f32[66,512]{1,0:T(8,128)} %copy-done.3, f32[66,512]{1,0:T(8,128)} %copy-done.4, f32[4,32,64]{2,1,0:T(8,128)} %refs_3_.1, f32[3,16,32]{2,1,0:T(8,128)} %refs_4_.1, f32[32,16]{1,0:T(8,128)} %copy.23.refs_5_, f32[7,32]{1,0:T(8,128)} %refs_6_.1, ...), custom_call_target="tpu_custom_call" | custom-call | tf_op jit(solution)/shard_map/decode_and_losses/pallas_call | solution.py:490
  20.8 4.9 %collective-permute-start.2 = (f32[272,128]{1,0:T(8,128)}, f32[272,128]{1,0:T(8,128)S(1)}, u32[]{:S(2)}, u32[]{:S(2)}) collective-permute-start(f32[272,128]{1,0:T(8,128)} %get-tuple-element.14), channel_id=1, source_target_pairs={{0,1},{1,0},{2,3},{3,2},{4,5},{5,4},{6,7},{7,6},{8,9},{9,8},{10,11... | collective-permute-start | bytes 417800 | tf_op jit(solution)/shard_map/ppermute | solution.py:507
  25.8 3.2 %collective-permute-done.2 = f32[272,128]{1,0:T(8,128)S(1)} collective-permute-done((f32[272,128]{1,0:T(8,128)}, f32[272,128]{1,0:T(8,128)S(1)}, u32[]{:S(2)}, u32[]{:S(2)}) %collective-permute-start.2) | collective-permute-done | bytes 139296 | tf_op jit(solution)/shard_map/ppermute | solution.py:507
  29.0 1.0 %select_select_fusion.1 = f32[272,128]{1,0:T(8,128)S(1)} fusion(f32[272,128]{1,0:T(8,128)S(1)} %collective-permute-done.2, f32[272,128]{1,0:T(8,128)} %get-tuple-element.14, pred[272]{0:T(512)(128)(4,1)S(1)} %iota_compare_fusion, pred[128]{0:T(512)(128)(4,1)S(1)} %compare_or_fusion), kind=kLoop, calls=%fused_computation.2 | loop fusion | flops 104448 | bytes 418192 | tf_op jit(solution)/shard_map/jit(_where)/select_n | solution.py:512
  30.0 2.3 %collective-permute-start.3 = (f32[272,128]{1,0:T(8,128)S(1)}, f32[272,128]{1,0:T(8,128)S(1)}, u32[]{:S(2)}, u32[]{:S(2)}) collective-permute-start(f32[272,128]{1,0:T(8,128)S(1)} %select_select_fusion.1), channel_id=1, source_target_pairs={{0,2},{1,3},{2,0},{3,1},{4,6},{5,7},{6,4},{7,5},{8,10},{9,11},{10,... | collective-permute-start | bytes 417800 | tf_op jit(solution)/shard_map/ppermute | solution.py:507
  32.4 3.0 %collective-permute-done.3 = f32[272,128]{1,0:T(8,128)S(1)} collective-permute-done((f32[272,128]{1,0:T(8,128)S(1)}, f32[272,128]{1,0:T(8,128)S(1)}, u32[]{:S(2)}, u32[]{:S(2)}) %collective-permute-start.3) | collective-permute-done | bytes 139296 | tf_op jit(solution)/shard_map/ppermute | solution.py:507
  35.5 4.0 %collective-permute-start.4 = (f32[272,128]{1,0:T(8,128)S(1)}, f32[272,128]{1,0:T(8,128)S(1)}, u32[]{:S(2)}, u32[]{:S(2)}) collective-permute-start(f32[272,128]{1,0:T(8,128)S(1)} %select_select_fusion.refs_0_), channel_id=1, source_target_pairs={{0,4},{1,5},{2,6},{3,7},{4,0},{5,1},{6,2},{7,3},{8,12},{9,13},{10,... | collective-permute-start | bytes 417800 | tf_op jit(solution)/shard_map/ppermute | solution.py:507
  39.5 4.5 %collective-permute-done.4.refs_1_ = f32[272,128]{1,0:T(8,128)S(1)} collective-permute-done((f32[272,128]{1,0:T(8,128)S(1)}, f32[272,128]{1,0:T(8,128)S(1)}, u32[]{:S(2)}, u32[]{:S(2)}) %collective-permute-start.4) | collective-permute-done | bytes 139296 | tf_op jit(solution)/shard_map/ppermute | solution.py:507
  44.1 0.7 %copy-done.5 = f32[272,128]{1,0:T(8,128)} copy-done((f32[272,128]{1,0:T(8,128)}, f32[272,128]{1,0:T(8,128)S(1)}, u32[]{:S(2)}) %copy-start.5) | copy-done | bytes 139288
  44.7 1.7 %combine.1 = (f32[88,128]{1,0:T(8,128)}, f32[16,128]{1,0:T(8,128)}) custom-call(f32[272,128]{1,0:T(8,128)} %copy-done.1, f32[272,128]{1,0:T(8,128)} %copy-done.5), custom_call_target="tpu_custom_call" | custom-call | tf_op jit(solution)/shard_map/combine/pallas_call | solution.py:517
  46.4 1.4 %collective-permute-done.5 = f32[88,128]{1,0:T(8,128)S(1)} collective-permute-done((f32[88,128]{1,0:T(8,128)}, f32[88,128]{1,0:T(8,128)S(1)}, u32[]{:S(2)}, u32[]{:S(2)}) %collective-permute-start.5) | collective-permute-done | bytes 45088 | tf_op jit(solution)/shard_map/ppermute | solution.py:539
  47.9 0.8 %add.17.refs_0_ = f32[88,128]{1,0:T(8,128)S(1)} add(f32[88,128]{1,0:T(8,128)} %get-tuple-element.16, f32[88,128]{1,0:T(8,128)S(1)} %collective-permute-done.5) | non-fusion elementwise | flops 11264 | bytes 135168 | tf_op jit(solution)/shard_map/add | solution.py:542
  48.7 1.5 %collective-permute-start.6 = (f32[88,128]{1,0:T(8,128)S(1)}, f32[88,128]{1,0:T(8,128)S(1)}, u32[]{:S(2)}, u32[]{:S(2)}) collective-permute-start(f32[88,128]{1,0:T(8,128)S(1)} %add.17.refs_0_), channel_id=1, source_target_pairs={{0,16},{8,24},{16,0},{24,8},{1,17},{9,25},{17,1},{25,9},{2,18},{10... | collective-permute-start | bytes 135176 | tf_op jit(solution)/shard_map/ppermute | solution.py:539
  50.2 1.8 %latent.1 = f32[1,64,512]{2,1,0:T(8,128)} custom-call(f32[192,512]{1,0:T(8,128)} %get-tuple-element.13.grads_ref, f32[16,128]{1,0:T(8,128)} %get-tuple-element.15.aux_ref), custom_call_target="tpu_custom_call" | custom-call | tf_op jit(solution)/shard_map/latent/pallas_call | solution.py:527
  52.0 0.7 %collective-permute-done.6.refs_1_ = f32[88,128]{1,0:T(8,128)S(1)} collective-permute-done((f32[88,128]{1,0:T(8,128)S(1)}, f32[88,128]{1,0:T(8,128)S(1)}, u32[]{:S(2)}, u32[]{:S(2)}) %collective-permute-start.6) | collective-permute-done | bytes 45088 | tf_op jit(solution)/shard_map/ppermute | solution.py:539
  53.3 1.7 %final.1 = (f32[4,32,64]{2,1,0:T(8,128)}, f32[3,16,32]{2,1,0:T(8,128)}, f32[32,16]{1,0:T(8,128)}, f32[7,32]{1,0:T(8,128)}) custom-call(f32[88,128]{1,0:T(8,128)} %copy-done.2, f32[88,128]{1,0:T(8,128)} %copy-done.6), custom_call_target="tpu_custom_call" | custom-call | tf_op jit(solution)/shard_map/final/pallas_call | solution.py:544
  55.0 1.4 %copy.24 = f32[32,16]{0,1:T(8,128)} copy(f32[32,16]{1,0:T(8,128)} %get-tuple-element.24) | data formatting | bytes 4096
  (22 shorter events, 1.9 us)
Async XLA Ops:
  2.5 4.7 %copy-start.7 = (f32[32,16]{0,1:T(8,128)S(1)}, f32[32,16]{0,1:T(8,128)}, u32[]{:S(2)}) copy-start(f32[32,16]{0,1:T(8,128)} %param.22) | copy-start | bytes 6148
  3.4 6.9 %copy-start = (f32[66,512]{1,0:T(8,128)}, f32[66,512]{1,0:T(8,128)S(1)}, u32[]{:S(2)}) copy-start(f32[66,512]{1,0:T(8,128)S(1)} %pad_maximum_fusion.refs_0_) | copy-start | bytes 405508
  3.5 6.9 %collective-permute-start = (f32[66,512]{1,0:T(8,128)S(1)}, f32[66,512]{1,0:T(8,128)S(1)}, u32[]{:S(2)}, u32[]{:S(2)}) collective-permute-start(f32[66,512]{1,0:T(8,128)S(1)} %pad_maximum_fusion.refs_0_), channel_id=1, source_target_pairs={{0,1},{1,0},{2,3},{3,2},{4,5},{5,4},{6,7},{7,6},{8,9},{9,8},{10,11... | collective-permute-start | bytes 405512 | tf_op jit(solution)/shard_map/ppermute | solution.py:459
  6.5 3.9 %collective-permute-start.1 = (f32[66,512]{1,0:T(8,128)S(1)}, f32[66,512]{1,0:T(8,128)S(1)}, u32[]{:S(2)}, u32[]{:S(2)}) collective-permute-start(f32[66,512]{1,0:T(8,128)S(1)} %pad_maximum_fusion.refs_0_), channel_id=1, source_target_pairs={{1,2},{2,1},{3,4},{4,3},{5,6},{6,5},{9,10},{10,9},{11,12},{12,11},... | collective-permute-start | bytes 405512 | tf_op jit(solution)/shard_map/ppermute | solution.py:461
  10.4 0.7 %copy-start.3 = (f32[66,512]{1,0:T(8,128)}, f32[66,512]{1,0:T(8,128)S(1)}, u32[]{:S(2)}) copy-start(f32[66,512]{1,0:T(8,128)S(1)} %collective-permute-done.refs_1_) | copy-start | bytes 405508
  11.0 0.7 %copy-start.4 = (f32[66,512]{1,0:T(8,128)}, f32[66,512]{1,0:T(8,128)S(1)}, u32[]{:S(2)}) copy-start(f32[66,512]{1,0:T(8,128)S(1)} %collective-permute-done.1.refs_2_) | copy-start | bytes 405508
  20.8 8.1 %collective-permute-start.2 = (f32[272,128]{1,0:T(8,128)}, f32[272,128]{1,0:T(8,128)S(1)}, u32[]{:S(2)}, u32[]{:S(2)}) collective-permute-start(f32[272,128]{1,0:T(8,128)} %get-tuple-element.14), channel_id=1, source_target_pairs={{0,1},{1,0},{2,3},{3,2},{4,5},{5,4},{6,7},{7,6},{8,9},{9,8},{10,11... | collective-permute-start | bytes 417800 | tf_op jit(solution)/shard_map/ppermute | solution.py:507
  30.0 5.4 %collective-permute-start.3 = (f32[272,128]{1,0:T(8,128)S(1)}, f32[272,128]{1,0:T(8,128)S(1)}, u32[]{:S(2)}, u32[]{:S(2)}) collective-permute-start(f32[272,128]{1,0:T(8,128)S(1)} %select_select_fusion.1), channel_id=1, source_target_pairs={{0,2},{1,3},{2,0},{3,1},{4,6},{5,7},{6,4},{7,5},{8,10},{9,11},{10,... | collective-permute-start | bytes 417800 | tf_op jit(solution)/shard_map/ppermute | solution.py:507
  35.5 8.6 %copy-start.1 = (f32[272,128]{1,0:T(8,128)}, f32[272,128]{1,0:T(8,128)S(1)}, u32[]{:S(2)}) copy-start(f32[272,128]{1,0:T(8,128)S(1)} %select_select_fusion.refs_0_) | copy-start | bytes 417796
  35.5 8.6 %collective-permute-start.4 = (f32[272,128]{1,0:T(8,128)S(1)}, f32[272,128]{1,0:T(8,128)S(1)}, u32[]{:S(2)}, u32[]{:S(2)}) collective-permute-start(f32[272,128]{1,0:T(8,128)S(1)} %select_select_fusion.refs_0_), channel_id=1, source_target_pairs={{0,4},{1,5},{2,6},{3,7},{4,0},{5,1},{6,2},{7,3},{8,12},{9,13},{10,... | collective-permute-start | bytes 417800 | tf_op jit(solution)/shard_map/ppermute | solution.py:507
  44.1 0.7 %copy-start.5 = (f32[272,128]{1,0:T(8,128)}, f32[272,128]{1,0:T(8,128)S(1)}, u32[]{:S(2)}) copy-start(f32[272,128]{1,0:T(8,128)S(1)} %collective-permute-done.4.refs_1_) | copy-start | bytes 417796
  46.4 1.4 %collective-permute-start.5 = (f32[88,128]{1,0:T(8,128)}, f32[88,128]{1,0:T(8,128)S(1)}, u32[]{:S(2)}, u32[]{:S(2)}) collective-permute-start(f32[88,128]{1,0:T(8,128)} %get-tuple-element.16), channel_id=1, source_target_pairs={{0,8},{8,0},{16,24},{24,16},{1,9},{9,1},{17,25},{25,17},{2,10},{10... | collective-permute-start | bytes 135176 | tf_op jit(solution)/shard_map/ppermute | solution.py:539
  48.7 3.3 %copy-start.2 = (f32[88,128]{1,0:T(8,128)}, f32[88,128]{1,0:T(8,128)S(1)}, u32[]{:S(2)}) copy-start(f32[88,128]{1,0:T(8,128)S(1)} %add.17.refs_0_) | copy-start | bytes 135172
  48.7 4.0 %collective-permute-start.6 = (f32[88,128]{1,0:T(8,128)S(1)}, f32[88,128]{1,0:T(8,128)S(1)}, u32[]{:S(2)}, u32[]{:S(2)}) collective-permute-start(f32[88,128]{1,0:T(8,128)S(1)} %add.17.refs_0_), channel_id=1, source_target_pairs={{0,16},{8,24},{16,0},{24,8},{1,17},{9,25},{17,1},{25,9},{2,18},{10... | collective-permute-start | bytes 135176 | tf_op jit(solution)/shard_map/ppermute | solution.py:539
  52.7 0.6 %copy-start.6 = (f32[88,128]{1,0:T(8,128)}, f32[88,128]{1,0:T(8,128)S(1)}, u32[]{:S(2)}) copy-start(f32[88,128]{1,0:T(8,128)S(1)} %collective-permute-done.6.refs_1_) | copy-start | bytes 135172

commit v2 on v1

--- a/solution.py
+++ b/solution.py
@@ -63,10 +63,14 @@
     hann = np.concatenate([hann, np.zeros_like(hann)], 0)
     deal = np.zeros((BLOCK, BLOCK), np.float32)
     deal[order, np.arange(BLOCK)] = 1.0
-    out = [hann, deal.astype(BF16)]
-    for table in (even, odd, fine, coarse_mel, fine_mel):
-        out += list(hi_lo(table))
-    return out
+    even, odd, fine = hi_lo(even), hi_lo(odd), hi_lo(fine)
+    banks = hi_lo(coarse_mel) + hi_lo(fine_mel)
+    return (
+        hann,
+        np.concatenate([deal.astype(BF16), *even, *fine], 0),
+        np.concatenate(odd, 0),
+        np.concatenate(banks, 0),
+    )
 
 
 def split(x):
@@ -107,11 +111,18 @@
 
 def main_kernel(sizes, *refs):
     (own_ref, first_ref, second_ref, up_ref, inner_ref, outer_ref, out_ref) = refs[:7]
-    (hann_ref, deal_ref, even_h, even_l, odd_h, odd_l, fine_h, fine_l) = refs[7:15]
-    (cmel_h, cmel_l, fmel_h, fmel_l) = refs[15:19]
-    payload_ref, grads_ref = refs[19:21]
-    (lat, act, slope_a, a_h, a_l, slope_u, e_h, e_l, slope_c, h_h, h_l, slope_m, g_h, g_l) = refs[21:35]
-    (square, wup, kfwd, wblock, shifted, wave_b, targ_b, lanes_b) = refs[35:43]
+    sources = refs[7:11]
+    payload_ref, grads_ref = refs[11:13]
+    (lat, act, slope_a, a_h, a_l, slope_u, e_h, e_l, slope_c, h_h, h_l, slope_m, g_h, g_l) = refs[13:27]
+    (square, wup, kfwd, wblock, shifted, wave_b, targ_b, lanes_b) = refs[27:35]
+    fetched, sems = refs[35:39], refs[39]
+    copies = [
+        pltpu.make_async_copy(source, space, sems.at[i])
+        for i, (source, space) in enumerate(zip(sources, fetched))
+    ]
+    for copy in copies:
+        copy.start()
+    hann_ref, square_ref, odd_ref, bank_ref = fetched
     channels, half, hidden, frames = sizes
     wide = 3 * frames
     own_blocks = frames // LANES
@@ -148,10 +159,10 @@
         square[(3 - j) * hidden : (4 - j) * hidden, half : 2 * half] = inner_ref[j]
     back_inner = jnp.transpose(square[...])[0 : 2 * half, 0 : 4 * hidden]
     square[...] = jnp.zeros_like(square)
-    square[0:half, 0:hidden] = outer_ref[...]
-    square[half : 2 * half, hidden : 2 * hidden] = outer_ref[...]
-    outer_fwd = square[0 : 2 * half, 0 : 2 * hidden]
-    outer_back = jnp.transpose(square[...])[0 : 2 * hidden, 0 : 2 * half]
+    square[0:hidden, 0:half] = outer_ref[...]
+    square[hidden : 2 * hidden, half : 2 * half] = outer_ref[...]
+    outer_back = square[0 : 2 * hidden, 0 : 2 * half]
+    outer_fwd = jnp.transpose(square[...])[0 : 2 * half, 0 : 2 * hidden]
     square[...] = jnp.zeros_like(square)
     square[1:8, 0:half] = out_ref[...]
     square[0:7, half : 2 * half] = out_ref[...]
@@ -203,7 +214,19 @@
     rest = whole - high.astype(F32)
     middle = rest.astype(BF16)
     last = (rest - middle.astype(F32)).astype(BF16)
-    deal = deal_ref[...]
+    for copy in copies:
+        copy.wait()
+    deal = square_ref[0:BLOCK]
+    even_h, even_l, odd_h, odd_l = (
+        square_ref.at[pl.ds(BLOCK, 2 * BLOCK)],
+        square_ref.at[pl.ds(3 * BLOCK, 2 * BLOCK)],
+        odd_ref.at[pl.ds(0, 2 * BLOCK)],
+        odd_ref.at[pl.ds(2 * BLOCK, 2 * BLOCK)],
+    )
+    fine_h, fine_l = square_ref.at[pl.ds(5 * BLOCK, BLOCK)], square_ref.at[pl.ds(6 * BLOCK, BLOCK)]
+    cmel_h, cmel_l = bank_ref.at[pl.ds(0, 2 * BLOCK)], bank_ref.at[pl.ds(2 * BLOCK, 2 * BLOCK)]
+    fmel_h = bank_ref.at[pl.ds(4 * BLOCK, LANES)]
+    fmel_l = bank_ref.at[pl.ds(4 * BLOCK + LANES, LANES)]
     targ_b[...] = dot(high, deal) + dot(middle, deal) + dot(last, deal)
 
     row_count = own_blocks + 4
@@ -421,7 +444,7 @@
     grad_ref[0, :, frames - LANES :] = grad_ref[0, :, frames - LANES :] + turned[channels:]
 
 
-def final_kernel(sizes, mine_ref, theirs_ref, up_ref, inner_ref, outer_ref, out_ref, square):
+def final_kernel(sizes, mine_ref, theirs_ref, up_ref, inner_ref, outer_ref, out_ref):
     channels, half, hidden, params = sizes
     total = mine_ref[...] + theirs_ref[...]
     squares = jnp.sum(total * total)
@@ -433,14 +456,42 @@
     inner = total[2 * half : 2 * half + hidden]
     for j in range(3):
         inner_ref[j] = inner[:, j * half : (j + 1) * half]
-    square[...] = jnp.zeros_like(square)
-    square[0:hidden, :] = inner
-    outer_ref[...] = jnp.transpose(square[...])[3 * half :, 0:hidden]
+    outer_ref[...] = inner[:, 3 * half :]
     out_ref[...] = total[2 * half + hidden : 2 * half + hidden + 7, 0:half]
 
 
-def in_vmem(count):
-    return [pl.BlockSpec(memory_space=VMEM)] * count
+def pack_kernel(latent_ref, target_ref, own_ref, sems):
+    channels, frames = latent_ref.shape[1:]
+    copies = [pltpu.make_async_copy(latent_ref.at[0], own_ref.at[pl.ds(0, channels)], sems.at[0])]
+    for row in range(2):
+        copies.append(
+            pltpu.make_async_copy(
+                target_ref.at[:, pl.ds(row * frames, frames)],
+                own_ref.at[pl.ds(channels + row, 1)],
+                sems.at[1 + row],
+            )
+        )
+    for copy in copies:
+        copy.start()
+    for copy in copies:
+        copy.wait()
+
+
+def run(kernel, out_shape, operands, scratch, name, mebibytes, left=0):
+    spec = pl.BlockSpec(memory_space=VMEM)
+    kept = len(operands) - left
+    hbm = [pltpu.with_memory_space_constraint(x, pltpu.MemorySpace.HBM) for x in operands[kept:]]
+    operands = [*operands[:kept], *hbm]
+    stay = pl.BlockSpec(memory_space=pltpu.MemorySpace.HBM)
+    return pl.pallas_call(
+        kernel,
+        out_shape=tuple(jax.ShapeDtypeStruct(shape, F32) for shape in out_shape),
+        in_specs=[spec] * (len(operands) - left) + [stay] * left,
+        out_specs=tuple([spec] * len(out_shape)),
+        scratch_shapes=scratch,
+        compiler_params=pltpu.CompilerParams(vmem_limit_bytes=mebibytes << 20),
+        name=name,
+    )(*operands)
 
 
 def local(latent, target, up_kernel, inner_kernel, outer_kernel, out_kernel):
@@ -454,7 +505,7 @@
     samples = target.shape[1] * count
     params = sum(x.size for x in (up_kernel, inner_kernel, outer_kernel, out_kernel))
 
-    own = jnp.concatenate([latent[0], target.reshape(2, frames)], axis=0)
+    (own,) = run(pack_kernel, [(channels + 8, frames)], [latent, target], [pltpu.SemaphoreType.DMA((3,))], "pack", 2, 2)
     pairs = [(i, i ^ 1) for i in range(count) if i ^ 1 < count]
     first = lax.ppermute(own, "tm", pairs)
     pairs = [(i, i + 1 if i % 2 else i - 1) for i in range(count)]
@@ -485,19 +536,19 @@
         pltpu.VMEM((3 * blocks, BLOCK), F32),
         pltpu.VMEM((3 * blocks, BLOCK), F32),
         pltpu.VMEM((STREAMS, 8, window), F32),
+        *[pltpu.VMEM(x.shape, x.dtype) for x in constants],
+        pltpu.SemaphoreType.DMA((len(constants),)),
     ]
     sizes = (channels, half, hidden, frames)
-    payload, grads = pl.pallas_call(
+    payload, grads = run(
         lambda *refs: main_kernel(sizes, *refs),
-        out_shape=(
-            jax.ShapeDtypeStruct((rows + 8 + 8 * STREAMS, LANES), F32),
-            jax.ShapeDtypeStruct((STREAMS * channels, frames), F32),
-        ),
-        in_specs=in_vmem(7 + len(constants)),
-        out_specs=tuple(in_vmem(2)),
-        scratch_shapes=scratch,
-        name="decode_and_losses",
-    )(own, first, second, up_kernel, inner_kernel, outer_kernel, out_kernel, *constants)
+        [(rows + 8 + 8 * STREAMS, LANES), (STREAMS * channels, frames)],
+        [own, first, second, up_kernel, inner_kernel, outer_kernel.T, out_kernel, *constants],
+        scratch,
+        "decode_and_losses",
+        24,
+        len(constants),
+    )
 
     index = lax.axis_index("tm")
     line = lax.broadcasted_iota(jnp.int32, payload.shape, 0)
@@ -514,24 +565,22 @@
         )
         step *= 2
 
-    weights, aux = pl.pallas_call(
+    weights, aux = run(
         lambda *refs: combine_kernel((half, hidden, samples), *refs),
-        out_shape=(
-            jax.ShapeDtypeStruct((2 * half + hidden + 8, LANES), F32),
-            jax.ShapeDtypeStruct((16, LANES), F32),
-        ),
-        in_specs=in_vmem(2),
-        out_specs=tuple(in_vmem(2)),
-        name="combine",
-    )(payload, theirs)
-    latent_grad = pl.pallas_call(
+        [(2 * half + hidden + 8, LANES), (16, LANES)],
+        [payload, theirs],
+        [],
+        "combine",
+        2,
+    )
+    (latent_grad,) = run(
         lambda grads_ref, aux_ref, out, square: latent_kernel(channels, grads_ref, aux_ref, square, out),
-        out_shape=jax.ShapeDtypeStruct(latent.shape, F32),
-        in_specs=in_vmem(2),
-        out_specs=in_vmem(1)[0],
-        scratch_shapes=[pltpu.VMEM((LANES, LANES), F32)],
-        name="latent",
-    )(grads, aux)
+        [latent.shape],
+        [grads, aux],
+        [pltpu.VMEM((LANES, LANES), F32)],
+        "latent",
+        2,
+    )
 
     count = lax.axis_size("dp")
     step = 1
@@ -541,18 +590,15 @@
             break
         weights = weights + theirs
         step *= 2
-    updates = pl.pallas_call(
+    up, inner, outer, out = run(
         lambda *refs: final_kernel((channels, half, hidden, params), *refs),
-        out_shape=tuple(
-            jax.ShapeDtypeStruct(x.shape, F32)
-            for x in (up_kernel, inner_kernel, outer_kernel, out_kernel)
-        ),
-        in_specs=in_vmem(2),
-        out_specs=tuple(in_vmem(4)),
-        scratch_shapes=[pltpu.VMEM((LANES, LANES), F32)],
-        name="final",
-    )(weights, theirs)
-    return (latent_grad, *updates)
+        [up_kernel.shape, inner_kernel.shape, outer_kernel.shape[::-1], out_kernel.shape],
+        [weights, theirs],
+        [],
+        "final",
+        2,
+    )
+    return (latent_grad, up, inner, outer.T, out)
 
 
 def solution(mesh):

time: 56.8 us -> 45.7 us (0.80)
  local copies, waits for them, and re-layouts: 5.21 us -> 0.02 us
  other arithmetic: 4.19 us -> 0.23 us
  Pallas kernels: 14.4 us -> 10.5 us
  waiting for transfers between devices: 15.4 us -> 16.7 us
  starting transfers between devices: 16.5 us -> 17.3 us
    unnamed x19 -> x8, local copies, waits for them, and re-layouts: 5.2 us -> 0.02 us
    pallas_call x4 -> x5, Pallas kernels: 14.4 us -> 10.5 us  [run(): pl.pallas_call(kernel, out_shape=tuple((jax.ShapeDtypeStruct(shape, F32)...]
    unnamed x1 -> x0, other arithmetic: 1.35 us -> none
    concatenate x1 -> x0, other arithmetic: 0.92 us -> none  [local(): own = jnp.concatenate([latent[0], target.reshape(2, frames)], axis=0)]
    select_n x2, other arithmetic: 1.11 us -> 0.2 us  [local(): jnp.where(line < rows + 8, payload + theirs, jnp.where(swap, theirs, payl...]
    add x1, other arithmetic: 0.8 us -> 0.01 us  [local(): weights = weights + theirs]
    ppermute x2, waiting for transfers between devices: 2.15 us -> 2.94 us  [local(): theirs = lax.ppermute(weights, 'dp', [(i, i ^ step) for i in range(count)])]
    ppermute x3, starting transfers between devices: 11.3 us -> 12 us  [local(): theirs = lax.ppermute(payload, 'tm', [(i, i ^ step) for i in range(count)])]
  transfers between devices with their start and end apart: 7 -> 7, of which waited for: 6 -> 6; matrix products, arithmetic and copies ran while one was open for 1% -> 0% of each run, Pallas kernels for 3% -> 2%
where the time goes in v2:
time: 45.7 us; the launch traced here: 45.5 us
  starting transfers between devices  17.3 us (38%)
  waiting for transfers between devices  16.7 us (37%)
  Pallas kernels  10.5 us (23%)
  between operations  0.75 us (2%)
    ppermute x3, starting transfers between devices, local(): theirs = lax.ppermute(payload, 'tm', [(i, i ^ step) for i in range(count)])  12 us
    ppermute x3, waiting for transfers between devices, local(): theirs = lax.ppermute(payload, 'tm', [(i, i ^ step) for i in range(count)])  10.6 us
    pallas_call x5, Pallas kernels, run(): pl.pallas_call(kernel, out_shape=tuple((jax.ShapeDtypeStruct(shape, F32)...  10.5 us
    ppermute x1, waiting for transfers between devices, local(): first = lax.ppermute(own, 'tm', pairs)  3.18 us
    ppermute x1, starting transfers between devices, local(): first = lax.ppermute(own, 'tm', pairs)  3.06 us
    ppermute x2, waiting for transfers between devices, local(): theirs = lax.ppermute(weights, 'dp', [(i, i ^ step) for i in range(count)])  2.94 us
    ppermute x2, starting transfers between devices, local(): theirs = lax.ppermute(weights, 'dp', [(i, i ^ step) for i in range(count)])  1.62 us
  transfers between devices with their start and end apart: 7, of which 6 were waited for; matrix products, arithmetic and copies ran while one was open for 0% of the time, Pallas kernels for 2%

profile of v2, /device:TPU:0, one launch (start us, length us, event | category | flops | bytes accessed | tf_op | source)
XLA Modules:
  0.0 45.5 jit_solution(3847122311796965236)
XLA Ops:
  0.6 0.0 copy-start
  0.7 1.0 %pack.1.refs_0_ = f32[72,512]{1,0:T(8,128)S(1)} custom-call(f32[1,64,512]{2,1,0:T(8,128)} %latent_ref.1, f32[1,1024]{1,0:T(1,128)} %target_ref.1), custom_call_target="tpu_custom_call" | custom-call | tf_op jit(solution)/shard_map/pack/pallas_call | solution.py:486
  1.7 3.1 %collective-permute-start = (f32[72,512]{1,0:T(8,128)S(1)}, f32[72,512]{1,0:T(8,128)S(1)}, u32[]{:S(2)}, u32[]{:S(2)}) collective-permute-start(f32[72,512]{1,0:T(8,128)S(1)} %pack.1.refs_0_), channel_id=1, source_target_pairs={{0,1},{1,0},{2,3},{3,2},{4,5},{5,4},{6,7},{7,6},{8,9},{9,8},{10,11... | collective-permute-start | bytes 442376 | tf_op jit(solution)/shard_map/ppermute | solution.py:510
  4.7 0.7 %collective-permute-start.1 = (f32[72,512]{1,0:T(8,128)S(1)}, f32[72,512]{1,0:T(8,128)S(1)}, u32[]{:S(2)}, u32[]{:S(2)}) collective-permute-start(f32[72,512]{1,0:T(8,128)S(1)} %pack.1.refs_0_), channel_id=1, source_target_pairs={{1,2},{2,1},{3,4},{4,3},{5,6},{6,5},{9,10},{10,9},{11,12},{12,11},... | collective-permute-start | bytes 442376 | tf_op jit(solution)/shard_map/ppermute | solution.py:512
  5.4 3.2 %collective-permute-done.refs_1_ = f32[72,512]{1,0:T(8,128)S(1)} collective-permute-done((f32[72,512]{1,0:T(8,128)S(1)}, f32[72,512]{1,0:T(8,128)S(1)}, u32[]{:S(2)}, u32[]{:S(2)}) %collective-permute-start) | collective-permute-done | bytes 147488 | tf_op jit(solution)/shard_map/ppermute | solution.py:510
  8.6 0.0 collective-permute-done.1.refs_2_
  8.6 0.0 copy-done.2
  8.6 0.0 copy-done.3
  8.6 7.7 %decode_and_losses.1 = (f32[272,128]{1,0:T(8,128)S(1)}, f32[192,512]{1,0:T(8,128)S(1)}) custom-call(f32[72,512]{1,0:T(8,128)S(1)} %pack.1.refs_0_, f32[72,512]{1,0:T(8,128)S(1)} %collective-permute-done.refs_1_, f32[72,512]{1,0:T(8,128)S(1)} %collective-permute-done.1.refs_2_, f32[4,32,64]{2,1,0:T(8,128)S(1)} %copy-done, f32[3,16,32]{2,1,0:T(8,128)S(1)} %copy-done.1, ...), custom_call_target="tpu_custom_call" | custom-call | tf_op jit(solution)/shard_map/decode_and_losses/pallas_call | solution.py:486
  16.3 5.0 %collective-permute-start.2 = (f32[272,128]{1,0:T(8,128)S(1)}, f32[272,128]{1,0:T(8,128)S(1)}, u32[]{:S(2)}, u32[]{:S(2)}) collective-permute-start(f32[272,128]{1,0:T(8,128)S(1)} %get-tuple-element.14), channel_id=1, source_target_pairs={{0,1},{1,0},{2,3},{3,2},{4,5},{5,4},{6,7},{7,6},{8,9},{9,8},{10,11... | collective-permute-start | bytes 417800 | tf_op jit(solution)/shard_map/ppermute | solution.py:558
  21.3 3.0 %collective-permute-done.2 = f32[272,128]{1,0:T(8,128)S(1)} collective-permute-done((f32[272,128]{1,0:T(8,128)S(1)}, f32[272,128]{1,0:T(8,128)S(1)}, u32[]{:S(2)}, u32[]{:S(2)}) %collective-permute-start.2) | collective-permute-done | bytes 139296 | tf_op jit(solution)/shard_map/ppermute | solution.py:558
  24.3 0.1 select_select_fusion.1
  24.4 3.0 %collective-permute-start.3 = (f32[272,128]{1,0:T(8,128)S(1)}, f32[272,128]{1,0:T(8,128)S(1)}, u32[]{:S(2)}, u32[]{:S(2)}) collective-permute-start(f32[272,128]{1,0:T(8,128)S(1)} %select_select_fusion.1), channel_id=1, source_target_pairs={{0,2},{1,3},{2,0},{3,1},{4,6},{5,7},{6,4},{7,5},{8,10},{9,11},{10,... | collective-permute-start | bytes 417800 | tf_op jit(solution)/shard_map/ppermute | solution.py:558
  27.4 3.0 %collective-permute-done.3 = f32[272,128]{1,0:T(8,128)S(1)} collective-permute-done((f32[272,128]{1,0:T(8,128)S(1)}, f32[272,128]{1,0:T(8,128)S(1)}, u32[]{:S(2)}, u32[]{:S(2)}) %collective-permute-start.3) | collective-permute-done | bytes 139296 | tf_op jit(solution)/shard_map/ppermute | solution.py:558
  30.5 0.1 select_select_fusion.refs_0_
  30.6 4.0 %collective-permute-start.4 = (f32[272,128]{1,0:T(8,128)S(1)}, f32[272,128]{1,0:T(8,128)S(1)}, u32[]{:S(2)}, u32[]{:S(2)}) collective-permute-start(f32[272,128]{1,0:T(8,128)S(1)} %select_select_fusion.refs_0_), channel_id=1, source_target_pairs={{0,4},{1,5},{2,6},{3,7},{4,0},{5,1},{6,2},{7,3},{8,12},{9,13},{10,... | collective-permute-start | bytes 417800 | tf_op jit(solution)/shard_map/ppermute | solution.py:558
  34.6 4.5 %collective-permute-done.4.refs_1_ = f32[272,128]{1,0:T(8,128)S(1)} collective-permute-done((f32[272,128]{1,0:T(8,128)S(1)}, f32[272,128]{1,0:T(8,128)S(1)}, u32[]{:S(2)}, u32[]{:S(2)}) %collective-permute-start.4) | collective-permute-done | bytes 139296 | tf_op jit(solution)/shard_map/ppermute | solution.py:558
  39.1 0.1 combine.1
  39.3 0.1 collective-permute-start.5
  39.3 1.2 %collective-permute-done.5 = f32[88,128]{1,0:T(8,128)S(1)} collective-permute-done((f32[88,128]{1,0:T(8,128)S(1)}, f32[88,128]{1,0:T(8,128)S(1)}, u32[]{:S(2)}, u32[]{:S(2)}) %collective-permute-start.5) | collective-permute-done | bytes 45088 | tf_op jit(solution)/shard_map/ppermute | solution.py:588
  40.6 1.5 %collective-permute-start.6 = (f32[88,128]{1,0:T(8,128)S(1)}, f32[88,128]{1,0:T(8,128)S(1)}, u32[]{:S(2)}, u32[]{:S(2)}) collective-permute-start(f32[88,128]{1,0:T(8,128)S(1)} %add.17.refs_0_), channel_id=1, source_target_pairs={{0,16},{8,24},{16,0},{24,8},{1,17},{9,25},{17,1},{25,9},{2,18},{10... | collective-permute-start | bytes 135176 | tf_op jit(solution)/shard_map/ppermute | solution.py:588
  42.1 0.8 %latent.1 = f32[1,64,512]{2,1,0:T(8,128)} custom-call(f32[192,512]{1,0:T(8,128)S(1)} %get-tuple-element.13.grads_ref, f32[16,128]{1,0:T(8,128)S(1)} %get-tuple-element.15.aux_ref), custom_call_target="tpu_custom_call" | custom-call | tf_op jit(solution)/shard_map/latent/pallas_call | solution.py:486
  42.9 1.7 %collective-permute-done.6.refs_1_ = f32[88,128]{1,0:T(8,128)S(1)} collective-permute-done((f32[88,128]{1,0:T(8,128)S(1)}, f32[88,128]{1,0:T(8,128)S(1)}, u32[]{:S(2)}, u32[]{:S(2)}) %collective-permute-start.6) | collective-permute-done | bytes 45088 | tf_op jit(solution)/shard_map/ppermute | solution.py:588
  44.7 0.9 %final.1 = (f32[4,32,64]{2,1,0:T(8,128)}, f32[3,16,32]{2,1,0:T(8,128)}, f32[16,32]{1,0:T(8,128)}, f32[7,32]{1,0:T(8,128)}) custom-call(f32[88,128]{1,0:T(8,128)S(1)} %add.17.refs_0_, f32[88,128]{1,0:T(8,128)S(1)} %collective-permute-done.6.refs_1_), custom_call_target="tpu_custom_call" | custom-call | tf_op jit(solution)/shard_map/final/pallas_call | solution.py:486
  (9 shorter events, 0.0 us)
Async XLA Ops:
  0.6 7.9 %copy-start = (f32[4,32,64]{2,1,0:T(8,128)S(1)}, f32[4,32,64]{2,1,0:T(8,128)}, u32[]{:S(2)}) copy-start(f32[4,32,64]{2,1,0:T(8,128)} %refs_3_.1) | copy-start | bytes 98308
  0.6 7.9 %copy-start.1 = (f32[3,16,32]{2,1,0:T(8,128)S(1)}, f32[3,16,32]{2,1,0:T(8,128)}, u32[]{:S(2)}) copy-start(f32[3,16,32]{2,1,0:T(8,128)} %refs_4_.1) | copy-start | bytes 18436
  0.7 7.9 %copy-start.2 = (f32[32,16]{0,1:T(8,128)S(1)}, f32[32,16]{0,1:T(8,128)}, u32[]{:S(2)}) copy-start(f32[32,16]{0,1:T(8,128)} %param.14) | copy-start | bytes 6148
  0.7 7.9 %copy-start.3 = (f32[7,32]{1,0:T(8,128)S(1)}, f32[7,32]{1,0:T(8,128)}, u32[]{:S(2)}) copy-start(f32[7,32]{1,0:T(8,128)} %refs_6_.1) | copy-start | bytes 2692
  1.7 6.9 %collective-permute-start = (f32[72,512]{1,0:T(8,128)S(1)}, f32[72,512]{1,0:T(8,128)S(1)}, u32[]{:S(2)}, u32[]{:S(2)}) collective-permute-start(f32[72,512]{1,0:T(8,128)S(1)} %pack.1.refs_0_), channel_id=1, source_target_pairs={{0,1},{1,0},{2,3},{3,2},{4,5},{5,4},{6,7},{7,6},{8,9},{9,8},{10,11... | collective-permute-start | bytes 442376 | tf_op jit(solution)/shard_map/ppermute | solution.py:510
  4.7 3.9 %collective-permute-start.1 = (f32[72,512]{1,0:T(8,128)S(1)}, f32[72,512]{1,0:T(8,128)S(1)}, u32[]{:S(2)}, u32[]{:S(2)}) collective-permute-start(f32[72,512]{1,0:T(8,128)S(1)} %pack.1.refs_0_), channel_id=1, source_target_pairs={{1,2},{2,1},{3,4},{4,3},{5,6},{6,5},{9,10},{10,9},{11,12},{12,11},... | collective-permute-start | bytes 442376 | tf_op jit(solution)/shard_map/ppermute | solution.py:512
  16.3 8.0 %collective-permute-start.2 = (f32[272,128]{1,0:T(8,128)S(1)}, f32[272,128]{1,0:T(8,128)S(1)}, u32[]{:S(2)}, u32[]{:S(2)}) collective-permute-start(f32[272,128]{1,0:T(8,128)S(1)} %get-tuple-element.14), channel_id=1, source_target_pairs={{0,1},{1,0},{2,3},{3,2},{4,5},{5,4},{6,7},{7,6},{8,9},{9,8},{10,11... | collective-permute-start | bytes 417800 | tf_op jit(solution)/shard_map/ppermute | solution.py:558
  24.4 6.0 %collective-permute-start.3 = (f32[272,128]{1,0:T(8,128)S(1)}, f32[272,128]{1,0:T(8,128)S(1)}, u32[]{:S(2)}, u32[]{:S(2)}) collective-permute-start(f32[272,128]{1,0:T(8,128)S(1)} %select_select_fusion.1), channel_id=1, source_target_pairs={{0,2},{1,3},{2,0},{3,1},{4,6},{5,7},{6,4},{7,5},{8,10},{9,11},{10,... | collective-permute-start | bytes 417800 | tf_op jit(solution)/shard_map/ppermute | solution.py:558
  30.6 8.6 %collective-permute-start.4 = (f32[272,128]{1,0:T(8,128)S(1)}, f32[272,128]{1,0:T(8,128)S(1)}, u32[]{:S(2)}, u32[]{:S(2)}) collective-permute-start(f32[272,128]{1,0:T(8,128)S(1)} %select_select_fusion.refs_0_), channel_id=1, source_target_pairs={{0,4},{1,5},{2,6},{3,7},{4,0},{5,1},{6,2},{7,3},{8,12},{9,13},{10,... | collective-permute-start | bytes 417800 | tf_op jit(solution)/shard_map/ppermute | solution.py:558
  39.3 1.3 %collective-permute-start.5 = (f32[88,128]{1,0:T(8,128)S(1)}, f32[88,128]{1,0:T(8,128)S(1)}, u32[]{:S(2)}, u32[]{:S(2)}) collective-permute-start(f32[88,128]{1,0:T(8,128)S(1)} %get-tuple-element.16), channel_id=1, source_target_pairs={{0,8},{8,0},{16,24},{24,16},{1,9},{9,1},{17,25},{25,17},{2,10},{10... | collective-permute-start | bytes 135176 | tf_op jit(solution)/shard_map/ppermute | solution.py:588
  40.6 4.1 %collective-permute-start.6 = (f32[88,128]{1,0:T(8,128)S(1)}, f32[88,128]{1,0:T(8,128)S(1)}, u32[]{:S(2)}, u32[]{:S(2)}) collective-permute-start(f32[88,128]{1,0:T(8,128)S(1)} %add.17.refs_0_), channel_id=1, source_target_pairs={{0,16},{8,24},{16,0},{24,8},{1,17},{9,25},{17,1},{25,9},{2,18},{10... | collective-permute-start | bytes 135176 | tf_op jit(solution)/shard_map/ppermute | solution.py:588

commit v3 on v2

v3 whole, which is shorter than its diff:
```python
import jax
import jax.numpy as jnp
import numpy as np
from jax import lax
from jax.experimental import pallas as pl
from jax.experimental.pallas import tpu as pltpu
from jax.sharding import PartitionSpec as P

MELS = 64
WIN_COARSE = 1024
WIN_FINE = 256
LOSS_WEIGHTS = (0.25, 0.5, 0.5)
LANES = 128
BLOCK = 2 * LANES
STREAMS = 3
MARGIN = LANES // 2
F32 = jnp.float32
BF16 = jnp.bfloat16
VMEM = pltpu.MemorySpace.VMEM


def hi_lo(table):
    high = table.astype(np.float32).astype(BF16)
    low = (table - high.astype(np.float64)).astype(np.float32).astype(BF16)
    return high, low


def mel_table(window):
    half = window // 2
    top = 2595.0 * np.log10(1.0 + 12000.0 / 700.0)
    points = (np.arange(MELS + 1) + 1.0) / (MELS + 2.0) * top
    centers = 700.0 * (10.0 ** (points / 2595.0) - 1.0) / 12000.0 * half
    spacing = np.maximum(centers[1:] - centers[:-1], 1.0)
    places = np.arange(half)[:, None]
    return np.maximum(0.0, 1.0 - np.abs(places - centers[None, :MELS]) / spacing[None, :])


def tables():
    order = np.concatenate([np.arange(0, BLOCK, 2), np.arange(1, BLOCK, 2)])
    p = np.arange(LANES)
    cos, sin = [], []
    for rho in range(4):
        angle = 2.0 * np.pi / WIN_COARSE * ((order[:, None] * (4 * p + rho)[None, :]) % WIN_COARSE)
        cos.append(np.cos(angle))
        sin.append(np.sin(angle))
    even = np.concatenate(
        [np.concatenate([cos[0], -sin[0]], 1), np.concatenate([cos[2], -sin[2]], 1)], 0
    )
    odd = np.concatenate([cos[1], -sin[1], cos[3], -sin[3]], 1)
    angle = 2.0 * np.pi / WIN_FINE * ((order[:, None] * p[None, :]) % WIN_FINE)
    taper = 0.5 - 0.5 * np.cos(2.0 * np.pi / WIN_FINE * order)[:, None]
    fine = np.concatenate([taper * np.cos(angle), -taper * np.sin(angle)], 1)
    coarse_mel = mel_table(WIN_COARSE)
    coarse_mel = np.concatenate([coarse_mel[rho::4] for rho in (0, 2, 1, 3)], 0)
    fine_mel = mel_table(WIN_FINE)
    hann = 0.5 - 0.5 * np.cos(2.0 * np.pi / WIN_COARSE * np.arange(WIN_COARSE))
    hann = hann.reshape(4, BLOCK)[:, order].astype(np.float32)
    hann = np.concatenate([hann, np.zeros_like(hann)], 0)
    deal = np.zeros((BLOCK, BLOCK), np.float32)
    deal[order, np.arange(BLOCK)] = 1.0
    banks = [np.concatenate(hi_lo(x), 1) for x in (coarse_mel, fine_mel)]
    return (
        deal.astype(BF16),
        np.concatenate(hi_lo(even), 0),
        np.concatenate(hi_lo(odd), 0),
        hann,
        np.concatenate(hi_lo(fine), 0),
        np.concatenate(banks, 0),
    )


def split(x):
    high = x.astype(BF16)
    return high, (x - high.astype(F32)).astype(BF16)


def stacked(x):
    high = x.astype(BF16).astype(F32)
    return jnp.concatenate([high, x - high], axis=0).astype(BF16)


def dot(left, right, transposed=False):
    dims = (((1,), (1 if transposed else 0,)), ((), ()))
    return lax.dot_general(left, right, dims, preferred_element_type=F32)


def dot3(left, right_high, right_low, transposed=False):
    rows = left.shape[0]
    both = stacked(left)
    first = dot(both, right_high, transposed)
    second = dot(left.astype(BF16), right_low, transposed)
    return first[:rows] + first[rows:] + second


def to_mel(energy, bank):
    rows = energy.shape[0]
    both = dot(stacked(energy), bank)
    both = both[:rows] + both[rows:]
    return both[:, :MELS] + both[:, MELS:]


def from_mel(push, bank):
    rows = push.shape[0]
    both = dot(stacked(jnp.concatenate([push, push], axis=1)), bank, True)
    return both[:rows] + both[rows:]


def three_wide(weight):
    high = weight.astype(BF16).astype(F32)
    return jnp.concatenate([high, weight - high, high], axis=1).astype(BF16)


def apply(weight3, pair):
    high, low = pair
    return dot(weight3, jnp.concatenate([high, high, low], axis=0))


def elu_pair(x):
    slope = jnp.exp(jnp.minimum(x, 0.0))
    return jnp.where(x > 0, x, slope - 1.0), slope


def moved(x, by):
    return pltpu.roll(x, by % x.shape[1], 1)


def decode(sizes, weights, latent, keep, mask):
    half = sizes[1]
    activated, slope = elu_pair(latent)
    keep("slope_a", slope)
    both = jnp.concatenate([activated, moved(activated, 1)], 0)
    pair = split(both)
    keep("a", pair)
    upper = apply(weights["up"], pair) * mask
    rect, slope = elu_pair(upper)
    keep("slope_u", slope)
    pair = split(
        jnp.concatenate([moved(rect[half:], 1), rect, moved(rect[:half], -1)], 0)
    )
    keep("e", pair)
    hid, slope = elu_pair(apply(weights["inner"], pair))
    keep("slope_c", slope)
    pair = split(hid)
    keep("h", pair)
    mixed = (upper + apply(weights["outer"], pair)) * mask
    rect, slope = elu_pair(mixed)
    keep("slope_m", slope)
    pair = split(rect)
    keep("g", pair)
    taps = apply(weights["out"], pair)
    plus1, plus2, minus1, minus2 = (moved(taps, by) for by in (1, 2, -1, -2))
    return (
        (plus2[0:1] + plus1[2:3] + taps[4:5] + minus1[6:7]) * mask,
        (plus1[1:2] + taps[3:4] + minus1[5:6] + minus2[7:8]) * mask,
    )


KEPT = ("slope_a", "a_h", "a_l", "slope_u", "e_h", "e_l", "slope_c", "h_h", "h_l", "slope_m", "g_h", "g_l")


def kept_shapes(channels, half, hidden, window):
    rows = (channels, 2 * channels, 2 * half, 4 * half, 2 * hidden, 2 * hidden, 2 * half, 2 * half)
    shapes = []
    for i in range(4):
        shapes.append(((rows[2 * i], window), F32))
        shapes += [((rows[2 * i + 1], window), BF16)] * 2
    return shapes


def forward_weights(sizes, up, inner, outer, out, square):
    channels, half, hidden, _ = sizes
    weights = {}
    weights["up"] = three_wide(
        jnp.concatenate(
            [jnp.concatenate([up[r], up[r + 2]], axis=1) for r in range(2)], axis=0
        )
    )
    square[...] = jnp.zeros_like(square)
    for j in range(3):
        square[0:hidden, j * half : (j + 1) * half] = inner[j]
        square[hidden : 2 * hidden, (j + 1) * half : (j + 2) * half] = inner[j]
    weights["inner"] = three_wide(square[0 : 2 * hidden, :])
    square[...] = jnp.zeros_like(square)
    square[0:hidden, 0:half] = outer[...]
    square[hidden : 2 * hidden, half : 2 * half] = outer[...]
    weights["outer"] = three_wide(jnp.transpose(square[...])[0 : 2 * half, 0 : 2 * hidden])
    square[...] = jnp.zeros_like(square)
    square[1:8, 0:half] = out[...]
    square[0:7, half : 2 * half] = out[...]
    weights["out"] = three_wide(square[0:8, 0 : 2 * half])
    return weights


FORWARD = ("up", "inner", "outer", "out")


def backward_kernel(sizes, *refs):
    up, inner, outer, out = refs[:4]
    up_ref, inner_ref, outer_ref, out_ref = refs[8:12]
    square, sems = refs[15:]
    copies = [pltpu.make_async_copy(refs[5 + i], refs[12 + i], sems.at[i]) for i in range(3)]
    for copy in copies:
        copy.start()
    channels, half, hidden, _ = sizes
    for r in range(4):
        square[r * half : (r + 1) * half, 0:channels] = up[r]
        square[r * half : (r + 1) * half, channels:] = up[r]
    up_ref[...] = three_wide(jnp.transpose(square[...])[0:channels, :])
    square[...] = jnp.zeros_like(square)
    for j in range(3):
        square[(2 - j) * hidden : (3 - j) * hidden, 0:half] = inner[j]
        square[(3 - j) * hidden : (4 - j) * hidden, half : 2 * half] = inner[j]
    inner_ref[...] = three_wide(jnp.transpose(square[...])[0 : 2 * half, 0 : 4 * hidden])
    square[...] = jnp.zeros_like(square)
    square[0:hidden, 0:half] = outer[...]
    square[hidden : 2 * hidden, half : 2 * half] = outer[...]
    outer_ref[...] = three_wide(square[0 : 2 * hidden, 0 : 2 * half])
    square[...] = jnp.zeros_like(square)
    square[1:8, 0:half] = out[...]
    square[0:7, half : 2 * half] = out[...]
    out_ref[...] = three_wide(jnp.transpose(square[...])[0 : 2 * half, 0:8])
    for copy in copies:
        copy.wait()


def own_kernel(sizes, *refs):
    sources = refs[:9]
    packet_ref, latent_ref = refs[9:11]
    weight_refs = refs[11:15]
    kept = dict(zip(KEPT, refs[15:27]))
    table_refs = refs[27:29]
    up_ref, inner_ref, outer_ref, out_ref, target_ref, deal_ref, square, rows_ref, sems = refs[29:]
    channels, half, hidden, frames = sizes
    spaces = (latent_ref, target_ref, up_ref, inner_ref, outer_ref, out_ref, deal_ref, *table_refs)
    copies = []
    for i, (source, space) in enumerate(zip(sources, spaces)):
        if i == 0:
            source = source.at[0]
        copies.append(pltpu.make_async_copy(source, space, sems.at[i]))
    for copy in copies:
        copy.start()
    for copy in copies[:7]:
        copy.wait()
    weights = forward_weights(sizes, up_ref, inner_ref, outer_ref, out_ref, square)
    for name, ref in zip(FORWARD, weight_refs):
        ref[...] = weights[name]

    def keep(name, value):
        if isinstance(value, tuple):
            kept[name + "_h"][...], kept[name + "_l"][...] = value
        else:
            kept[name][...] = value

    latent = latent_ref[...]
    spread = moved(jnp.concatenate([latent, jnp.zeros((channels, LANES), F32)], 1), MARGIN)
    wave = jnp.concatenate(decode(sizes, weights, spread, keep, 1.0), 0)
    wave = moved(wave, -MARGIN)
    blocks = frames // LANES
    rows_ref[...] = jnp.zeros_like(rows_ref)
    for b in range(blocks):
        rows_ref[b : b + 1, :] = target_ref[:, b * BLOCK : (b + 1) * BLOCK]
    whole = rows_ref[...]
    high = whole.astype(BF16)
    rest = whole - high.astype(F32)
    middle = rest.astype(BF16)
    last = (rest - middle.astype(F32)).astype(BF16)
    deal = deal_ref[...]
    dealt = dot(high, deal) + dot(middle, deal) + dot(last, deal)
    packet_ref[0:8, 0:channels] = jnp.transpose(latent[:, 0:LANES])[0:8]
    packet_ref[0:8, channels:] = jnp.transpose(latent[:, frames - LANES :])[LANES - 8 :]
    for r in range(2):
        for b in range(blocks):
            packet_ref[8 + r * blocks + b : 9 + r * blocks + b, :] = wave[
                r : r + 1, b * LANES : (b + 1) * LANES
            ]
        at = 8 + (2 + r) * blocks
        packet_ref[at : at + blocks, :] = dealt[0:blocks, r * LANES : (r + 1) * LANES]
    for copy in copies[7:]:
        copy.wait()


def main_kernel(sizes, *refs):
    own_ref, first_ref, second_ref, latent_ref = refs[:4]
    weights = {name: ref[...] for name, ref in zip(FORWARD, refs[4:8])}
    kept = dict(zip(KEPT, refs[8:20]))
    up_back, back_inner, outer_back, out_back = (ref[...] for ref in refs[20:24])
    even_ref, odd_ref, hann_ref, fine_ref, bank_ref = refs[24:29]
    payload_ref, grads_ref = refs[29:31]
    (square, wblock, shifted, wave_b, targ_b, lanes_b) = refs[31:37]
    channels, half, hidden, frames = sizes
    window = frames + LANES
    own_blocks = frames // LANES
    index = lax.axis_index("tm")
    count = lax.axis_size("tm")
    odd_place = lax.rem(index, 2) == 1

    first, second = first_ref[...], second_ref[...]
    left = jnp.where(odd_place, first, second)
    right = jnp.where(odd_place, second, first)
    square[...] = jnp.zeros_like(square)
    square[MARGIN - 8 : MARGIN, 0:channels] = left[0:8, channels:]
    square[MARGIN : MARGIN + 8, channels:] = right[0:8, 0:channels]
    turned = jnp.transpose(square[...])
    lane = lax.broadcasted_iota(jnp.int32, (1, LANES), 1)
    ends = jnp.concatenate(
        [
            jnp.where(lane < MARGIN, turned[0:channels], moved(latent_ref[:, 0:LANES], MARGIN)),
            jnp.where(
                lane < MARGIN, moved(latent_ref[:, frames - LANES :], MARGIN), turned[channels:]
            ),
        ],
        axis=1,
    )
    place = lax.broadcasted_iota(jnp.int32, (1, window), 1) + index * frames - MARGIN
    mask = ((place >= 0) & (place < count * frames)).astype(F32)
    ends_mask = jnp.concatenate([mask[:, :LANES], mask[:, window - LANES :]], axis=1)
    saved = {}

    def joined(name, value):
        inside = kept[name]
        quarter = LANES // 4
        lane = lax.broadcasted_iota(jnp.int32, (value.shape[0], LANES), 1)
        head = jnp.where(lane < 3 * quarter, value[:, :LANES], inside[:, :LANES])
        tail = jnp.where(lane >= quarter, value[:, LANES:], inside[:, window - LANES :])
        saved[name] = jnp.concatenate([head, inside[:, LANES : window - LANES], tail], axis=1)

    def keep(name, value):
        if isinstance(value, tuple):
            joined(name + "_h", value[0])
            joined(name + "_l", value[1])
        else:
            joined(name, value)

    ends_wave = decode(sizes, weights, ends, keep, ends_mask)
    slope_a, slope_u, slope_c, slope_m = (saved["slope_" + x] for x in "aucm")

    for side, packet in enumerate((left, own_ref[...], right)):
        rows = slice(side * own_blocks, (side + 1) * own_blocks)
        for r in range(2):
            columns = slice(r * LANES, (r + 1) * LANES)
            at = 8 + r * own_blocks
            wave_b[rows, columns] = packet[at : at + own_blocks]
            at = 8 + (2 + r) * own_blocks
            targ_b[rows, columns] = packet[at : at + own_blocks]
    for r in range(2):
        columns = slice(r * LANES, (r + 1) * LANES)
        for side in range(2):
            piece = moved(ends_wave[r][:, side * LANES : (side + 1) * LANES], MARGIN)
            row = own_blocks * (1 + side)
            wave_b[row - 1 : row, columns] = jnp.where(
                lane >= LANES - 4, piece, wave_b[row - 1 : row, columns]
            )
            wave_b[row : row + 1, columns] = jnp.where(lane < 4, piece, wave_b[row : row + 1, columns])
    size = 2 * BLOCK
    even_h, even_l = even_ref.at[pl.ds(0, size)], even_ref.at[pl.ds(size, size)]
    odd_h, odd_l = odd_ref[0:BLOCK], odd_ref[BLOCK:]
    fine_h, fine_l = fine_ref.at[pl.ds(0, BLOCK)], fine_ref.at[pl.ds(BLOCK, BLOCK)]
    coarse_bank, fine_bank = bank_ref[0:size], bank_ref[size:]

    row_count = own_blocks + 4
    start = own_blocks - 3
    parts = []
    for j in range(4):
        rows = jnp.concatenate(
            [wave_b[pl.ds(start + j, row_count), :], targ_b[pl.ds(start + j, row_count), :]], 0
        )
        parts.append(rows * hann_ref[j : j + 1, :])
    even_sum, odd_sum = parts[0] + parts[2], parts[1] + parts[3]
    turned = jnp.concatenate([parts[0] - parts[2], parts[1] - parts[3]], axis=0)
    spec0 = dot3(even_sum + odd_sum, even_h[0:BLOCK], even_l[0:BLOCK])
    spec2 = dot3(even_sum - odd_sum, even_h[BLOCK:], even_l[BLOCK:])
    spec1 = dot3(turned, odd_h, odd_l)
    rows = 2 * row_count
    quarter = [(spec1[:rows, at : at + LANES], spec1[rows:, at : at + LANES]) for at in range(0, size, LANES)]
    real = jnp.concatenate(
        [
            spec0[:, :LANES],
            spec2[:, :LANES],
            quarter[0][0] + quarter[1][1],
            quarter[2][0] - quarter[3][1],
        ],
        1,
    )
    imag = jnp.concatenate(
        [
            spec0[:, LANES:],
            spec2[:, LANES:],
            quarter[1][0] - quarter[0][1],
            quarter[3][0] + quarter[2][1],
        ],
        1,
    )
    mel = to_mel(real * real + imag * imag, coarse_bank)
    level = jnp.sqrt(mel + 1.0)
    level_wave = level[:row_count]
    frame = lax.broadcasted_iota(jnp.int32, (row_count, MELS), 0) + index * own_blocks - 3
    slope = jnp.where(frame >= 0, (level_wave - level[row_count:]) / level_wave, 0.0)
    push = 2.0 * from_mel(slope, coarse_bank)
    real, imag = real[:row_count] * push, imag[:row_count] * push
    back0 = dot3(
        jnp.concatenate([real[:, :LANES], imag[:, :LANES]], 1), even_h[0:BLOCK], even_l[0:BLOCK], True
    )
    back2 = dot3(
        jnp.concatenate([real[:, LANES:BLOCK], imag[:, LANES:BLOCK]], 1),
        even_h[BLOCK:],
        even_l[BLOCK:],
        True,
    )
    real1, real3 = real[:, BLOCK : BLOCK + LANES], real[:, BLOCK + LANES :]
    imag1, imag3 = imag[:, BLOCK : BLOCK + LANES], imag[:, BLOCK + LANES :]
    back1 = dot3(
        jnp.concatenate(
            [
                jnp.concatenate([real1, imag1, real3, imag3], 1),
                jnp.concatenate([-imag1, real1, imag3, -real3], 1),
            ],
            0,
        ),
        odd_h,
        odd_l,
        True,
    )
    back1 = [back1[:row_count], back1[row_count:]]
    plus, minus = back0 + back2, back0 - back2
    backs = [
        plus + back1[0],
        minus + back1[1],
        plus - back1[0],
        minus - back1[1],
    ]
    coarse = jnp.zeros((own_blocks, BLOCK), F32)
    for j in range(4):
        coarse = coarse + (backs[j] * hann_ref[j : j + 1, :])[3 - j : 3 - j + own_blocks]

    hop = LANES // 4
    lane = lax.broadcasted_iota(jnp.int32, (1, LANES), 1)
    start = own_blocks - 1
    for which, source in enumerate((wave_b, targ_b)):
        for s in range(4):
            base = (which * 4 + s) * row_count
            for r in range(2):
                here = source[pl.ds(start, row_count), r * LANES : (r + 1) * LANES]
                if s:
                    there = source[pl.ds(start + 1, row_count), r * LANES : (r + 1) * LANES]
                    here = jnp.where(
                        lane < LANES - s * hop,
                        pltpu.roll(here, LANES - s * hop, 1),
                        pltpu.roll(there, LANES - s * hop, 1),
                    )
                shifted[base : base + row_count, r * LANES : (r + 1) * LANES] = here
    spec = dot3(shifted[...], fine_h[...], fine_l[...])
    real, imag = spec[:, :LANES], spec[:, LANES:]
    mel = to_mel(real * real + imag * imag, fine_bank)
    level = jnp.sqrt(mel + 1.0)
    fine_rows = 4 * row_count
    level_wave = level[:fine_rows]
    row = lax.broadcasted_iota(jnp.int32, (fine_rows, MELS), 0)
    frame = (lax.rem(row, row_count) - 1 + index * own_blocks) * 4 + row // row_count
    slope = jnp.where(frame >= 0, (level_wave - level[fine_rows:]) / level_wave, 0.0)
    push = 2.0 * from_mel(slope, fine_bank)
    back = dot3(
        jnp.concatenate([real[:fine_rows] * push, imag[:fine_rows] * push], 1),
        fine_h[...],
        fine_l[...],
        True,
    )
    fine = []
    for r in range(2):
        total = jnp.zeros((own_blocks, LANES), F32)
        for s in range(4):
            piece = back[s * row_count : (s + 1) * row_count, r * LANES : (r + 1) * LANES]
            if s:
                piece = pltpu.roll(piece, s * hop, 1)
                total = total + jnp.where(
                    lane >= s * hop, piece[1 : 1 + own_blocks], piece[0:own_blocks]
                )
            else:
                total = total + piece[1 : 1 + own_blocks]
        fine.append(total)
    fine = jnp.concatenate(fine, axis=1)

    own_rows = pl.ds(own_blocks, own_blocks)
    timed = 2.0 * (wave_b[own_rows, :] - targ_b[own_rows, :])

    totals, views, uppers, inners, mixeds, edges = [], [], [], [], [], []
    for i, stream in enumerate((timed, coarse, fine)):
        totals.append(jnp.sum(stream * stream))
        lanes_b[i] = jnp.zeros((8, window), F32)
        for b in range(own_blocks):
            for r in range(2):
                lanes_b[i, r : r + 1, b * LANES : (b + 1) * LANES] = stream[
                    b : b + 1, r * LANES : (r + 1) * LANES
                ]
        evens, odds = lanes_b[i, 0:1, :], lanes_b[i, 1:2, :]
        for k in range(8):
            source = odds if k % 2 else evens
            lanes_b[i, k : k + 1, :] = moved(source, MARGIN - (4 - k) // 2)
        view = lanes_b[i]
        views.append(view)
        high = view.astype(BF16).astype(F32)
        three = jnp.concatenate([high, high, view - high], axis=0).astype(BF16)
        grad_mixed = dot(out_back, three) * slope_m * mask
        mixed = split(grad_mixed)
        mixeds.append(mixed)
        grad_inner = apply(outer_back, mixed) * slope_c
        inners.append(split(grad_inner))
        spread = jnp.concatenate(
            [moved(grad_inner[hidden:], 1), grad_inner, moved(grad_inner[:hidden], -1)], 0
        )
        grad_upper = (grad_mixed + apply(back_inner, split(spread)) * slope_u) * mask
        uppers.append(split(grad_upper))
        both = jnp.concatenate([grad_upper, moved(grad_upper, -1)], 0)
        grads = moved(apply(up_back, split(both)) * slope_a * mask, -MARGIN)
        grads_ref[i * channels : (i + 1) * channels, :] = grads[:, :frames]
        turned = jnp.transpose(grads[:, frames:])
        edges.append(jnp.concatenate([turned[LANES - 8 :], turned[:8]], axis=1))

    def summed(pairs, name):
        rows = pairs[0][0].shape[0]
        both = jnp.concatenate([x for pair in pairs for x in pair], axis=0)
        highs = jnp.concatenate([pair[0] for pair in pairs], axis=0)
        first = dot(both, saved[name + "_h"], True)
        second = dot(highs, saved[name + "_l"], True)
        return [
            first[2 * i * rows : (2 * i + 1) * rows]
            + first[(2 * i + 1) * rows : (2 * i + 2) * rows]
            + second[i * rows : (i + 1) * rows]
            for i in range(STREAMS)
        ]

    for i, value in enumerate(summed(uppers, "a")):
        payload_ref[i * 2 * half : (i + 1) * 2 * half, :] = value
    base = STREAMS * 2 * half
    for i, value in enumerate(summed(inners, "e")):
        at = base + i * hidden
        payload_ref[at : at + hidden, 0 : 3 * half] = value[:hidden, : 3 * half] + value[hidden:, half:]
    highs = jnp.concatenate([pair[0] for pair in mixeds], axis=0)
    lows = jnp.concatenate([pair[1] for pair in mixeds], axis=0)
    both = jnp.concatenate([saved["h_h"], saved["h_l"]], axis=0)
    first = dot(both, highs, True)
    value = first[: 2 * hidden] + first[2 * hidden :] + dot(saved["h_h"], lows, True)
    for i in range(STREAMS):
        at = base + i * hidden
        columns = i * 2 * half
        payload_ref[at : at + hidden, 3 * half : 4 * half] = (
            value[:hidden, columns : columns + half] + value[hidden:, columns + half : columns + 2 * half]
        )
    taps = dot3(jnp.concatenate(views, axis=0), saved["g_h"], saved["g_l"], True)
    for i in range(STREAMS):
        wblock[0:7, i * half : (i + 1) * half] = (
            taps[8 * i + 1 : 8 * i + 8, :half] + taps[8 * i : 8 * i + 7, half:]
        )
    base = STREAMS * (2 * half + hidden)
    lane = lax.broadcasted_iota(jnp.int32, (1, half), 1)
    sums = jnp.where(lane == 0, totals[0], jnp.where(lane == 1, totals[1], totals[2]))
    wblock[7:8, :] = jnp.zeros((1, 4 * half), F32)
    wblock[0:7, STREAMS * half :] = jnp.zeros((7, half), F32)
    wblock[7:8, STREAMS * half :] = sums
    payload_ref[base : base + 8, :] = wblock[...]
    payload_ref[base + 8 :, :] = jnp.concatenate(edges, axis=0)


def combine_kernel(sizes, mine_ref, theirs_ref, weights_ref, aux_ref):
    half, hidden, samples = sizes
    rows = STREAMS * (2 * half + hidden)
    total = mine_ref[0 : rows + 8, :] + theirs_ref[0 : rows + 8, :]
    line = total[rows + 7 : rows + 8, :]
    lane = lax.broadcasted_iota(jnp.int32, line.shape, 1) - STREAMS * half
    wanted = jnp.where(lane == 0, LOSS_WEIGHTS[0], jnp.where(lane == 1, LOSS_WEIGHTS[1], LOSS_WEIGHTS[2]))
    line = wanted / jnp.sqrt(line / samples + 1e-06)
    scale = [
        jnp.sum(jnp.where(lane == i, line, 0.0), axis=1, keepdims=True) for i in range(STREAMS)
    ]
    up = sum(total[i * 2 * half : (i + 1) * 2 * half] * scale[i] for i in range(STREAMS))
    base = STREAMS * 2 * half
    inner = sum(total[base + i * hidden : base + (i + 1) * hidden] * scale[i] for i in range(STREAMS))
    last = total[rows : rows + 8]
    out = sum(
        (pltpu.roll(last, (4 - i) * half % (4 * half), 1) if i else last) * scale[i]
        for i in range(STREAMS)
    )
    place = lax.broadcasted_iota(jnp.int32, out.shape, 0)
    lane = lax.broadcasted_iota(jnp.int32, out.shape, 1)
    weights_ref[0 : 2 * half, :] = up
    weights_ref[2 * half : 2 * half + hidden, :] = inner
    weights_ref[2 * half + hidden :, :] = jnp.where((place < 7) & (lane < half), out, 0.0)
    index = lax.axis_index("tm")
    step = lax.axis_size("tm") // 2
    low = lax.rem(index, step)
    edge_lane = lax.broadcasted_iota(jnp.int32, (1, LANES), 1)
    swap = ((low == 0) & (edge_lane >= LANES // 2)) | ((low == step - 1) & (edge_lane < LANES // 2))
    edges = jnp.where(swap, theirs_ref[rows + 8 :, :], mine_ref[rows + 8 :, :])
    aux_ref[0:8, :] = sum(edges[8 * i : 8 * i + 8] * scale[i] for i in range(STREAMS))
    for i in range(STREAMS):
        aux_ref[8 + i : 9 + i, :] = jnp.broadcast_to(scale[i], (1, LANES))


def latent_kernel(channels, grads_ref, aux_ref, square, grad_ref):
    frames = grads_ref.shape[1]
    total = sum(
        grads_ref[i * channels : (i + 1) * channels, :] * aux_ref[8 + i : 9 + i, 0:1]
        for i in range(STREAMS)
    )
    grad_ref[0] = total
    square[...] = jnp.zeros_like(square)
    square[0:8, 0:channels] = aux_ref[0:8, channels:]
    square[LANES - 8 :, channels:] = aux_ref[0:8, 0:channels]
    turned = jnp.transpose(square[...])
    grad_ref[0, :, 0:LANES] = grad_ref[0, :, 0:LANES] + turned[0:channels]
    grad_ref[0, :, frames - LANES :] = grad_ref[0, :, frames - LANES :] + turned[channels:]


def final_kernel(sizes, mine_ref, theirs_ref, up_ref, inner_ref, outer_ref, out_ref):
    channels, half, hidden, params = sizes
    total = mine_ref[...] + theirs_ref[...]
    squares = jnp.sum(total * total)
    factor = jnp.minimum(1.0, 1.0 / jnp.sqrt(jnp.full((1, 1), squares / params + 1e-06, F32)))
    total = total * factor
    for r in range(2):
        up_ref[r] = total[r * half : (r + 1) * half, 0:channels]
        up_ref[r + 2] = total[r * half : (r + 1) * half, channels:]
    inner = total[2 * half : 2 * half + hidden]
    for j in range(3):
        inner_ref[j] = inner[:, j * half : (j + 1) * half]
    outer_ref[...] = inner[:, 3 * half :]
    out_ref[...] = total[2 * half + hidden : 2 * half + hidden + 7, 0:half]


def run(kernel, out_shape, operands, scratch, name, mebibytes, left=0):
    spec = pl.BlockSpec(memory_space=VMEM)
    kept = len(operands) - left
    hbm = [pltpu.with_memory_space_constraint(x, pltpu.MemorySpace.HBM) for x in operands[kept:]]
    operands = [*operands[:kept], *hbm]
    stay = pl.BlockSpec(memory_space=pltpu.MemorySpace.HBM)
    return pl.pallas_call(
        kernel,
        out_shape=tuple(
            jax.ShapeDtypeStruct(*(x if isinstance(x[1], type) else (x, F32))) for x in out_shape
        ),
        in_specs=[spec] * (len(operands) - left) + [stay] * left,
        out_specs=tuple([spec] * len(out_shape)),
        scratch_shapes=scratch,
        compiler_params=pltpu.CompilerParams(vmem_limit_bytes=mebibytes << 20),
        name=name,
    )(*operands)


def local(latent, target, up_kernel, inner_kernel, outer_kernel, out_kernel):
    assert latent.shape[0] == 1
    channels, frames = latent.shape[1:]
    half, hidden = outer_kernel.shape
    window = frames + LANES
    blocks = frames // LANES
    count = lax.axis_size("tm")
    samples = target.shape[1] * count
    params = sum(x.size for x in (up_kernel, inner_kernel, outer_kernel, out_kernel))

    constants = tables()
    sizes = (channels, half, hidden, frames)
    weights = [up_kernel, inner_kernel, outer_kernel.T, out_kernel]
    forward = [
        ((2 * half, 6 * channels), BF16),
        ((2 * hidden, 12 * half), BF16),
        ((2 * half, 6 * hidden), BF16),
        ((8, 6 * half), BF16),
    ]
    own, own_latent, *made, even, odd = run(
        lambda *refs: own_kernel(sizes, *refs),
        [
            (8 + 4 * blocks, LANES),
            (channels, frames),
            *forward,
            *kept_shapes(channels, half, hidden, window),
            *[(x.shape, BF16) for x in constants[1:3]],
        ],
        [latent, target, *weights, *constants[:3]],
        [
            *[pltpu.VMEM(x.shape, F32) for x in weights],
            pltpu.VMEM(target.shape, F32),
            pltpu.VMEM((BLOCK, BLOCK), BF16),
            pltpu.VMEM((LANES, LANES), F32),
            pltpu.VMEM((8, BLOCK), F32),
            pltpu.SemaphoreType.DMA((9,)),
        ],
        "own_decode",
        8,
        9,
    )
    backward = run(
        lambda *refs: backward_kernel(sizes, *refs),
        [
            ((channels, 12 * half), BF16),
            ((2 * half, 12 * hidden), BF16),
            ((2 * hidden, 6 * half), BF16),
            ((2 * half, 24), BF16),
            constants[3].shape,
            *[(x.shape, BF16) for x in constants[4:]],
        ],
        [*weights, own, *constants[3:]],
        [pltpu.VMEM((LANES, LANES), F32), pltpu.SemaphoreType.DMA((3,))],
        "backward_weights",
        4,
        3,
    )
    pairs = [(i, i ^ 1) for i in range(count) if i ^ 1 < count]
    first = lax.ppermute(own, "tm", pairs)
    pairs = [(i, i + 1 if i % 2 else i - 1) for i in range(count)]
    second = lax.ppermute(own, "tm", [(a, b) for a, b in pairs if 0 <= b < count])

    rows = STREAMS * (2 * half + hidden)

    payload, grads = run(
        lambda *refs: main_kernel(sizes, *refs),
        [(rows + 8 + 8 * STREAMS, LANES), (STREAMS * channels, frames)],
        [own, first, second, own_latent, *made, *backward[:4], even, odd, *backward[4:]],
        [
            pltpu.VMEM((LANES, LANES), F32),
            pltpu.VMEM((8, 4 * half), F32),
            pltpu.VMEM((8 * (blocks + 4), BLOCK), F32),
            pltpu.VMEM((3 * blocks, BLOCK), F32),
            pltpu.VMEM((3 * blocks, BLOCK), F32),
            pltpu.VMEM((STREAMS, 8, window), F32),
        ],
        "losses",
        16,
    )

    index = lax.axis_index("tm")
    line = lax.broadcasted_iota(jnp.int32, payload.shape, 0)
    lane = lax.broadcasted_iota(jnp.int32, payload.shape, 1)
    step = 1
    while True:
        theirs = lax.ppermute(payload, "tm", [(i, i ^ step) for i in range(count)])
        if 2 * step == count:
            break
        low = index % step
        swap = ((low == 0) & (lane >= LANES // 2)) | ((low == step - 1) & (lane < LANES // 2))
        payload = jnp.where(
            line < rows + 8, payload + theirs, jnp.where(swap, theirs, payload)
        )
        step *= 2

    weights, aux = run(
        lambda *refs: combine_kernel((half, hidden, samples), *refs),
        [(2 * half + hidden + 8, LANES), (16, LANES)],
        [payload, theirs],
        [],
        "combine",
        2,
    )
    (latent_grad,) = run(
        lambda grads_ref, aux_ref, out, square: latent_kernel(channels, grads_ref, aux_ref, square, out),
        [latent.shape],
        [grads, aux],
        [pltpu.VMEM((LANES, LANES), F32)],
        "latent",
        2,
    )

    count = lax.axis_size("dp")
    step = 1
    while True:
        theirs = lax.ppermute(weights, "dp", [(i, i ^ step) for i in range(count)])
        if 2 * step == count:
            break
        weights = weights + theirs
        step *= 2
    up, inner, outer, out = run(
        lambda *refs: final_kernel((channels, half, hidden, params), *refs),
        [up_kernel.shape, inner_kernel.shape, outer_kernel.shape[::-1], out_kernel.shape],
        [weights, theirs],
        [],
        "final",
        2,
    )
    return (latent_grad, up, inner, outer.T, out)


def solution(mesh):
    for axis in ("dp", "tm"):
        size = mesh.shape[axis]
        assert size > 1 and size & (size - 1) == 0
    placed = (P("dp", None, "tm"), P("dp", "tm"), P(), P(), P(), P())
    return jax.shard_map(
        local,
        mesh=mesh,
        in_specs=placed,
        out_specs=(P("dp", None, "tm"), P(), P(), P(), P()),
        check_vma=False,
    )
```

time: 45.7 us -> 43.6 us (0.954)
  waiting for transfers between devices: 16.7 us -> 13.5 us
  starting transfers between devices: 17.3 us -> 18.1 us
    ppermute x1, waiting for transfers between devices: 3.18 us -> 0.01 us  [local(): first = lax.ppermute(own, 'tm', pairs)]
    ppermute x3, starting transfers between devices: 12 us -> 12.8 us  [local(): theirs = lax.ppermute(payload, 'tm', [(i, i ^ step) for i in range(count)])]
    pallas_call x5 -> x6, Pallas kernels: 10.5 us -> 10.8 us  [run(): pl.pallas_call(kernel, out_shape=tuple((jax.ShapeDtypeStruct(*(x if isins...]
  transfers between devices with their start and end apart: 7 -> 7, of which waited for: 6 -> 5; matrix products, arithmetic and copies ran while one was open for 0% -> 0% of each run, Pallas kernels for 2% -> 4%
where the time goes in v3:
time: 43.6 us; the launch traced here: 43.4 us
  starting transfers between devices  18.1 us (42%)
  waiting for transfers between devices  13.5 us (31%)
  Pallas kernels  10.8 us (25%)
  between operations  0.78 us (2%)
    ppermute x3, starting transfers between devices, local(): theirs = lax.ppermute(payload, 'tm', [(i, i ^ step) for i in range(count)])  12.8 us
    pallas_call x6, Pallas kernels, run(): pl.pallas_call(kernel, out_shape=tuple((jax.ShapeDtypeStruct(*(x if isins...  10.8 us
    ppermute x3, waiting for transfers between devices, local(): theirs = lax.ppermute(payload, 'tm', [(i, i ^ step) for i in range(count)])  10.6 us
    ppermute x1, starting transfers between devices, local(): first = lax.ppermute(own, 'tm', pairs)  3.06 us
    ppermute x2, waiting for transfers between devices, local(): theirs = lax.ppermute(weights, 'dp', [(i, i ^ step) for i in range(count)])  2.94 us
    ppermute x2, starting transfers between devices, local(): theirs = lax.ppermute(weights, 'dp', [(i, i ^ step) for i in range(count)])  1.62 us
  transfers between devices with their start and end apart: 7, of which 5 were waited for; matrix products, arithmetic and copies ran while one was open for 0% of the time, Pallas kernels for 4%

profile of v3, /device:TPU:0, one launch (start us, length us, event | category | flops | bytes accessed | tf_op | source)
XLA Modules:
  0.0 43.4 jit_solution(11594906070508452379)
XLA Ops:
  0.6 0.0 copy-start
  0.6 0.0 copy-start.1
  0.7 2.5 %own_decode.1 = (f32[24,128]{1,0:T(8,128)S(1)}, f32[64,512]{1,0:T(8,128)S(1)}, bf16[64,384]{1,0:T(8,128)(2,1)S(1)}, bf16[32,384]{1,0:T(8,128)(2,1)S(1)}, bf16[64...) custom-call(f32[1,64,512]{2,1,0:T(8,128)} %refs_0_.2, ...), custom_call_target="tpu_custom_call" | custom-call | tf_op jit(solution)/shard_map/own_decode/pallas_call | solution.py:635
  3.1 3.1 %collective-permute-start = (f32[24,128]{1,0:T(8,128)S(1)}, f32[24,128]{1,0:T(8,128)S(1)}, u32[]{:S(2)}, u32[]{:S(2)}) collective-permute-start(f32[24,128]{1,0:T(8,128)S(1)} %get-tuple-element.40.refs_4_.refs_0_), channel_id=1, source_target_pairs={{0,1},{1,0},{2,3},{3,2},{4,5},{5,4},{6,7},{7,6},{8,9},{9,8},{10,11... | collective-permute-start | bytes 36872 | tf_op jit(solution)/shard_map/ppermute | solution.py:706
  6.2 0.7 %collective-permute-start.1 = (f32[24,128]{1,0:T(8,128)S(1)}, f32[24,128]{1,0:T(8,128)S(1)}, u32[]{:S(2)}, u32[]{:S(2)}) collective-permute-start(f32[24,128]{1,0:T(8,128)S(1)} %get-tuple-element.40.refs_4_.refs_0_), channel_id=1, source_target_pairs={{1,2},{2,1},{3,4},{4,3},{5,6},{6,5},{9,10},{10,9},{11,12},{12,11},... | collective-permute-start | bytes 36872 | tf_op jit(solution)/shard_map/ppermute | solution.py:708
  6.9 1.0 %backward_weights.1 = (bf16[64,384]{1,0:T(8,128)(2,1)S(1)}, bf16[64,192]{1,0:T(8,128)(2,1)S(1)}, bf16[32,192]{1,0:T(8,128)(2,1)S(1)}, bf16[64,24]{1,0:T(8,128)(2...) custom-call(f32[4,32,64]{2,1,0:T(8,128)S(1)} %copy-done, ...), custom_call_target="tpu_custom_call" | custom-call | tf_op jit(solution)/shard_map/backward_weights/pallas_call | solution.py:635
  7.9 0.0 collective-permute-done.refs_1_
  8.0 0.0 collective-permute-done.1.refs_2_
  8.0 5.5 %losses.1 = (f32[272,128]{1,0:T(8,128)S(1)}, f32[192,512]{1,0:T(8,128)S(1)}) custom-call(f32[24,128]{1,0:T(8,128)S(1)} %get-tuple-element.40.refs_4_.refs_0_, f32[24,128]{1,0:T(8,128)S(1)} %collective-permute-done.refs_1_, f32[24,128]{1,0:T(8,128)S(1)} %collective-permute-done.1.refs_2_, f32[64,512]{1,0:T(8,128)S(1)} %get-tuple-element.41.refs_3_, ...), custom_call_target="tpu_custom_call" | custom-call | tf_op jit(solution)/shard_map/losses/pallas_call | solution.py:635
  13.5 4.9 %collective-permute-start.2 = (f32[272,128]{1,0:T(8,128)S(1)}, f32[272,128]{1,0:T(8,128)S(1)}, u32[]{:S(2)}, u32[]{:S(2)}) collective-permute-start(f32[272,128]{1,0:T(8,128)S(1)} %get-tuple-element.68), channel_id=1, source_target_pairs={{0,1},{1,0},{2,3},{3,2},{4,5},{5,4},{6,7},{7,6},{8,9},{9,8},{10,11... | collective-permute-start | bytes 417800 | tf_op jit(solution)/shard_map/ppermute | solution.py:733
  18.3 3.0 %collective-permute-done.2 = f32[272,128]{1,0:T(8,128)S(1)} collective-permute-done((f32[272,128]{1,0:T(8,128)S(1)}, f32[272,128]{1,0:T(8,128)S(1)}, u32[]{:S(2)}, u32[]{:S(2)}) %collective-permute-start.2) | collective-permute-done | bytes 139296 | tf_op jit(solution)/shard_map/ppermute | solution.py:733
  21.4 0.1 select_select_fusion.1
  21.5 3.5 %collective-permute-start.3 = (f32[272,128]{1,0:T(8,128)S(1)}, f32[272,128]{1,0:T(8,128)S(1)}, u32[]{:S(2)}, u32[]{:S(2)}) collective-permute-start(f32[272,128]{1,0:T(8,128)S(1)} %select_select_fusion.1), channel_id=1, source_target_pairs={{0,2},{1,3},{2,0},{3,1},{4,6},{5,7},{6,4},{7,5},{8,10},{9,11},{10,... | collective-permute-start | bytes 417800 | tf_op jit(solution)/shard_map/ppermute | solution.py:733
  25.0 3.0 %collective-permute-done.3 = f32[272,128]{1,0:T(8,128)S(1)} collective-permute-done((f32[272,128]{1,0:T(8,128)S(1)}, f32[272,128]{1,0:T(8,128)S(1)}, u32[]{:S(2)}, u32[]{:S(2)}) %collective-permute-start.3) | collective-permute-done | bytes 139296 | tf_op jit(solution)/shard_map/ppermute | solution.py:733
  28.1 0.1 select_select_fusion.refs_0_
  28.2 4.3 %collective-permute-start.4 = (f32[272,128]{1,0:T(8,128)S(1)}, f32[272,128]{1,0:T(8,128)S(1)}, u32[]{:S(2)}, u32[]{:S(2)}) collective-permute-start(f32[272,128]{1,0:T(8,128)S(1)} %select_select_fusion.refs_0_), channel_id=1, source_target_pairs={{0,4},{1,5},{2,6},{3,7},{4,0},{5,1},{6,2},{7,3},{8,12},{9,13},{10,... | collective-permute-start | bytes 417800 | tf_op jit(solution)/shard_map/ppermute | solution.py:733
  32.5 4.5 %collective-permute-done.4.refs_1_ = f32[272,128]{1,0:T(8,128)S(1)} collective-permute-done((f32[272,128]{1,0:T(8,128)S(1)}, f32[272,128]{1,0:T(8,128)S(1)}, u32[]{:S(2)}, u32[]{:S(2)}) %collective-permute-start.4) | collective-permute-done | bytes 139296 | tf_op jit(solution)/shard_map/ppermute | solution.py:733
  37.0 0.1 combine.1
  37.1 0.1 collective-permute-start.5
  37.2 1.2 %collective-permute-done.5 = f32[88,128]{1,0:T(8,128)S(1)} collective-permute-done((f32[88,128]{1,0:T(8,128)S(1)}, f32[88,128]{1,0:T(8,128)S(1)}, u32[]{:S(2)}, u32[]{:S(2)}) %collective-permute-start.5) | collective-permute-done | bytes 45088 | tf_op jit(solution)/shard_map/ppermute | solution.py:763
  38.4 1.5 %collective-permute-start.6 = (f32[88,128]{1,0:T(8,128)S(1)}, f32[88,128]{1,0:T(8,128)S(1)}, u32[]{:S(2)}, u32[]{:S(2)}) collective-permute-start(f32[88,128]{1,0:T(8,128)S(1)} %add.17.refs_0_), channel_id=1, source_target_pairs={{0,16},{8,24},{16,0},{24,8},{1,17},{9,25},{17,1},{25,9},{2,18},{10... | collective-permute-start | bytes 135176 | tf_op jit(solution)/shard_map/ppermute | solution.py:763
  40.0 0.8 %latent.1 = f32[1,64,512]{2,1,0:T(8,128)} custom-call(f32[192,512]{1,0:T(8,128)S(1)} %get-tuple-element.67.grads_ref, f32[16,128]{1,0:T(8,128)S(1)} %get-tuple-element.69.aux_ref), custom_call_target="tpu_custom_call" | custom-call | tf_op jit(solution)/shard_map/latent/pallas_call | solution.py:635
  40.8 1.7 %collective-permute-done.6.refs_1_ = f32[88,128]{1,0:T(8,128)S(1)} collective-permute-done((f32[88,128]{1,0:T(8,128)S(1)}, f32[88,128]{1,0:T(8,128)S(1)}, u32[]{:S(2)}, u32[]{:S(2)}) %collective-permute-start.6) | collective-permute-done | bytes 45088 | tf_op jit(solution)/shard_map/ppermute | solution.py:763
  42.5 0.9 %final.1 = (f32[4,32,64]{2,1,0:T(8,128)}, f32[3,16,32]{2,1,0:T(8,128)}, f32[16,32]{1,0:T(8,128)}, f32[7,32]{1,0:T(8,128)}) custom-call(f32[88,128]{1,0:T(8,128)S(1)} %add.17.refs_0_, f32[88,128]{1,0:T(8,128)S(1)} %collective-permute-done.6.refs_1_), custom_call_target="tpu_custom_call" | custom-call | tf_op jit(solution)/shard_map/final/pallas_call | solution.py:635
  (10 shorter events, 0.0 us)
Async XLA Ops:
  0.6 6.2 %copy-start = (f32[4,32,64]{2,1,0:T(8,128)S(1)}, f32[4,32,64]{2,1,0:T(8,128)}, u32[]{:S(2)}) copy-start(f32[4,32,64]{2,1,0:T(8,128)} %refs_0_.3) | copy-start | bytes 98308
  0.6 6.2 %copy-start.1 = (f32[3,16,32]{2,1,0:T(8,128)S(1)}, f32[3,16,32]{2,1,0:T(8,128)}, u32[]{:S(2)}) copy-start(f32[3,16,32]{2,1,0:T(8,128)} %refs_1_.3) | copy-start | bytes 18436
  0.7 6.2 %copy-start.2 = (f32[32,16]{0,1:T(8,128)S(1)}, f32[32,16]{0,1:T(8,128)}, u32[]{:S(2)}) copy-start(f32[32,16]{0,1:T(8,128)} %param.16) | copy-start | bytes 6148
  0.7 6.2 %copy-start.3 = (f32[7,32]{1,0:T(8,128)S(1)}, f32[7,32]{1,0:T(8,128)}, u32[]{:S(2)}) copy-start(f32[7,32]{1,0:T(8,128)} %refs_3_.3) | copy-start | bytes 2692
  3.1 4.8 %collective-permute-start = (f32[24,128]{1,0:T(8,128)S(1)}, f32[24,128]{1,0:T(8,128)S(1)}, u32[]{:S(2)}, u32[]{:S(2)}) collective-permute-start(f32[24,128]{1,0:T(8,128)S(1)} %get-tuple-element.40.refs_4_.refs_0_), channel_id=1, source_target_pairs={{0,1},{1,0},{2,3},{3,2},{4,5},{5,4},{6,7},{7,6},{8,9},{9,8},{10,11... | collective-permute-start | bytes 36872 | tf_op jit(solution)/shard_map/ppermute | solution.py:706
  6.2 1.8 %collective-permute-start.1 = (f32[24,128]{1,0:T(8,128)S(1)}, f32[24,128]{1,0:T(8,128)S(1)}, u32[]{:S(2)}, u32[]{:S(2)}) collective-permute-start(f32[24,128]{1,0:T(8,128)S(1)} %get-tuple-element.40.refs_4_.refs_0_), channel_id=1, source_target_pairs={{1,2},{2,1},{3,4},{4,3},{5,6},{6,5},{9,10},{10,9},{11,12},{12,11},... | collective-permute-start | bytes 36872 | tf_op jit(solution)/shard_map/ppermute | solution.py:708
  13.5 7.9 %collective-permute-start.2 = (f32[272,128]{1,0:T(8,128)S(1)}, f32[272,128]{1,0:T(8,128)S(1)}, u32[]{:S(2)}, u32[]{:S(2)}) collective-permute-start(f32[272,128]{1,0:T(8,128)S(1)} %get-tuple-element.68), channel_id=1, source_target_pairs={{0,1},{1,0},{2,3},{3,2},{4,5},{5,4},{6,7},{7,6},{8,9},{9,8},{10,11... | collective-permute-start | bytes 417800 | tf_op jit(solution)/shard_map/ppermute | solution.py:733
  21.5 6.6 %collective-permute-start.3 = (f32[272,128]{1,0:T(8,128)S(1)}, f32[272,128]{1,0:T(8,128)S(1)}, u32[]{:S(2)}, u32[]{:S(2)}) collective-permute-start(f32[272,128]{1,0:T(8,128)S(1)} %select_select_fusion.1), channel_id=1, source_target_pairs={{0,2},{1,3},{2,0},{3,1},{4,6},{5,7},{6,4},{7,5},{8,10},{9,11},{10,... | collective-permute-start | bytes 417800 | tf_op jit(solution)/shard_map/ppermute | solution.py:733
  28.2 8.9 %collective-permute-start.4 = (f32[272,128]{1,0:T(8,128)S(1)}, f32[272,128]{1,0:T(8,128)S(1)}, u32[]{:S(2)}, u32[]{:S(2)}) collective-permute-start(f32[272,128]{1,0:T(8,128)S(1)} %select_select_fusion.refs_0_), channel_id=1, source_target_pairs={{0,4},{1,5},{2,6},{3,7},{4,0},{5,1},{6,2},{7,3},{8,12},{9,13},{10,... | collective-permute-start | bytes 417800 | tf_op jit(solution)/shard_map/ppermute | solution.py:733
  37.1 1.3 %collective-permute-start.5 = (f32[88,128]{1,0:T(8,128)S(1)}, f32[88,128]{1,0:T(8,128)S(1)}, u32[]{:S(2)}, u32[]{:S(2)}) collective-permute-start(f32[88,128]{1,0:T(8,128)S(1)} %get-tuple-element.70), channel_id=1, source_target_pairs={{0,8},{8,0},{16,24},{24,16},{1,9},{9,1},{17,25},{25,17},{2,10},{10... | collective-permute-start | bytes 135176 | tf_op jit(solution)/shard_map/ppermute | solution.py:763
  38.4 4.1 %collective-permute-start.6 = (f32[88,128]{1,0:T(8,128)S(1)}, f32[88,128]{1,0:T(8,128)S(1)}, u32[]{:S(2)}, u32[]{:S(2)}) collective-permute-start(f32[88,128]{1,0:T(8,128)S(1)} %add.17.refs_0_), channel_id=1, source_target_pairs={{0,16},{8,24},{16,0},{24,8},{1,17},{9,25},{17,1},{25,9},{2,18},{10... | collective-permute-start | bytes 135176 | tf_op jit(solution)/shard_map/ppermute | solution.py:763

commit v4 on v3

--- a/solution.py
+++ b/solution.py
@@ -37,36 +37,20 @@
 
 def tables():
     order = np.concatenate([np.arange(0, BLOCK, 2), np.arange(1, BLOCK, 2)])
-    p = np.arange(LANES)
-    cos, sin = [], []
-    for rho in range(4):
-        angle = 2.0 * np.pi / WIN_COARSE * ((order[:, None] * (4 * p + rho)[None, :]) % WIN_COARSE)
-        cos.append(np.cos(angle))
-        sin.append(np.sin(angle))
-    even = np.concatenate(
-        [np.concatenate([cos[0], -sin[0]], 1), np.concatenate([cos[2], -sin[2]], 1)], 0
-    )
-    odd = np.concatenate([cos[1], -sin[1], cos[3], -sin[3]], 1)
-    angle = 2.0 * np.pi / WIN_FINE * ((order[:, None] * p[None, :]) % WIN_FINE)
-    taper = 0.5 - 0.5 * np.cos(2.0 * np.pi / WIN_FINE * order)[:, None]
-    fine = np.concatenate([taper * np.cos(angle), -taper * np.sin(angle)], 1)
+    angle = 2.0 * np.pi / BLOCK * ((order[:, None] * np.arange(LANES)[None, :]) % BLOCK)
+    turns = np.concatenate([np.cos(angle), -np.sin(angle)], 1)
     coarse_mel = mel_table(WIN_COARSE)
-    coarse_mel = np.concatenate([coarse_mel[rho::4] for rho in (0, 2, 1, 3)], 0)
+    coarse_mel = np.concatenate([coarse_mel[rho::4] for rho in range(4)], 0)
     fine_mel = mel_table(WIN_FINE)
     hann = 0.5 - 0.5 * np.cos(2.0 * np.pi / WIN_COARSE * np.arange(WIN_COARSE))
-    hann = hann.reshape(4, BLOCK)[:, order].astype(np.float32)
-    hann = np.concatenate([hann, np.zeros_like(hann)], 0)
+    twist = 2.0 * np.pi / WIN_COARSE * np.arange(1, 4)[:, None] * order[None, :]
+    taper = 0.5 - 0.5 * np.cos(2.0 * np.pi / WIN_FINE * order)[None, :]
+    lines = [hann.reshape(4, BLOCK)[:, order], np.cos(twist), np.sin(twist), taper]
+    lines = np.concatenate(lines + [np.zeros((5, BLOCK))], 0).astype(np.float32)
     deal = np.zeros((BLOCK, BLOCK), np.float32)
     deal[order, np.arange(BLOCK)] = 1.0
     banks = [np.concatenate(hi_lo(x), 1) for x in (coarse_mel, fine_mel)]
-    return (
-        deal.astype(BF16),
-        np.concatenate(hi_lo(even), 0),
-        np.concatenate(hi_lo(odd), 0),
-        hann,
-        np.concatenate(hi_lo(fine), 0),
-        np.concatenate(banks, 0),
-    )
+    return deal.astype(BF16), lines, np.concatenate(hi_lo(turns), 0), np.concatenate(banks, 0)
 
 
 def split(x):
@@ -224,14 +208,13 @@
 
 
 def own_kernel(sizes, *refs):
-    sources = refs[:9]
-    packet_ref, latent_ref = refs[9:11]
-    weight_refs = refs[11:15]
-    kept = dict(zip(KEPT, refs[15:27]))
-    table_refs = refs[27:29]
-    up_ref, inner_ref, outer_ref, out_ref, target_ref, deal_ref, square, rows_ref, sems = refs[29:]
+    sources = refs[:7]
+    packet_ref, latent_ref = refs[7:9]
+    weight_refs = refs[9:13]
+    kept = dict(zip(KEPT, refs[13:25]))
+    up_ref, inner_ref, outer_ref, out_ref, target_ref, deal_ref, square, rows_ref, sems = refs[25:]
     channels, half, hidden, frames = sizes
-    spaces = (latent_ref, target_ref, up_ref, inner_ref, outer_ref, out_ref, deal_ref, *table_refs)
+    spaces = (latent_ref, target_ref, up_ref, inner_ref, outer_ref, out_ref, deal_ref)
     copies = []
     for i, (source, space) in enumerate(zip(sources, spaces)):
         if i == 0:
@@ -239,7 +222,7 @@
         copies.append(pltpu.make_async_copy(source, space, sems.at[i]))
     for copy in copies:
         copy.start()
-    for copy in copies[:7]:
+    for copy in copies:
         copy.wait()
     weights = forward_weights(sizes, up_ref, inner_ref, outer_ref, out_ref, square)
     for name, ref in zip(FORWARD, weight_refs):
@@ -275,8 +258,6 @@
             ]
         at = 8 + (2 + r) * blocks
         packet_ref[at : at + blocks, :] = dealt[0:blocks, r * LANES : (r + 1) * LANES]
-    for copy in copies[7:]:
-        copy.wait()
 
 
 def main_kernel(sizes, *refs):
@@ -284,9 +265,9 @@
     weights = {name: ref[...] for name, ref in zip(FORWARD, refs[4:8])}
     kept = dict(zip(KEPT, refs[8:20]))
     up_back, back_inner, outer_back, out_back = (ref[...] for ref in refs[20:24])
-    even_ref, odd_ref, hann_ref, fine_ref, bank_ref = refs[24:29]
-    payload_ref, grads_ref = refs[29:31]
-    (square, wblock, shifted, wave_b, targ_b, lanes_b) = refs[31:37]
+    lines_ref, turns_ref, bank_ref = refs[24:27]
+    keep_ref, send_ref, grads_ref = refs[27:30]
+    (square, wblock, shifted, wave_b, targ_b, lanes_b) = refs[30:36]
     channels, half, hidden, frames = sizes
     window = frames + LANES
     own_blocks = frames // LANES
@@ -351,11 +332,10 @@
                 lane >= LANES - 4, piece, wave_b[row - 1 : row, columns]
             )
             wave_b[row : row + 1, columns] = jnp.where(lane < 4, piece, wave_b[row : row + 1, columns])
-    size = 2 * BLOCK
-    even_h, even_l = even_ref.at[pl.ds(0, size)], even_ref.at[pl.ds(size, size)]
-    odd_h, odd_l = odd_ref[0:BLOCK], odd_ref[BLOCK:]
-    fine_h, fine_l = fine_ref.at[pl.ds(0, BLOCK)], fine_ref.at[pl.ds(BLOCK, BLOCK)]
-    coarse_bank, fine_bank = bank_ref[0:size], bank_ref[size:]
+    turns_h, turns_l = turns_ref[0:BLOCK], turns_ref[BLOCK:]
+    coarse_bank, fine_bank = bank_ref[0 : 2 * BLOCK], bank_ref[2 * BLOCK :]
+    line = [lines_ref[i : i + 1, :] for i in range(11)]
+    hann, cos, sin, taper = line[0:4], line[4:7], line[7:10], line[10]
 
     row_count = own_blocks + 4
     start = own_blocks - 3
@@ -364,63 +344,94 @@
         rows = jnp.concatenate(
             [wave_b[pl.ds(start + j, row_count), :], targ_b[pl.ds(start + j, row_count), :]], 0
         )
-        parts.append(rows * hann_ref[j : j + 1, :])
+        parts.append(rows * hann[j])
     even_sum, odd_sum = parts[0] + parts[2], parts[1] + parts[3]
-    turned = jnp.concatenate([parts[0] - parts[2], parts[1] - parts[3]], axis=0)
-    spec0 = dot3(even_sum + odd_sum, even_h[0:BLOCK], even_l[0:BLOCK])
-    spec2 = dot3(even_sum - odd_sum, even_h[BLOCK:], even_l[BLOCK:])
-    spec1 = dot3(turned, odd_h, odd_l)
+    pair0, pair1 = even_sum + odd_sum, even_sum - odd_sum
+    part0, part1 = parts[0] - parts[2], parts[1] - parts[3]
+    blocks_in = [
+        pair0,
+        part0 * cos[0] - part1 * sin[0],
+        -part1 * cos[0] - part0 * sin[0],
+        pair1 * cos[1],
+        -pair1 * sin[1],
+        part0 * cos[2] + part1 * sin[2],
+        part1 * cos[2] - part0 * sin[2],
+    ]
+
+    hop = LANES // 4
+    lane = lax.broadcasted_iota(jnp.int32, (1, LANES), 1)
+    start_fine = own_blocks - 1
+    for which, source in enumerate((wave_b, targ_b)):
+        for s in range(4):
+            base = (which * 4 + s) * row_count
+            for r in range(2):
+                here = source[pl.ds(start_fine, row_count), r * LANES : (r + 1) * LANES]
+                if s:
+                    there = source[pl.ds(start_fine + 1, row_count), r * LANES : (r + 1) * LANES]
+                    here = jnp.where(
+                        lane < LANES - s * hop,
+                        pltpu.roll(here, LANES - s * hop, 1),
+                        pltpu.roll(there, LANES - s * hop, 1),
+                    )
+                shifted[base : base + row_count, r * LANES : (r + 1) * LANES] = here
+    spec = dot3(jnp.concatenate([*blocks_in, shifted[...] * taper], axis=0), turns_h, turns_l)
     rows = 2 * row_count
-    quarter = [(spec1[:rows, at : at + LANES], spec1[rows:, at : at + LANES]) for at in range(0, size, LANES)]
-    real = jnp.concatenate(
-        [
-            spec0[:, :LANES],
-            spec2[:, :LANES],
-            quarter[0][0] + quarter[1][1],
-            quarter[2][0] - quarter[3][1],
-        ],
-        1,
-    )
-    imag = jnp.concatenate(
-        [
-            spec0[:, LANES:],
-            spec2[:, LANES:],
-            quarter[1][0] - quarter[0][1],
-            quarter[3][0] + quarter[2][1],
-        ],
-        1,
-    )
+    bins = [spec[i * rows : (i + 1) * rows] for i in range(7)]
+    real, imag = [bins[0][:, :LANES]], [bins[0][:, LANES:]]
+    for first_bin, second_bin in (bins[1:3], bins[3:5], bins[5:7]):
+        real.append(first_bin[:, :LANES] - second_bin[:, LANES:])
+        imag.append(first_bin[:, LANES:] + second_bin[:, :LANES])
+    real, imag = jnp.concatenate(real, axis=1), jnp.concatenate(imag, axis=1)
+    spec_fine = spec[7 * rows :]
+    real_fine, imag_fine = spec_fine[:, :LANES], spec_fine[:, LANES:]
+    mel_fine = to_mel(real_fine * real_fine + imag_fine * imag_fine, fine_bank)
+    level_fine = jnp.sqrt(mel_fine + 1.0)
+    fine_rows = 4 * row_count
+    level_wave_fine = level_fine[:fine_rows]
+    row_fine = lax.broadcasted_iota(jnp.int32, (fine_rows, MELS), 0)
+    frame_fine = (lax.rem(row_fine, row_count) - 1 + index * own_blocks) * 4 + row_fine // row_count
+    slope_fine = jnp.where(frame_fine >= 0, (level_wave_fine - level_fine[fine_rows:]) / level_wave_fine, 0.0)
     mel = to_mel(real * real + imag * imag, coarse_bank)
     level = jnp.sqrt(mel + 1.0)
     level_wave = level[:row_count]
     frame = lax.broadcasted_iota(jnp.int32, (row_count, MELS), 0) + index * own_blocks - 3
     slope = jnp.where(frame >= 0, (level_wave - level[row_count:]) / level_wave, 0.0)
+    push_fine = 2.0 * from_mel(slope_fine, fine_bank)
     push = 2.0 * from_mel(slope, coarse_bank)
     real, imag = real[:row_count] * push, imag[:row_count] * push
-    back0 = dot3(
-        jnp.concatenate([real[:, :LANES], imag[:, :LANES]], 1), even_h[0:BLOCK], even_l[0:BLOCK], True
-    )
-    back2 = dot3(
-        jnp.concatenate([real[:, LANES:BLOCK], imag[:, LANES:BLOCK]], 1),
-        even_h[BLOCK:],
-        even_l[BLOCK:],
-        True,
-    )
-    real1, real3 = real[:, BLOCK : BLOCK + LANES], real[:, BLOCK + LANES :]
-    imag1, imag3 = imag[:, BLOCK : BLOCK + LANES], imag[:, BLOCK + LANES :]
-    back1 = dot3(
-        jnp.concatenate(
-            [
-                jnp.concatenate([real1, imag1, real3, imag3], 1),
-                jnp.concatenate([-imag1, real1, imag3, -real3], 1),
-            ],
-            0,
-        ),
-        odd_h,
-        odd_l,
-        True,
-    )
-    back1 = [back1[:row_count], back1[row_count:]]
+    wide = []
+    for rho in range(4):
+        columns = slice(rho * LANES, (rho + 1) * LANES)
+        first_bin, second_bin = real[:, columns], imag[:, columns]
+        wide.append(jnp.concatenate([first_bin, second_bin], axis=1))
+        if rho:
+            wide.append(jnp.concatenate([second_bin, -first_bin], axis=1))
+    wide.append(
+        jnp.concatenate([real_fine[:fine_rows] * push_fine, imag_fine[:fine_rows] * push_fine], 1)
+    )
+    back = dot3(jnp.concatenate(wide, axis=0), turns_h, turns_l, True)
+    back_fine = back[7 * row_count :] * taper
+    back = [back[i * row_count : (i + 1) * row_count] for i in range(7)]
+    back0, back2 = back[0], back[3] * cos[1] - back[4] * sin[1]
+    back1 = [
+        back[1] * cos[0] - back[2] * sin[0] + back[5] * cos[2] - back[6] * sin[2],
+        back[5] * sin[2] + back[6] * cos[2] - back[1] * sin[0] - back[2] * cos[0],
+    ]
+    fine = []
+    for r in range(2):
+        total = jnp.zeros((own_blocks, LANES), F32)
+        for s in range(4):
+            piece = back_fine[s * row_count : (s + 1) * row_count, r * LANES : (r + 1) * LANES]
+            if s:
+                piece = pltpu.roll(piece, s * hop, 1)
+                total = total + jnp.where(
+                    lane >= s * hop, piece[1 : 1 + own_blocks], piece[0:own_blocks]
+                )
+            else:
+                total = total + piece[1 : 1 + own_blocks]
+        fine.append(total)
+    fine = jnp.concatenate(fine, axis=1)
+
     plus, minus = back0 + back2, back0 - back2
     backs = [
         plus + back1[0],
@@ -430,87 +441,47 @@
     ]
     coarse = jnp.zeros((own_blocks, BLOCK), F32)
     for j in range(4):
-        coarse = coarse + (backs[j] * hann_ref[j : j + 1, :])[3 - j : 3 - j + own_blocks]
-
-    hop = LANES // 4
-    lane = lax.broadcasted_iota(jnp.int32, (1, LANES), 1)
-    start = own_blocks - 1
-    for which, source in enumerate((wave_b, targ_b)):
-        for s in range(4):
-            base = (which * 4 + s) * row_count
-            for r in range(2):
-                here = source[pl.ds(start, row_count), r * LANES : (r + 1) * LANES]
-                if s:
-                    there = source[pl.ds(start + 1, row_count), r * LANES : (r + 1) * LANES]
-                    here = jnp.where(
-                        lane < LANES - s * hop,
-                        pltpu.roll(here, LANES - s * hop, 1),
-                        pltpu.roll(there, LANES - s * hop, 1),
-                    )
-                shifted[base : base + row_count, r * LANES : (r + 1) * LANES] = here
-    spec = dot3(shifted[...], fine_h[...], fine_l[...])
-    real, imag = spec[:, :LANES], spec[:, LANES:]
-    mel = to_mel(real * real + imag * imag, fine_bank)
-    level = jnp.sqrt(mel + 1.0)
-    fine_rows = 4 * row_count
-    level_wave = level[:fine_rows]
-    row = lax.broadcasted_iota(jnp.int32, (fine_rows, MELS), 0)
-    frame = (lax.rem(row, row_count) - 1 + index * own_blocks) * 4 + row // row_count
-    slope = jnp.where(frame >= 0, (level_wave - level[fine_rows:]) / level_wave, 0.0)
-    push = 2.0 * from_mel(slope, fine_bank)
-    back = dot3(
-        jnp.concatenate([real[:fine_rows] * push, imag[:fine_rows] * push], 1),
-        fine_h[...],
-        fine_l[...],
-        True,
-    )
-    fine = []
-    for r in range(2):
-        total = jnp.zeros((own_blocks, LANES), F32)
-        for s in range(4):
-            piece = back[s * row_count : (s + 1) * row_count, r * LANES : (r + 1) * LANES]
-            if s:
-                piece = pltpu.roll(piece, s * hop, 1)
-                total = total + jnp.where(
-                    lane >= s * hop, piece[1 : 1 + own_blocks], piece[0:own_blocks]
-                )
-            else:
-                total = total + piece[1 : 1 + own_blocks]
-        fine.append(total)
-    fine = jnp.concatenate(fine, axis=1)
+        coarse = coarse + (backs[j] * hann[j])[3 - j : 3 - j + own_blocks]
 
     own_rows = pl.ds(own_blocks, own_blocks)
     timed = 2.0 * (wave_b[own_rows, :] - targ_b[own_rows, :])
 
-    totals, views, uppers, inners, mixeds, edges = [], [], [], [], [], []
-    for i, stream in enumerate((timed, coarse, fine)):
-        totals.append(jnp.sum(stream * stream))
-        lanes_b[i] = jnp.zeros((8, window), F32)
+    streams = (timed, coarse, fine)
+    totals = [jnp.sum(stream * stream) for stream in streams]
+    lanes_b[...] = jnp.zeros_like(lanes_b)
+    for i, stream in enumerate(streams):
         for b in range(own_blocks):
             for r in range(2):
-                lanes_b[i, r : r + 1, b * LANES : (b + 1) * LANES] = stream[
+                lanes_b[r, i : i + 1, b * LANES : (b + 1) * LANES] = stream[
                     b : b + 1, r * LANES : (r + 1) * LANES
                 ]
-        evens, odds = lanes_b[i, 0:1, :], lanes_b[i, 1:2, :]
-        for k in range(8):
-            source = odds if k % 2 else evens
-            lanes_b[i, k : k + 1, :] = moved(source, MARGIN - (4 - k) // 2)
-        view = lanes_b[i]
-        views.append(view)
+    evens, odds = lanes_b[0], lanes_b[1]
+    shifted_rows = [moved(odds if k % 2 else evens, MARGIN - (4 - k) // 2) for k in range(8)]
+    views = [
+        jnp.concatenate([shifted_rows[k][i : i + 1] for k in range(8)], axis=0) for i in range(STREAMS)
+    ]
+    threes = []
+    for view in views:
         high = view.astype(BF16).astype(F32)
-        three = jnp.concatenate([high, high, view - high], axis=0).astype(BF16)
-        grad_mixed = dot(out_back, three) * slope_m * mask
-        mixed = split(grad_mixed)
-        mixeds.append(mixed)
-        grad_inner = apply(outer_back, mixed) * slope_c
-        inners.append(split(grad_inner))
-        spread = jnp.concatenate(
-            [moved(grad_inner[hidden:], 1), grad_inner, moved(grad_inner[:hidden], -1)], 0
-        )
-        grad_upper = (grad_mixed + apply(back_inner, split(spread)) * slope_u) * mask
-        uppers.append(split(grad_upper))
-        both = jnp.concatenate([grad_upper, moved(grad_upper, -1)], 0)
-        grads = moved(apply(up_back, split(both)) * slope_a * mask, -MARGIN)
+        threes.append(jnp.concatenate([high, high, view - high], axis=0).astype(BF16))
+    slope_m, slope_u = slope_m * mask, slope_u * mask
+    slope_a = slope_a * mask
+    grad_mixed = [dot(out_back, three) * slope_m for three in threes]
+    mixeds = [split(x) for x in grad_mixed]
+    grad_inner = [apply(outer_back, pair) * slope_c for pair in mixeds]
+    inners = [split(x) for x in grad_inner]
+    spreads = [
+        split(jnp.concatenate([moved(x[hidden:], 1), x, moved(x[:hidden], -1)], 0)) for x in grad_inner
+    ]
+    grad_upper = [
+        x + apply(back_inner, pair) * slope_u for x, pair in zip(grad_mixed, spreads)
+    ]
+    uppers = [split(x) for x in grad_upper]
+    nexts = [split(moved(x, -1)) for x in grad_upper]
+    edges = []
+    for i in range(STREAMS):
+        both = tuple(jnp.concatenate([x, y], 0) for x, y in zip(uppers[i], nexts[i]))
+        grads = moved(apply(up_back, both) * slope_a, -MARGIN)
         grads_ref[i * channels : (i + 1) * channels, :] = grads[:, :frames]
         turned = jnp.transpose(grads[:, frames:])
         edges.append(jnp.concatenate([turned[LANES - 8 :], turned[:8]], axis=1))
@@ -528,41 +499,50 @@
             for i in range(STREAMS)
         ]
 
+    def put(value, at, columns):
+        rows = value.shape[0] // 2
+        low, high = value[:rows], value[rows:]
+        keep_ref[at : at + rows, columns] = jnp.where(odd_place, high, low)
+        send_ref[at : at + rows, columns] = jnp.where(odd_place, low, high)
+
+    step = half + hidden // 2
     for i, value in enumerate(summed(uppers, "a")):
-        payload_ref[i * 2 * half : (i + 1) * 2 * half, :] = value
-    base = STREAMS * 2 * half
+        put(value, i * step, slice(0, 2 * channels))
     for i, value in enumerate(summed(inners, "e")):
-        at = base + i * hidden
-        payload_ref[at : at + hidden, 0 : 3 * half] = value[:hidden, : 3 * half] + value[hidden:, half:]
+        put(value[:hidden, : 3 * half] + value[hidden:, half:], i * step + half, slice(0, 3 * half))
     highs = jnp.concatenate([pair[0] for pair in mixeds], axis=0)
     lows = jnp.concatenate([pair[1] for pair in mixeds], axis=0)
     both = jnp.concatenate([saved["h_h"], saved["h_l"]], axis=0)
     first = dot(both, highs, True)
     value = first[: 2 * hidden] + first[2 * hidden :] + dot(saved["h_h"], lows, True)
     for i in range(STREAMS):
-        at = base + i * hidden
         columns = i * 2 * half
-        payload_ref[at : at + hidden, 3 * half : 4 * half] = (
-            value[:hidden, columns : columns + half] + value[hidden:, columns + half : columns + 2 * half]
+        put(
+            value[:hidden, columns : columns + half]
+            + value[hidden:, columns + half : columns + 2 * half],
+            i * step + half,
+            slice(3 * half, 4 * half),
         )
     taps = dot3(jnp.concatenate(views, axis=0), saved["g_h"], saved["g_l"], True)
     for i in range(STREAMS):
         wblock[0:7, i * half : (i + 1) * half] = (
             taps[8 * i + 1 : 8 * i + 8, :half] + taps[8 * i : 8 * i + 7, half:]
         )
-    base = STREAMS * (2 * half + hidden)
     lane = lax.broadcasted_iota(jnp.int32, (1, half), 1)
     sums = jnp.where(lane == 0, totals[0], jnp.where(lane == 1, totals[1], totals[2]))
     wblock[7:8, :] = jnp.zeros((1, 4 * half), F32)
     wblock[0:7, STREAMS * half :] = jnp.zeros((7, half), F32)
     wblock[7:8, STREAMS * half :] = sums
-    payload_ref[base : base + 8, :] = wblock[...]
-    payload_ref[base + 8 :, :] = jnp.concatenate(edges, axis=0)
+    edges = jnp.concatenate(edges, axis=0)
+    for ref in (keep_ref, send_ref):
+        ref[STREAMS * step : STREAMS * step + 8, :] = wblock[...]
+        ref[STREAMS * step + 8 :, :] = edges
 
 
 def combine_kernel(sizes, mine_ref, theirs_ref, weights_ref, aux_ref):
     half, hidden, samples = sizes
-    rows = STREAMS * (2 * half + hidden)
+    step = half + hidden // 2
+    rows = STREAMS * step
     total = mine_ref[0 : rows + 8, :] + theirs_ref[0 : rows + 8, :]
     line = total[rows + 7 : rows + 8, :]
     lane = lax.broadcasted_iota(jnp.int32, line.shape, 1) - STREAMS * half
@@ -571,9 +551,7 @@
     scale = [
         jnp.sum(jnp.where(lane == i, line, 0.0), axis=1, keepdims=True) for i in range(STREAMS)
     ]
-    up = sum(total[i * 2 * half : (i + 1) * 2 * half] * scale[i] for i in range(STREAMS))
-    base = STREAMS * 2 * half
-    inner = sum(total[base + i * hidden : base + (i + 1) * hidden] * scale[i] for i in range(STREAMS))
+    weights_ref[0:step, :] = sum(total[i * step : (i + 1) * step] * scale[i] for i in range(STREAMS))
     last = total[rows : rows + 8]
     out = sum(
         (pltpu.roll(last, (4 - i) * half % (4 * half), 1) if i else last) * scale[i]
@@ -581,9 +559,7 @@
     )
     place = lax.broadcasted_iota(jnp.int32, out.shape, 0)
     lane = lax.broadcasted_iota(jnp.int32, out.shape, 1)
-    weights_ref[0 : 2 * half, :] = up
-    weights_ref[2 * half : 2 * half + hidden, :] = inner
-    weights_ref[2 * half + hidden :, :] = jnp.where((place < 7) & (lane < half), out, 0.0)
+    weights_ref[step:, :] = jnp.where((place < 7) & (lane < half), out, 0.0)
     index = lax.axis_index("tm")
     step = lax.axis_size("tm") // 2
     low = lax.rem(index, step)
@@ -612,18 +588,23 @@
 
 def final_kernel(sizes, mine_ref, theirs_ref, up_ref, inner_ref, outer_ref, out_ref):
     channels, half, hidden, params = sizes
-    total = mine_ref[...] + theirs_ref[...]
-    squares = jnp.sum(total * total)
+    step = half + hidden // 2
+    mine, theirs = mine_ref[...], theirs_ref[...]
+    odd_place = lax.rem(lax.axis_index("tm"), 2) == 1
+    low = jnp.where(odd_place, theirs[:step], mine[:step])
+    high = jnp.where(odd_place, mine[:step], theirs[:step])
+    out = mine[step:]
+    squares = jnp.sum(low * low) + jnp.sum(high * high) + jnp.sum(out * out)
     factor = jnp.minimum(1.0, 1.0 / jnp.sqrt(jnp.full((1, 1), squares / params + 1e-06, F32)))
-    total = total * factor
-    for r in range(2):
-        up_ref[r] = total[r * half : (r + 1) * half, 0:channels]
-        up_ref[r + 2] = total[r * half : (r + 1) * half, channels:]
-    inner = total[2 * half : 2 * half + hidden]
+    low, high = low * factor, high * factor
+    for r, part in enumerate((low, high)):
+        up_ref[r] = part[0:half, 0:channels]
+        up_ref[r + 2] = part[0:half, channels:]
+    inner = jnp.concatenate([low[half:], high[half:]], axis=0)
     for j in range(3):
         inner_ref[j] = inner[:, j * half : (j + 1) * half]
     outer_ref[...] = inner[:, 3 * half :]
-    out_ref[...] = total[2 * half + hidden : 2 * half + hidden + 7, 0:half]
+    out_ref[...] = (out * factor)[0:7, 0:half]
 
 
 def run(kernel, out_shape, operands, scratch, name, mebibytes, left=0):
@@ -664,27 +645,26 @@
         ((2 * half, 6 * hidden), BF16),
         ((8, 6 * half), BF16),
     ]
-    own, own_latent, *made, even, odd = run(
+    own, own_latent, *made = run(
         lambda *refs: own_kernel(sizes, *refs),
         [
             (8 + 4 * blocks, LANES),
             (channels, frames),
             *forward,
             *kept_shapes(channels, half, hidden, window),
-            *[(x.shape, BF16) for x in constants[1:3]],
         ],
-        [latent, target, *weights, *constants[:3]],
+        [latent, target, *weights, constants[0]],
         [
             *[pltpu.VMEM(x.shape, F32) for x in weights],
             pltpu.VMEM(target.shape, F32),
             pltpu.VMEM((BLOCK, BLOCK), BF16),
             pltpu.VMEM((LANES, LANES), F32),
             pltpu.VMEM((8, BLOCK), F32),
-            pltpu.SemaphoreType.DMA((9,)),
+            pltpu.SemaphoreType.DMA((7,)),
         ],
         "own_decode",
         8,
-        9,
+        7,
     )
     backward = run(
         lambda *refs: backward_kernel(sizes, *refs),
@@ -693,10 +673,10 @@
             ((2 * half, 12 * hidden), BF16),
             ((2 * hidden, 6 * half), BF16),
             ((2 * half, 24), BF16),
-            constants[3].shape,
-            *[(x.shape, BF16) for x in constants[4:]],
+            constants[1].shape,
+            *[(x.shape, BF16) for x in constants[2:]],
         ],
-        [*weights, own, *constants[3:]],
+        [*weights, own, *constants[1:]],
         [pltpu.VMEM((LANES, LANES), F32), pltpu.SemaphoreType.DMA((3,))],
         "backward_weights",
         4,
@@ -707,19 +687,20 @@
     pairs = [(i, i + 1 if i % 2 else i - 1) for i in range(count)]
     second = lax.ppermute(own, "tm", [(a, b) for a, b in pairs if 0 <= b < count])
 
-    rows = STREAMS * (2 * half + hidden)
-
-    payload, grads = run(
+    part = half + hidden // 2
+    rows = STREAMS * part
+
+    payload, sent, grads = run(
         lambda *refs: main_kernel(sizes, *refs),
-        [(rows + 8 + 8 * STREAMS, LANES), (STREAMS * channels, frames)],
-        [own, first, second, own_latent, *made, *backward[:4], even, odd, *backward[4:]],
+        [*[(rows + 8 + 8 * STREAMS, LANES)] * 2, (STREAMS * channels, frames)],
+        [own, first, second, own_latent, *made, *backward],
         [
             pltpu.VMEM((LANES, LANES), F32),
             pltpu.VMEM((8, 4 * half), F32),
             pltpu.VMEM((8 * (blocks + 4), BLOCK), F32),
             pltpu.VMEM((3 * blocks, BLOCK), F32),
             pltpu.VMEM((3 * blocks, BLOCK), F32),
-            pltpu.VMEM((STREAMS, 8, window), F32),
+            pltpu.VMEM((2, 8, window), F32),
         ],
         "losses",
         16,
@@ -730,7 +711,7 @@
     lane = lax.broadcasted_iota(jnp.int32, payload.shape, 1)
     step = 1
     while True:
-        theirs = lax.ppermute(payload, "tm", [(i, i ^ step) for i in range(count)])
+        theirs = lax.ppermute(sent, "tm", [(i, i ^ step) for i in range(count)])
         if 2 * step == count:
             break
         low = index % step
@@ -738,11 +719,12 @@
         payload = jnp.where(
             line < rows + 8, payload + theirs, jnp.where(swap, theirs, payload)
         )
+        sent = payload
         step *= 2
 
     weights, aux = run(
         lambda *refs: combine_kernel((half, hidden, samples), *refs),
-        [(2 * half + hidden + 8, LANES), (16, LANES)],
+        [(part + 8, LANES), (16, LANES)],
         [payload, theirs],
         [],
         "combine",
@@ -761,10 +743,12 @@
     step = 1
     while True:
         theirs = lax.ppermute(weights, "dp", [(i, i ^ step) for i in range(count)])
-        if 2 * step == count:
-            break
         weights = weights + theirs
         step *= 2
+        if step == count:
+            break
+    count = lax.axis_size("tm")
+    theirs = lax.ppermute(weights, "tm", [(i, i ^ 1) for i in range(count)])
     up, inner, outer, out = run(
         lambda *refs: final_kernel((channels, half, hidden, params), *refs),
         [up_kernel.shape, inner_kernel.shape, outer_kernel.shape[::-1], out_kernel.shape],

time: 43.6 us -> 41.3 us (0.947)
  Pallas kernels: 10.8 us -> 9.17 us
  waiting for transfers between devices: 13.5 us -> 12.1 us
  local copies, waits for them, and re-layouts: 0.02 us -> 0.67 us
    ppermute x3 -> x4, waiting for transfers between devices: 10.6 us -> 8.57 us  [the longest x3 7.12 us: local(): theirs = lax.ppermute(sent, 'tm', [(i, i ^ step) for i in range(count)])]
    pallas_call x6, Pallas kernels: 10.8 us -> 9.17 us  [run(): pl.pallas_call(kernel, out_shape=tuple((jax.ShapeDtypeStruct(*(x if isins...]
    unnamed x8, local copies, waits for them, and re-layouts: 0.02 us -> 0.67 us
    ppermute x2, waiting for transfers between devices: 2.94 us -> 3.52 us  [local(): theirs = lax.ppermute(weights, 'dp', [(i, i ^ step) for i in range(count)])]
    ppermute x3 -> x4, starting transfers between devices: 12.8 us -> 12.8 us  [the longest x3 11.2 us: local(): theirs = lax.ppermute(sent, 'tm', [(i, i ^ step) for i in range(count)])]
  transfers between devices with their start and end apart: 7 -> 8, of which waited for: 5 -> 6; matrix products, arithmetic and copies ran while one was open for 0% -> 0% of each run, Pallas kernels for 4% -> 5%
where the time goes in v4:
time: 41.3 us; the launch traced here: 41 us
  starting transfers between devices  18.1 us (44%)
  waiting for transfers between devices  12.1 us (29%)
  Pallas kernels  9.17 us (22%)
  between operations  0.79 us (2%)
  local copies, waits for them, and re-layouts  0.67 us (2%)
    ppermute x3, starting transfers between devices, local(): theirs = lax.ppermute(sent, 'tm', [(i, i ^ step) for i in range(count)])  11.2 us
    pallas_call x6, Pallas kernels, run(): pl.pallas_call(kernel, out_shape=tuple((jax.ShapeDtypeStruct(*(x if isins...  9.17 us
    ppermute x3, waiting for transfers between devices, local(): theirs = lax.ppermute(sent, 'tm', [(i, i ^ step) for i in range(count)])  7.12 us
    ppermute x2, waiting for transfers between devices, local(): theirs = lax.ppermute(weights, 'dp', [(i, i ^ step) for i in range(count)])  3.52 us
    ppermute x1, starting transfers between devices, local(): first = lax.ppermute(own, 'tm', pairs)  3.06 us
    ppermute x2, starting transfers between devices, local(): theirs = lax.ppermute(weights, 'dp', [(i, i ^ step) for i in range(count)])  1.56 us
    ppermute x1, starting transfers between devices, local(): theirs = lax.ppermute(weights, 'tm', [(i, i ^ 1) for i in range(count)])  1.54 us
    ppermute x1, waiting for transfers between devices, local(): theirs = lax.ppermute(weights, 'tm', [(i, i ^ 1) for i in range(count)])  1.46 us
  transfers between devices with their start and end apart: 8, of which 6 were waited for; matrix products, arithmetic and copies ran while one was open for 0% of the time, Pallas kernels for 5%

profile of v4, /device:TPU:0, one launch (start us, length us, event | category | flops | bytes accessed | tf_op | source)
XLA Modules:
  0.0 41.0 jit_solution(9499134391545399907)
XLA Ops:
  0.7 2.4 %own_decode.1 = (f32[24,128]{1,0:T(8,128)S(1)}, f32[64,512]{1,0:T(8,128)S(1)}, bf16[64,384]{1,0:T(8,128)(2,1)S(1)}, bf16[32,384]{1,0:T(8,128)(2,1)S(1)}, bf16[64...) custom-call(f32[1,64,512]{2,1,0:T(8,128)} %refs_0_.2, ...), custom_call_target="tpu_custom_call" | custom-call | tf_op jit(solution)/shard_map/own_decode/pallas_call | solution.py:616
  3.1 0.0 copy-start.1
  3.1 3.1 %collective-permute-start = (f32[24,128]{1,0:T(8,128)S(1)}, f32[24,128]{1,0:T(8,128)S(1)}, u32[]{:S(2)}, u32[]{:S(2)}) collective-permute-start(f32[24,128]{1,0:T(8,128)S(1)} %get-tuple-element.39.refs_4_.refs_0_), channel_id=1, source_target_pairs={{0,1},{1,0},{2,3},{3,2},{4,5},{5,4},{6,7},{7,6},{8,9},{9,8},{10,11... | collective-permute-start | bytes 36872 | tf_op jit(solution)/shard_map/ppermute | solution.py:686
  6.2 0.7 %collective-permute-start.1 = (f32[24,128]{1,0:T(8,128)S(1)}, f32[24,128]{1,0:T(8,128)S(1)}, u32[]{:S(2)}, u32[]{:S(2)}) collective-permute-start(f32[24,128]{1,0:T(8,128)S(1)} %get-tuple-element.39.refs_4_.refs_0_), channel_id=1, source_target_pairs={{1,2},{2,1},{3,4},{4,3},{5,6},{6,5},{9,10},{10,9},{11,12},{12,11},... | collective-permute-start | bytes 36872 | tf_op jit(solution)/shard_map/ppermute | solution.py:688
  6.9 0.6 %copy-done.2 = f32[32,16]{0,1:T(8,128)S(1)} copy-done((f32[32,16]{0,1:T(8,128)S(1)}, f32[32,16]{0,1:T(8,128)}, u32[]{:S(2)}) %copy-start.2) | copy-done | bytes 2072
  7.5 1.0 %backward_weights.1 = (bf16[64,384]{1,0:T(8,128)(2,1)S(1)}, bf16[64,192]{1,0:T(8,128)(2,1)S(1)}, bf16[32,192]{1,0:T(8,128)(2,1)S(1)}, bf16[64,24]{1,0:T(8,128)(2...) custom-call(f32[4,32,64]{2,1,0:T(8,128)S(1)} %copy-done, ...), custom_call_target="tpu_custom_call" | custom-call | tf_op jit(solution)/shard_map/backward_weights/pallas_call | solution.py:616
  8.6 3.9 %losses.1 = (f32[152,128]{1,0:T(8,128)S(1)}, f32[152,128]{1,0:T(8,128)S(1)}, f32[192,512]{1,0:T(8,128)S(1)}) custom-call(f32[24,128]{1,0:T(8,128)S(1)} %get-tuple-element.39.refs_4_.refs_0_, f32[24,128]{1,0:T(8,128)S(1)} %collective-permute-done.refs_1_, f32[24,128]{1,0:T(8,128)S(1)} %collective-permute-done.1.refs_2_, ...), custom_call_target="tpu_custom_call" | custom-call | tf_op jit(solution)/shard_map/losses/pallas_call | solution.py:616
  12.5 4.3 %collective-permute-start.2 = (f32[152,128]{1,0:T(8,128)S(1)}, f32[152,128]{1,0:T(8,128)S(1)}, u32[]{:S(2)}, u32[]{:S(2)}) collective-permute-start(f32[152,128]{1,0:T(8,128)S(1)} %get-tuple-element.66), channel_id=1, source_target_pairs={{0,1},{1,0},{2,3},{3,2},{4,5},{5,4},{6,7},{7,6},{8,9},{9,8},{10,11... | collective-permute-start | bytes 233480 | tf_op jit(solution)/shard_map/ppermute | solution.py:714
  16.9 2.4 %collective-permute-done.2 = f32[152,128]{1,0:T(8,128)S(1)} collective-permute-done((f32[152,128]{1,0:T(8,128)S(1)}, f32[152,128]{1,0:T(8,128)S(1)}, u32[]{:S(2)}, u32[]{:S(2)}) %collective-permute-start.2) | collective-permute-done | bytes 77856 | tf_op jit(solution)/shard_map/ppermute | solution.py:714
  19.2 0.1 select_select_fusion.1
  19.3 3.4 %collective-permute-start.3 = (f32[152,128]{1,0:T(8,128)S(1)}, f32[152,128]{1,0:T(8,128)S(1)}, u32[]{:S(2)}, u32[]{:S(2)}) collective-permute-start(f32[152,128]{1,0:T(8,128)S(1)} %select_select_fusion.1), channel_id=1, source_target_pairs={{0,2},{1,3},{2,0},{3,1},{4,6},{5,7},{6,4},{7,5},{8,10},{9,11},{10,... | collective-permute-start | bytes 233480 | tf_op jit(solution)/shard_map/ppermute | solution.py:714
  22.7 2.4 %collective-permute-done.3 = f32[152,128]{1,0:T(8,128)S(1)} collective-permute-done((f32[152,128]{1,0:T(8,128)S(1)}, f32[152,128]{1,0:T(8,128)S(1)}, u32[]{:S(2)}, u32[]{:S(2)}) %collective-permute-start.3) | collective-permute-done | bytes 77856 | tf_op jit(solution)/shard_map/ppermute | solution.py:714
  25.1 0.1 select_select_fusion.refs_0_
  25.2 3.5 %collective-permute-start.4 = (f32[152,128]{1,0:T(8,128)S(1)}, f32[152,128]{1,0:T(8,128)S(1)}, u32[]{:S(2)}, u32[]{:S(2)}) collective-permute-start(f32[152,128]{1,0:T(8,128)S(1)} %select_select_fusion.refs_0_), channel_id=1, source_target_pairs={{0,4},{1,5},{2,6},{3,7},{4,0},{5,1},{6,2},{7,3},{8,12},{9,13},{10,... | collective-permute-start | bytes 233480 | tf_op jit(solution)/shard_map/ppermute | solution.py:714
  28.7 2.4 %collective-permute-done.4.refs_1_ = f32[152,128]{1,0:T(8,128)S(1)} collective-permute-done((f32[152,128]{1,0:T(8,128)S(1)}, f32[152,128]{1,0:T(8,128)S(1)}, u32[]{:S(2)}, u32[]{:S(2)}) %collective-permute-start.4) | collective-permute-done | bytes 77856 | tf_op jit(solution)/shard_map/ppermute | solution.py:714
  31.1 0.1 combine.1
  31.2 0.1 collective-permute-start.5
  31.3 1.2 %collective-permute-done.5 = f32[48,128]{1,0:T(8,128)S(1)} collective-permute-done((f32[48,128]{1,0:T(8,128)S(1)}, f32[48,128]{1,0:T(8,128)S(1)}, u32[]{:S(2)}, u32[]{:S(2)}) %collective-permute-start.5) | collective-permute-done | bytes 24608 | tf_op jit(solution)/shard_map/ppermute | solution.py:745
  32.5 1.5 %collective-permute-start.6 = (f32[48,128]{1,0:T(8,128)S(1)}, f32[48,128]{1,0:T(8,128)S(1)}, u32[]{:S(2)}, u32[]{:S(2)}) collective-permute-start(f32[48,128]{1,0:T(8,128)S(1)} %add.20), channel_id=1, source_target_pairs={{0,16},{8,24},{16,0},{24,8},{1,17},{9,25},{17,1},{25,9},{2,18},{10... | collective-permute-start | bytes 73736 | tf_op jit(solution)/shard_map/ppermute | solution.py:745
  33.9 2.3 %collective-permute-done.6 = f32[48,128]{1,0:T(8,128)S(1)} collective-permute-done((f32[48,128]{1,0:T(8,128)S(1)}, f32[48,128]{1,0:T(8,128)S(1)}, u32[]{:S(2)}, u32[]{:S(2)}) %collective-permute-start.6) | collective-permute-done | bytes 24608 | tf_op jit(solution)/shard_map/ppermute | solution.py:745
  36.3 1.5 %collective-permute-start.7 = (f32[48,128]{1,0:T(8,128)S(1)}, f32[48,128]{1,0:T(8,128)S(1)}, u32[]{:S(2)}, u32[]{:S(2)}) collective-permute-start(f32[48,128]{1,0:T(8,128)S(1)} %add.21.refs_0_), channel_id=1, source_target_pairs={{0,1},{1,0},{2,3},{3,2},{4,5},{5,4},{6,7},{7,6},{8,9},{9,8},{10,11... | collective-permute-start | bytes 73736 | tf_op jit(solution)/shard_map/ppermute | solution.py:751
  37.8 0.8 %latent.1 = f32[1,64,512]{2,1,0:T(8,128)} custom-call(f32[192,512]{1,0:T(8,128)S(1)} %get-tuple-element.64.grads_ref, f32[16,128]{1,0:T(8,128)S(1)} %get-tuple-element.67.aux_ref), custom_call_target="tpu_custom_call" | custom-call | tf_op jit(solution)/shard_map/latent/pallas_call | solution.py:616
  38.7 1.5 %collective-permute-done.7.refs_1_ = f32[48,128]{1,0:T(8,128)S(1)} collective-permute-done((f32[48,128]{1,0:T(8,128)S(1)}, f32[48,128]{1,0:T(8,128)S(1)}, u32[]{:S(2)}, u32[]{:S(2)}) %collective-permute-start.7) | collective-permute-done | bytes 24608 | tf_op jit(solution)/shard_map/ppermute | solution.py:751
  40.1 0.9 %final.1 = (f32[4,32,64]{2,1,0:T(8,128)}, f32[3,16,32]{2,1,0:T(8,128)}, f32[16,32]{1,0:T(8,128)}, f32[7,32]{1,0:T(8,128)}) custom-call(f32[48,128]{1,0:T(8,128)S(1)} %add.21.refs_0_, f32[48,128]{1,0:T(8,128)S(1)} %collective-permute-done.7.refs_1_), custom_call_target="tpu_custom_call" | custom-call | tf_op jit(solution)/shard_map/final/pallas_call | solution.py:616
  (13 shorter events, 0.0 us)
Async XLA Ops:
  0.6 6.2 %copy-start = (f32[4,32,64]{2,1,0:T(8,128)S(1)}, f32[4,32,64]{2,1,0:T(8,128)}, u32[]{:S(2)}) copy-start(f32[4,32,64]{2,1,0:T(8,128)} %refs_0_.3) | copy-start | bytes 98308
  0.6 6.2 %copy-start.3 = (f32[7,32]{1,0:T(8,128)S(1)}, f32[7,32]{1,0:T(8,128)}, u32[]{:S(2)}) copy-start(f32[7,32]{1,0:T(8,128)} %refs_3_.3) | copy-start | bytes 2692
  3.1 3.8 %copy-start.1 = (f32[3,16,32]{2,1,0:T(8,128)S(1)}, f32[3,16,32]{2,1,0:T(8,128)}, u32[]{:S(2)}) copy-start(f32[3,16,32]{2,1,0:T(8,128)} %refs_1_.3) | copy-start | bytes 18436
  3.1 5.5 %collective-permute-start = (f32[24,128]{1,0:T(8,128)S(1)}, f32[24,128]{1,0:T(8,128)S(1)}, u32[]{:S(2)}, u32[]{:S(2)}) collective-permute-start(f32[24,128]{1,0:T(8,128)S(1)} %get-tuple-element.39.refs_4_.refs_0_), channel_id=1, source_target_pairs={{0,1},{1,0},{2,3},{3,2},{4,5},{5,4},{6,7},{7,6},{8,9},{9,8},{10,11... | collective-permute-start | bytes 36872 | tf_op jit(solution)/shard_map/ppermute | solution.py:686
  6.2 2.4 %collective-permute-start.1 = (f32[24,128]{1,0:T(8,128)S(1)}, f32[24,128]{1,0:T(8,128)S(1)}, u32[]{:S(2)}, u32[]{:S(2)}) collective-permute-start(f32[24,128]{1,0:T(8,128)S(1)} %get-tuple-element.39.refs_4_.refs_0_), channel_id=1, source_target_pairs={{1,2},{2,1},{3,4},{4,3},{5,6},{6,5},{9,10},{10,9},{11,12},{12,11},... | collective-permute-start | bytes 36872 | tf_op jit(solution)/shard_map/ppermute | solution.py:688
  6.8 0.7 %copy-start.2 = (f32[32,16]{0,1:T(8,128)S(1)}, f32[32,16]{0,1:T(8,128)}, u32[]{:S(2)}) copy-start(f32[32,16]{0,1:T(8,128)} %param.14) | copy-start | bytes 6148
  12.5 6.7 %collective-permute-start.2 = (f32[152,128]{1,0:T(8,128)S(1)}, f32[152,128]{1,0:T(8,128)S(1)}, u32[]{:S(2)}, u32[]{:S(2)}) collective-permute-start(f32[152,128]{1,0:T(8,128)S(1)} %get-tuple-element.66), channel_id=1, source_target_pairs={{0,1},{1,0},{2,3},{3,2},{4,5},{5,4},{6,7},{7,6},{8,9},{9,8},{10,11... | collective-permute-start | bytes 233480 | tf_op jit(solution)/shard_map/ppermute | solution.py:714
  19.3 5.8 %collective-permute-start.3 = (f32[152,128]{1,0:T(8,128)S(1)}, f32[152,128]{1,0:T(8,128)S(1)}, u32[]{:S(2)}, u32[]{:S(2)}) collective-permute-start(f32[152,128]{1,0:T(8,128)S(1)} %select_select_fusion.1), channel_id=1, source_target_pairs={{0,2},{1,3},{2,0},{3,1},{4,6},{5,7},{6,4},{7,5},{8,10},{9,11},{10,... | collective-permute-start | bytes 233480 | tf_op jit(solution)/shard_map/ppermute | solution.py:714
  25.2 5.9 %collective-permute-start.4 = (f32[152,128]{1,0:T(8,128)S(1)}, f32[152,128]{1,0:T(8,128)S(1)}, u32[]{:S(2)}, u32[]{:S(2)}) collective-permute-start(f32[152,128]{1,0:T(8,128)S(1)} %select_select_fusion.refs_0_), channel_id=1, source_target_pairs={{0,4},{1,5},{2,6},{3,7},{4,0},{5,1},{6,2},{7,3},{8,12},{9,13},{10,... | collective-permute-start | bytes 233480 | tf_op jit(solution)/shard_map/ppermute | solution.py:714
  31.2 1.3 %collective-permute-start.5 = (f32[48,128]{1,0:T(8,128)S(1)}, f32[48,128]{1,0:T(8,128)S(1)}, u32[]{:S(2)}, u32[]{:S(2)}) collective-permute-start(f32[48,128]{1,0:T(8,128)S(1)} %get-tuple-element.68), channel_id=1, source_target_pairs={{0,8},{8,0},{16,24},{24,16},{1,9},{9,1},{17,25},{25,17},{2,10},{10... | collective-permute-start | bytes 73736 | tf_op jit(solution)/shard_map/ppermute | solution.py:745
  32.5 3.8 %collective-permute-start.6 = (f32[48,128]{1,0:T(8,128)S(1)}, f32[48,128]{1,0:T(8,128)S(1)}, u32[]{:S(2)}, u32[]{:S(2)}) collective-permute-start(f32[48,128]{1,0:T(8,128)S(1)} %add.20), channel_id=1, source_target_pairs={{0,16},{8,24},{16,0},{24,8},{1,17},{9,25},{17,1},{25,9},{2,18},{10... | collective-permute-start | bytes 73736 | tf_op jit(solution)/shard_map/ppermute | solution.py:745
  36.3 3.8 %collective-permute-start.7 = (f32[48,128]{1,0:T(8,128)S(1)}, f32[48,128]{1,0:T(8,128)S(1)}, u32[]{:S(2)}, u32[]{:S(2)}) collective-permute-start(f32[48,128]{1,0:T(8,128)S(1)} %add.21.refs_0_), channel_id=1, source_target_pairs={{0,1},{1,0},{2,3},{3,2},{4,5},{5,4},{6,7},{7,6},{8,9},{9,8},{10,11... | collective-permute-start | bytes 73736 | tf_op jit(solution)/shard_map/ppermute | solution.py:751

commit v5 on v4

--- a/solution.py
+++ b/solution.py
@@ -13,6 +13,7 @@
 LANES = 128
 BLOCK = 2 * LANES
 STREAMS = 3
+REACH = 3
 MARGIN = LANES // 2
 F32 = jnp.float32
 BF16 = jnp.bfloat16
@@ -50,7 +51,7 @@
     deal = np.zeros((BLOCK, BLOCK), np.float32)
     deal[order, np.arange(BLOCK)] = 1.0
     banks = [np.concatenate(hi_lo(x), 1) for x in (coarse_mel, fine_mel)]
-    return deal.astype(BF16), lines, np.concatenate(hi_lo(turns), 0), np.concatenate(banks, 0)
+    return lines, np.concatenate(hi_lo(turns), 0), np.concatenate(banks, 0), deal.astype(BF16)
 
 
 def split(x):
@@ -180,9 +181,9 @@
 
 def backward_kernel(sizes, *refs):
     up, inner, outer, out = refs[:4]
-    up_ref, inner_ref, outer_ref, out_ref = refs[8:12]
-    square, sems = refs[15:]
-    copies = [pltpu.make_async_copy(refs[5 + i], refs[12 + i], sems.at[i]) for i in range(3)]
+    up_ref, inner_ref, outer_ref, out_ref = refs[9:13]
+    square, sems = refs[17:]
+    copies = [pltpu.make_async_copy(refs[5 + i], refs[13 + i], sems.at[i]) for i in range(4)]
     for copy in copies:
         copy.start()
     channels, half, hidden, _ = sizes
@@ -208,13 +209,13 @@
 
 
 def own_kernel(sizes, *refs):
-    sources = refs[:7]
-    packet_ref, latent_ref = refs[7:9]
-    weight_refs = refs[9:13]
-    kept = dict(zip(KEPT, refs[13:25]))
-    up_ref, inner_ref, outer_ref, out_ref, target_ref, deal_ref, square, rows_ref, sems = refs[25:]
+    sources = refs[:6]
+    packet_ref, latent_ref = refs[6:8]
+    weight_refs = refs[8:12]
+    kept = dict(zip(KEPT, refs[12:24]))
+    up_ref, inner_ref, outer_ref, out_ref, target_ref, square, sems = refs[24:]
     channels, half, hidden, frames = sizes
-    spaces = (latent_ref, target_ref, up_ref, inner_ref, outer_ref, out_ref, deal_ref)
+    spaces = (latent_ref, target_ref, up_ref, inner_ref, outer_ref, out_ref)
     copies = []
     for i, (source, space) in enumerate(zip(sources, spaces)):
         if i == 0:
@@ -239,16 +240,6 @@
     wave = jnp.concatenate(decode(sizes, weights, spread, keep, 1.0), 0)
     wave = moved(wave, -MARGIN)
     blocks = frames // LANES
-    rows_ref[...] = jnp.zeros_like(rows_ref)
-    for b in range(blocks):
-        rows_ref[b : b + 1, :] = target_ref[:, b * BLOCK : (b + 1) * BLOCK]
-    whole = rows_ref[...]
-    high = whole.astype(BF16)
-    rest = whole - high.astype(F32)
-    middle = rest.astype(BF16)
-    last = (rest - middle.astype(F32)).astype(BF16)
-    deal = deal_ref[...]
-    dealt = dot(high, deal) + dot(middle, deal) + dot(last, deal)
     packet_ref[0:8, 0:channels] = jnp.transpose(latent[:, 0:LANES])[0:8]
     packet_ref[0:8, channels:] = jnp.transpose(latent[:, frames - LANES :])[LANES - 8 :]
     for r in range(2):
@@ -256,8 +247,9 @@
             packet_ref[8 + r * blocks + b : 9 + r * blocks + b, :] = wave[
                 r : r + 1, b * LANES : (b + 1) * LANES
             ]
-        at = 8 + (2 + r) * blocks
-        packet_ref[at : at + blocks, :] = dealt[0:blocks, r * LANES : (r + 1) * LANES]
+    for row in range(2 * blocks):
+        at = 8 + 2 * blocks + row
+        packet_ref[at : at + 1, :] = target_ref[:, row * LANES : (row + 1) * LANES]
 
 
 def main_kernel(sizes, *refs):
@@ -265,9 +257,9 @@
     weights = {name: ref[...] for name, ref in zip(FORWARD, refs[4:8])}
     kept = dict(zip(KEPT, refs[8:20]))
     up_back, back_inner, outer_back, out_back = (ref[...] for ref in refs[20:24])
-    lines_ref, turns_ref, bank_ref = refs[24:27]
-    keep_ref, send_ref, grads_ref = refs[27:30]
-    (square, wblock, shifted, wave_b, targ_b, lanes_b) = refs[30:36]
+    lines_ref, turns_ref, bank_ref, deal_ref = refs[24:28]
+    keep_ref, send_ref, upper_ref, slope_ref = refs[28:32]
+    (square, wblock, shifted, wave_b, targ_b, lanes_b) = refs[32:38]
     channels, half, hidden, frames = sizes
     window = frames + LANES
     own_blocks = frames // LANES
@@ -278,6 +270,24 @@
     first, second = first_ref[...], second_ref[...]
     left = jnp.where(odd_place, first, second)
     right = jnp.where(odd_place, second, first)
+    for side, packet in enumerate((left, own_ref[...], right)):
+        rows = slice(side * own_blocks, (side + 1) * own_blocks)
+        for r in range(2):
+            columns = slice(r * LANES, (r + 1) * LANES)
+            at = 8 + r * own_blocks
+            wave_b[rows, columns] = packet[at : at + own_blocks]
+            for b in range(own_blocks):
+                at = 8 + 2 * own_blocks + 2 * b + r
+                row = side * own_blocks + b
+                targ_b[row : row + 1, columns] = packet[at : at + 1]
+    whole = targ_b[...]
+    high = whole.astype(BF16).astype(F32)
+    middle = (whole - high).astype(BF16).astype(F32)
+    dealt = dot(
+        jnp.concatenate([high, middle, whole - high - middle], axis=0).astype(BF16), deal_ref[...]
+    )
+    size = targ_b.shape[0]
+    targ_b[...] = dealt[:size] + dealt[size : 2 * size] + dealt[2 * size :]
     square[...] = jnp.zeros_like(square)
     square[MARGIN - 8 : MARGIN, 0:channels] = left[0:8, channels:]
     square[MARGIN : MARGIN + 8, channels:] = right[0:8, 0:channels]
@@ -315,14 +325,6 @@
     ends_wave = decode(sizes, weights, ends, keep, ends_mask)
     slope_a, slope_u, slope_c, slope_m = (saved["slope_" + x] for x in "aucm")
 
-    for side, packet in enumerate((left, own_ref[...], right)):
-        rows = slice(side * own_blocks, (side + 1) * own_blocks)
-        for r in range(2):
-            columns = slice(r * LANES, (r + 1) * LANES)
-            at = 8 + r * own_blocks
-            wave_b[rows, columns] = packet[at : at + own_blocks]
-            at = 8 + (2 + r) * own_blocks
-            targ_b[rows, columns] = packet[at : at + own_blocks]
     for r in range(2):
         columns = slice(r * LANES, (r + 1) * LANES)
         for side in range(2):
@@ -477,27 +479,32 @@
         x + apply(back_inner, pair) * slope_u for x, pair in zip(grad_mixed, spreads)
     ]
     uppers = [split(x) for x in grad_upper]
-    nexts = [split(moved(x, -1)) for x in grad_upper]
+    low = lane < MARGIN
+    slope_edge = jnp.where(low, slope_a[:, :LANES], slope_a[:, frames:])
     edges = []
-    for i in range(STREAMS):
-        both = tuple(jnp.concatenate([x, y], 0) for x, y in zip(uppers[i], nexts[i]))
-        grads = moved(apply(up_back, both) * slope_a, -MARGIN)
-        grads_ref[i * channels : (i + 1) * channels, :] = grads[:, :frames]
-        turned = jnp.transpose(grads[:, frames:])
-        edges.append(jnp.concatenate([turned[LANES - 8 :], turned[:8]], axis=1))
+    for i, value in enumerate(grad_upper):
+        upper_ref[i * 2 * half : (i + 1) * 2 * half, :] = value
+        head, tail = value[:, :LANES], value[:, frames:]
+        both = jnp.concatenate(
+            [jnp.where(low, head, tail), jnp.where(low, moved(head, -1), moved(tail, -1))], 0
+        )
+        turned = jnp.transpose(apply(up_back, split(both)) * slope_edge)
+        edges.append(
+            jnp.concatenate([turned[MARGIN - REACH : MARGIN], turned[MARGIN : MARGIN + REACH]], axis=1)
+        )
+    slope_ref[...] = slope_a
+
+    def against(highs, lows, name):
+        high, low = saved[name + "_h"], saved[name + "_l"]
+        count = high.shape[0]
+        wide = dot(highs, jnp.concatenate([high, low], axis=0), True)
+        return wide[:, :count] + wide[:, count:] + dot(lows, high, True)
 
     def summed(pairs, name):
         rows = pairs[0][0].shape[0]
-        both = jnp.concatenate([x for pair in pairs for x in pair], axis=0)
-        highs = jnp.concatenate([pair[0] for pair in pairs], axis=0)
-        first = dot(both, saved[name + "_h"], True)
-        second = dot(highs, saved[name + "_l"], True)
-        return [
-            first[2 * i * rows : (2 * i + 1) * rows]
-            + first[(2 * i + 1) * rows : (2 * i + 2) * rows]
-            + second[i * rows : (i + 1) * rows]
-            for i in range(STREAMS)
-        ]
+        highs, lows = (jnp.concatenate([pair[i] for pair in pairs], axis=0) for i in range(2))
+        value = against(highs, lows, name)
+        return [value[i * rows : (i + 1) * rows] for i in range(STREAMS)]
 
     def put(value, at, columns):
         rows = value.shape[0] // 2
@@ -523,7 +530,7 @@
             i * step + half,
             slice(3 * half, 4 * half),
         )
-    taps = dot3(jnp.concatenate(views, axis=0), saved["g_h"], saved["g_l"], True)
+    taps = against(*split(jnp.concatenate(views, axis=0)), "g")
     for i in range(STREAMS):
         wblock[0:7, i * half : (i + 1) * half] = (
             taps[8 * i + 1 : 8 * i + 8, :half] + taps[8 * i : 8 * i + 7, half:]
@@ -566,24 +573,26 @@
     edge_lane = lax.broadcasted_iota(jnp.int32, (1, LANES), 1)
     swap = ((low == 0) & (edge_lane >= LANES // 2)) | ((low == step - 1) & (edge_lane < LANES // 2))
     edges = jnp.where(swap, theirs_ref[rows + 8 :, :], mine_ref[rows + 8 :, :])
-    aux_ref[0:8, :] = sum(edges[8 * i : 8 * i + 8] * scale[i] for i in range(STREAMS))
+    aux_ref[0:REACH, :] = sum(edges[REACH * i : REACH * (i + 1)] * scale[i] for i in range(STREAMS))
     for i in range(STREAMS):
         aux_ref[8 + i : 9 + i, :] = jnp.broadcast_to(scale[i], (1, LANES))
 
 
-def latent_kernel(channels, grads_ref, aux_ref, square, grad_ref):
-    frames = grads_ref.shape[1]
-    total = sum(
-        grads_ref[i * channels : (i + 1) * channels, :] * aux_ref[8 + i : 9 + i, 0:1]
-        for i in range(STREAMS)
-    )
-    grad_ref[0] = total
+def latent_kernel(channels, upper_ref, slope_ref, weight_ref, aux_ref, grad_ref, square):
+    frames = grad_ref.shape[2]
+    rows = upper_ref.shape[0] // STREAMS
+    upper = sum(
+        upper_ref[i * rows : (i + 1) * rows, :] * aux_ref[8 + i : 9 + i, 0:1] for i in range(STREAMS)
+    )
+    both = split(jnp.concatenate([upper, moved(upper, -1)], 0))
+    grads = moved(apply(weight_ref[...], both) * slope_ref[...], -MARGIN)[:, :frames]
     square[...] = jnp.zeros_like(square)
-    square[0:8, 0:channels] = aux_ref[0:8, channels:]
-    square[LANES - 8 :, channels:] = aux_ref[0:8, 0:channels]
+    square[0:REACH, 0:channels] = aux_ref[0:REACH, channels:]
+    square[LANES - REACH :, channels:] = aux_ref[0:REACH, 0:channels]
     turned = jnp.transpose(square[...])
-    grad_ref[0, :, 0:LANES] = grad_ref[0, :, 0:LANES] + turned[0:channels]
-    grad_ref[0, :, frames - LANES :] = grad_ref[0, :, frames - LANES :] + turned[channels:]
+    grad_ref[0, :, 0:LANES] = grads[:, :LANES] + turned[0:channels]
+    grad_ref[0, :, LANES : frames - LANES] = grads[:, LANES : frames - LANES]
+    grad_ref[0, :, frames - LANES :] = grads[:, frames - LANES :] + turned[channels:]
 
 
 def final_kernel(sizes, mine_ref, theirs_ref, up_ref, inner_ref, outer_ref, out_ref):
@@ -653,18 +662,16 @@
             *forward,
             *kept_shapes(channels, half, hidden, window),
         ],
-        [latent, target, *weights, constants[0]],
+        [latent, target, *weights],
         [
             *[pltpu.VMEM(x.shape, F32) for x in weights],
             pltpu.VMEM(target.shape, F32),
-            pltpu.VMEM((BLOCK, BLOCK), BF16),
             pltpu.VMEM((LANES, LANES), F32),
-            pltpu.VMEM((8, BLOCK), F32),
-            pltpu.SemaphoreType.DMA((7,)),
+            pltpu.SemaphoreType.DMA((6,)),
         ],
         "own_decode",
         8,
-        7,
+        6,
     )
     backward = run(
         lambda *refs: backward_kernel(sizes, *refs),
@@ -673,14 +680,14 @@
             ((2 * half, 12 * hidden), BF16),
             ((2 * hidden, 6 * half), BF16),
             ((2 * half, 24), BF16),
-            constants[1].shape,
-            *[(x.shape, BF16) for x in constants[2:]],
+            constants[0].shape,
+            *[(x.shape, BF16) for x in constants[1:]],
         ],
-        [*weights, own, *constants[1:]],
-        [pltpu.VMEM((LANES, LANES), F32), pltpu.SemaphoreType.DMA((3,))],
+        [*weights, own, *constants],
+        [pltpu.VMEM((LANES, LANES), F32), pltpu.SemaphoreType.DMA((4,))],
         "backward_weights",
         4,
-        3,
+        4,
     )
     pairs = [(i, i ^ 1) for i in range(count) if i ^ 1 < count]
     first = lax.ppermute(own, "tm", pairs)
@@ -690,9 +697,13 @@
     part = half + hidden // 2
     rows = STREAMS * part
 
-    payload, sent, grads = run(
+    payload, sent, upper, slope = run(
         lambda *refs: main_kernel(sizes, *refs),
-        [*[(rows + 8 + 8 * STREAMS, LANES)] * 2, (STREAMS * channels, frames)],
+        [
+            *[(rows + 8 + REACH * STREAMS, LANES)] * 2,
+            (STREAMS * 2 * half, window),
+            (channels, window),
+        ],
         [own, first, second, own_latent, *made, *backward],
         [
             pltpu.VMEM((LANES, LANES), F32),
@@ -731,12 +742,12 @@
         2,
     )
     (latent_grad,) = run(
-        lambda grads_ref, aux_ref, out, square: latent_kernel(channels, grads_ref, aux_ref, square, out),
+        lambda *refs: latent_kernel(channels, *refs),
         [latent.shape],
-        [grads, aux],
+        [upper, slope, backward[0], aux],
         [pltpu.VMEM((LANES, LANES), F32)],
         "latent",
-        2,
+        4,
     )
 
     count = lax.axis_size("dp")

time: 41.3 us -> 40.9 us (level)
  starting transfers between devices: 18.1 us -> 17.1 us
    ppermute x1, starting transfers between devices: 1.54 us -> 0.73 us  [local(): theirs = lax.ppermute(weights, 'tm', [(i, i ^ 1) for i in range(count)])]
    ppermute x1, waiting for transfers between devices: 1.46 us -> 1.98 us  [local(): theirs = lax.ppermute(weights, 'tm', [(i, i ^ 1) for i in range(count)])]
  transfers between devices with their start and end apart: 8 -> 8, of which waited for: 6 -> 6; matrix products, arithmetic and copies ran while one was open for 0% -> 0% of each run, Pallas kernels for 5% -> 6%
where the time goes in v5:
time: 40.9 us; the launch traced here: 40.6 us
  starting transfers between devices  17.1 us (42%)
  waiting for transfers between devices  12.5 us (31%)
  Pallas kernels  9.39 us (23%)
  between operations  0.79 us (2%)
  local copies, waits for them, and re-layouts  0.67 us (2%)
    ppermute x3, starting transfers between devices, local(): theirs = lax.ppermute(sent, 'tm', [(i, i ^ step) for i in range(count)])  11.1 us
    pallas_call x6, Pallas kernels, run(): pl.pallas_call(kernel, out_shape=tuple((jax.ShapeDtypeStruct(*(x if isins...  9.39 us
    ppermute x3, waiting for transfers between devices, local(): theirs = lax.ppermute(sent, 'tm', [(i, i ^ step) for i in range(count)])  6.98 us
    ppermute x2, waiting for transfers between devices, local(): theirs = lax.ppermute(weights, 'dp', [(i, i ^ step) for i in range(count)])  3.53 us
    ppermute x1, starting transfers between devices, local(): first = lax.ppermute(own, 'tm', pairs)  3.06 us
    ppermute x1, waiting for transfers between devices, local(): theirs = lax.ppermute(weights, 'tm', [(i, i ^ 1) for i in range(count)])  1.98 us
    ppermute x2, starting transfers between devices, local(): theirs = lax.ppermute(weights, 'dp', [(i, i ^ step) for i in range(count)])  1.55 us
  transfers between devices with their start and end apart: 8, of which 6 were waited for; matrix products, arithmetic and copies ran while one was open for 0% of the time, Pallas kernels for 6%

profile of v5, /device:TPU:0, one launch (start us, length us, event | category | flops | bytes accessed | tf_op | source)
XLA Modules:
  0.0 40.6 jit_solution(9612981244500157641)
XLA Ops:
  0.7 2.2 %own_decode.1 = (f32[24,128]{1,0:T(8,128)S(1)}, f32[64,512]{1,0:T(8,128)S(1)}, bf16[64,384]{1,0:T(8,128)(2,1)S(1)}, bf16[32,384]{1,0:T(8,128)(2,1)S(1)}, bf16[64...) custom-call(f32[1,64,512]{2,1,0:T(8,128)} %refs_0_.2, ...), custom_call_target="tpu_custom_call" | custom-call | tf_op jit(solution)/shard_map/own_decode/pallas_call | solution.py:625
  2.9 3.1 %collective-permute-start = (f32[24,128]{1,0:T(8,128)S(1)}, f32[24,128]{1,0:T(8,128)S(1)}, u32[]{:S(2)}, u32[]{:S(2)}) collective-permute-start(f32[24,128]{1,0:T(8,128)S(1)} %get-tuple-element.41.refs_4_.refs_0_), channel_id=1, source_target_pairs={{0,1},{1,0},{2,3},{3,2},{4,5},{5,4},{6,7},{7,6},{8,9},{9,8},{10,11... | collective-permute-start | bytes 36872 | tf_op jit(solution)/shard_map/ppermute | solution.py:693
  6.0 0.7 %collective-permute-start.1 = (f32[24,128]{1,0:T(8,128)S(1)}, f32[24,128]{1,0:T(8,128)S(1)}, u32[]{:S(2)}, u32[]{:S(2)}) collective-permute-start(f32[24,128]{1,0:T(8,128)S(1)} %get-tuple-element.41.refs_4_.refs_0_), channel_id=1, source_target_pairs={{1,2},{2,1},{3,4},{4,3},{5,6},{6,5},{9,10},{10,9},{11,12},{12,11},... | collective-permute-start | bytes 36872 | tf_op jit(solution)/shard_map/ppermute | solution.py:695
  6.6 0.0 copy-start.2
  6.7 0.6 %copy-done.2 = f32[32,16]{0,1:T(8,128)S(1)} copy-done((f32[32,16]{0,1:T(8,128)S(1)}, f32[32,16]{0,1:T(8,128)}, u32[]{:S(2)}) %copy-start.2) | copy-done | bytes 2072
  7.3 1.1 %backward_weights.1 = (bf16[64,384]{1,0:T(8,128)(2,1)S(1)}, bf16[64,192]{1,0:T(8,128)(2,1)S(1)}, bf16[32,192]{1,0:T(8,128)(2,1)S(1)}, bf16[64,24]{1,0:T(8,128)(2...) custom-call(f32[4,32,64]{2,1,0:T(8,128)S(1)} %copy-done, ...), custom_call_target="tpu_custom_call" | custom-call | tf_op jit(solution)/shard_map/backward_weights/pallas_call | solution.py:625
  8.5 4.0 %losses.1 = (f32[137,128]{1,0:T(8,128)S(1)}, f32[137,128]{1,0:T(8,128)S(1)}, f32[192,640]{1,0:T(8,128)S(1)}, f32[64,640]{1,0:T(8,128)S(1)}) custom-call(f32[24,128]{1,0:T(8,128)S(1)} %get-tuple-element.41.refs_4_.refs_0_, f32[24,128]{1,0:T(8,128)S(1)} %collective-permute-done.refs_1_, f32[24,128]{1,0:T(8,128)S(1)} %collective-permute-done.1.refs_2_, ...), custom_call_target="tpu_custom_call" | custom-call | tf_op jit(solution)/shard_map/losses/pallas_call | solution.py:625
  12.4 4.3 %collective-permute-start.2 = (f32[137,128]{1,0:T(8,128)S(1)}, f32[137,128]{1,0:T(8,128)S(1)}, u32[]{:S(2)}, u32[]{:S(2)}) collective-permute-start(f32[137,128]{1,0:T(8,128)S(1)} %get-tuple-element.70), channel_id=1, source_target_pairs={{0,1},{1,0},{2,3},{3,2},{4,5},{5,4},{6,7},{7,6},{8,9},{9,8},{10,11... | collective-permute-start | bytes 210440 | tf_op jit(solution)/shard_map/ppermute | solution.py:725
  16.8 2.3 %collective-permute-done.2 = f32[137,128]{1,0:T(8,128)S(1)} collective-permute-done((f32[137,128]{1,0:T(8,128)S(1)}, f32[137,128]{1,0:T(8,128)S(1)}, u32[]{:S(2)}, u32[]{:S(2)}) %collective-permute-start.2) | collective-permute-done | bytes 70176 | tf_op jit(solution)/shard_map/ppermute | solution.py:725
  19.1 0.1 select_select_fusion.1
  19.2 3.3 %collective-permute-start.3 = (f32[137,128]{1,0:T(8,128)S(1)}, f32[137,128]{1,0:T(8,128)S(1)}, u32[]{:S(2)}, u32[]{:S(2)}) collective-permute-start(f32[137,128]{1,0:T(8,128)S(1)} %select_select_fusion.1), channel_id=1, source_target_pairs={{0,2},{1,3},{2,0},{3,1},{4,6},{5,7},{6,4},{7,5},{8,10},{9,11},{10,... | collective-permute-start | bytes 210440 | tf_op jit(solution)/shard_map/ppermute | solution.py:725
  22.5 2.3 %collective-permute-done.3 = f32[137,128]{1,0:T(8,128)S(1)} collective-permute-done((f32[137,128]{1,0:T(8,128)S(1)}, f32[137,128]{1,0:T(8,128)S(1)}, u32[]{:S(2)}, u32[]{:S(2)}) %collective-permute-start.3) | collective-permute-done | bytes 70176 | tf_op jit(solution)/shard_map/ppermute | solution.py:725
  24.9 0.1 select_select_fusion.refs_0_
  25.0 3.4 %collective-permute-start.4 = (f32[137,128]{1,0:T(8,128)S(1)}, f32[137,128]{1,0:T(8,128)S(1)}, u32[]{:S(2)}, u32[]{:S(2)}) collective-permute-start(f32[137,128]{1,0:T(8,128)S(1)} %select_select_fusion.refs_0_), channel_id=1, source_target_pairs={{0,4},{1,5},{2,6},{3,7},{4,0},{5,1},{6,2},{7,3},{8,12},{9,13},{10,... | collective-permute-start | bytes 210440 | tf_op jit(solution)/shard_map/ppermute | solution.py:725
  28.4 2.3 %collective-permute-done.4.refs_1_ = f32[137,128]{1,0:T(8,128)S(1)} collective-permute-done((f32[137,128]{1,0:T(8,128)S(1)}, f32[137,128]{1,0:T(8,128)S(1)}, u32[]{:S(2)}, u32[]{:S(2)}) %collective-permute-start.4) | collective-permute-done | bytes 70176 | tf_op jit(solution)/shard_map/ppermute | solution.py:725
  30.7 0.1 combine.1
  30.8 0.1 collective-permute-start.5
  30.9 1.2 %collective-permute-done.5 = f32[48,128]{1,0:T(8,128)S(1)} collective-permute-done((f32[48,128]{1,0:T(8,128)S(1)}, f32[48,128]{1,0:T(8,128)S(1)}, u32[]{:S(2)}, u32[]{:S(2)}) %collective-permute-start.5) | collective-permute-done | bytes 24608 | tf_op jit(solution)/shard_map/ppermute | solution.py:756
  32.1 1.5 %collective-permute-start.6 = (f32[48,128]{1,0:T(8,128)S(1)}, f32[48,128]{1,0:T(8,128)S(1)}, u32[]{:S(2)}, u32[]{:S(2)}) collective-permute-start(f32[48,128]{1,0:T(8,128)S(1)} %add.20), channel_id=1, source_target_pairs={{0,16},{8,24},{16,0},{24,8},{1,17},{9,25},{17,1},{25,9},{2,18},{10... | collective-permute-start | bytes 73736 | tf_op jit(solution)/shard_map/ppermute | solution.py:756
  33.6 2.3 %collective-permute-done.6 = f32[48,128]{1,0:T(8,128)S(1)} collective-permute-done((f32[48,128]{1,0:T(8,128)S(1)}, f32[48,128]{1,0:T(8,128)S(1)}, u32[]{:S(2)}, u32[]{:S(2)}) %collective-permute-start.6) | collective-permute-done | bytes 24608 | tf_op jit(solution)/shard_map/ppermute | solution.py:756
  35.9 0.7 %collective-permute-start.7 = (f32[48,128]{1,0:T(8,128)S(1)}, f32[48,128]{1,0:T(8,128)S(1)}, u32[]{:S(2)}, u32[]{:S(2)}) collective-permute-start(f32[48,128]{1,0:T(8,128)S(1)} %add.21.refs_0_), channel_id=1, source_target_pairs={{0,1},{1,0},{2,3},{3,2},{4,5},{5,4},{6,7},{7,6},{8,9},{9,8},{10,11... | collective-permute-start | bytes 73736 | tf_op jit(solution)/shard_map/ppermute | solution.py:762
  36.7 1.1 %latent.1 = f32[1,64,512]{2,1,0:T(8,128)} custom-call(f32[192,640]{1,0:T(8,128)S(1)} %get-tuple-element.67.refs_0_, f32[64,640]{1,0:T(8,128)S(1)} %get-tuple-element.68.refs_1_, bf16[64,384]{1,0:T(8,128)(2,1)S(1)} %get-tuple-element.59.refs_20_.refs_2_, f32[16,128]{1,0:T(8,128)S(1)} %get-tuple-element.71.refs_3_), custom_call_target="tpu_custom_call" | custom-call | tf_op jit(solution)/shard_map/latent/pallas_call | solution.py:625
  37.8 2.0 %collective-permute-done.7.refs_1_ = f32[48,128]{1,0:T(8,128)S(1)} collective-permute-done((f32[48,128]{1,0:T(8,128)S(1)}, f32[48,128]{1,0:T(8,128)S(1)}, u32[]{:S(2)}, u32[]{:S(2)}) %collective-permute-start.7) | collective-permute-done | bytes 24608 | tf_op jit(solution)/shard_map/ppermute | solution.py:762
  39.8 0.9 %final.1 = (f32[4,32,64]{2,1,0:T(8,128)}, f32[3,16,32]{2,1,0:T(8,128)}, f32[16,32]{1,0:T(8,128)}, f32[7,32]{1,0:T(8,128)}) custom-call(f32[48,128]{1,0:T(8,128)S(1)} %add.21.refs_0_, f32[48,128]{1,0:T(8,128)S(1)} %collective-permute-done.7.refs_1_), custom_call_target="tpu_custom_call" | custom-call | tf_op jit(solution)/shard_map/final/pallas_call | solution.py:625
  (13 shorter events, 0.0 us)
Async XLA Ops:
  0.6 6.0 %copy-start = (f32[4,32,64]{2,1,0:T(8,128)S(1)}, f32[4,32,64]{2,1,0:T(8,128)}, u32[]{:S(2)}) copy-start(f32[4,32,64]{2,1,0:T(8,128)} %refs_0_.3) | copy-start | bytes 98308
  0.6 6.0 %copy-start.3 = (f32[7,32]{1,0:T(8,128)S(1)}, f32[7,32]{1,0:T(8,128)}, u32[]{:S(2)}) copy-start(f32[7,32]{1,0:T(8,128)} %refs_3_.3) | copy-start | bytes 2692
  2.9 3.8 %copy-start.1 = (f32[3,16,32]{2,1,0:T(8,128)S(1)}, f32[3,16,32]{2,1,0:T(8,128)}, u32[]{:S(2)}) copy-start(f32[3,16,32]{2,1,0:T(8,128)} %refs_1_.3) | copy-start | bytes 18436
  2.9 5.6 %collective-permute-start = (f32[24,128]{1,0:T(8,128)S(1)}, f32[24,128]{1,0:T(8,128)S(1)}, u32[]{:S(2)}, u32[]{:S(2)}) collective-permute-start(f32[24,128]{1,0:T(8,128)S(1)} %get-tuple-element.41.refs_4_.refs_0_), channel_id=1, source_target_pairs={{0,1},{1,0},{2,3},{3,2},{4,5},{5,4},{6,7},{7,6},{8,9},{9,8},{10,11... | collective-permute-start | bytes 36872 | tf_op jit(solution)/shard_map/ppermute | solution.py:693
  6.0 2.5 %collective-permute-start.1 = (f32[24,128]{1,0:T(8,128)S(1)}, f32[24,128]{1,0:T(8,128)S(1)}, u32[]{:S(2)}, u32[]{:S(2)}) collective-permute-start(f32[24,128]{1,0:T(8,128)S(1)} %get-tuple-element.41.refs_4_.refs_0_), channel_id=1, source_target_pairs={{1,2},{2,1},{3,4},{4,3},{5,6},{6,5},{9,10},{10,9},{11,12},{12,11},... | collective-permute-start | bytes 36872 | tf_op jit(solution)/shard_map/ppermute | solution.py:695
  6.6 0.7 %copy-start.2 = (f32[32,16]{0,1:T(8,128)S(1)}, f32[32,16]{0,1:T(8,128)}, u32[]{:S(2)}) copy-start(f32[32,16]{0,1:T(8,128)} %param.14) | copy-start | bytes 6148
  12.4 6.7 %collective-permute-start.2 = (f32[137,128]{1,0:T(8,128)S(1)}, f32[137,128]{1,0:T(8,128)S(1)}, u32[]{:S(2)}, u32[]{:S(2)}) collective-permute-start(f32[137,128]{1,0:T(8,128)S(1)} %get-tuple-element.70), channel_id=1, source_target_pairs={{0,1},{1,0},{2,3},{3,2},{4,5},{5,4},{6,7},{7,6},{8,9},{9,8},{10,11... | collective-permute-start | bytes 210440 | tf_op jit(solution)/shard_map/ppermute | solution.py:725
  19.2 5.7 %collective-permute-start.3 = (f32[137,128]{1,0:T(8,128)S(1)}, f32[137,128]{1,0:T(8,128)S(1)}, u32[]{:S(2)}, u32[]{:S(2)}) collective-permute-start(f32[137,128]{1,0:T(8,128)S(1)} %select_select_fusion.1), channel_id=1, source_target_pairs={{0,2},{1,3},{2,0},{3,1},{4,6},{5,7},{6,4},{7,5},{8,10},{9,11},{10,... | collective-permute-start | bytes 210440 | tf_op jit(solution)/shard_map/ppermute | solution.py:725
  25.0 5.8 %collective-permute-start.4 = (f32[137,128]{1,0:T(8,128)S(1)}, f32[137,128]{1,0:T(8,128)S(1)}, u32[]{:S(2)}, u32[]{:S(2)}) collective-permute-start(f32[137,128]{1,0:T(8,128)S(1)} %select_select_fusion.refs_0_), channel_id=1, source_target_pairs={{0,4},{1,5},{2,6},{3,7},{4,0},{5,1},{6,2},{7,3},{8,12},{9,13},{10,... | collective-permute-start | bytes 210440 | tf_op jit(solution)/shard_map/ppermute | solution.py:725
  30.8 1.3 %collective-permute-start.5 = (f32[48,128]{1,0:T(8,128)S(1)}, f32[48,128]{1,0:T(8,128)S(1)}, u32[]{:S(2)}, u32[]{:S(2)}) collective-permute-start(f32[48,128]{1,0:T(8,128)S(1)} %get-tuple-element.72), channel_id=1, source_target_pairs={{0,8},{8,0},{16,24},{24,16},{1,9},{9,1},{17,25},{25,17},{2,10},{10... | collective-permute-start | bytes 73736 | tf_op jit(solution)/shard_map/ppermute | solution.py:756
  32.1 3.8 %collective-permute-start.6 = (f32[48,128]{1,0:T(8,128)S(1)}, f32[48,128]{1,0:T(8,128)S(1)}, u32[]{:S(2)}, u32[]{:S(2)}) collective-permute-start(f32[48,128]{1,0:T(8,128)S(1)} %add.20), channel_id=1, source_target_pairs={{0,16},{8,24},{16,0},{24,8},{1,17},{9,25},{17,1},{25,9},{2,18},{10... | collective-permute-start | bytes 73736 | tf_op jit(solution)/shard_map/ppermute | solution.py:756
  35.9 3.8 %collective-permute-start.7 = (f32[48,128]{1,0:T(8,128)S(1)}, f32[48,128]{1,0:T(8,128)S(1)}, u32[]{:S(2)}, u32[]{:S(2)}) collective-permute-start(f32[48,128]{1,0:T(8,128)S(1)} %add.21.refs_0_), channel_id=1, source_target_pairs={{0,1},{1,0},{2,3},{3,2},{4,5},{5,4},{6,7},{7,6},{8,9},{9,8},{10,11... | collective-permute-start | bytes 73736 | tf_op jit(solution)/shard_map/ppermute | solution.py:762

commit v6 on v5

--- a/solution.py
+++ b/solution.py
@@ -595,10 +595,10 @@
     grad_ref[0, :, frames - LANES :] = grads[:, frames - LANES :] + turned[channels:]
 
 
-def final_kernel(sizes, mine_ref, theirs_ref, up_ref, inner_ref, outer_ref, out_ref):
+def final_kernel(sizes, mine_ref, far_ref, theirs_ref, theirs_far_ref, up_ref, inner_ref, outer_ref, out_ref):
     channels, half, hidden, params = sizes
     step = half + hidden // 2
-    mine, theirs = mine_ref[...], theirs_ref[...]
+    mine, theirs = mine_ref[...] + far_ref[...], theirs_ref[...] + theirs_far_ref[...]
     odd_place = lax.rem(lax.axis_index("tm"), 2) == 1
     low = jnp.where(odd_place, theirs[:step], mine[:step])
     high = jnp.where(odd_place, mine[:step], theirs[:step])
@@ -750,20 +750,22 @@
         4,
     )
 
-    count = lax.axis_size("dp")
+    depth = lax.axis_size("dp")
     step = 1
-    while True:
-        theirs = lax.ppermute(weights, "dp", [(i, i ^ step) for i in range(count)])
-        weights = weights + theirs
+    while 2 * step < depth:
+        weights = weights + lax.ppermute(weights, "dp", [(i, i ^ step) for i in range(depth)])
         step *= 2
-        if step == count:
-            break
-    count = lax.axis_size("tm")
-    theirs = lax.ppermute(weights, "tm", [(i, i ^ 1) for i in range(count)])
+    places = [(d, t) for d in range(depth) for t in range(count)]
+
+    def partner(far, near):
+        pairs = [(d * count + t, (d ^ far) * count + (t ^ near)) for d, t in places]
+        return lax.ppermute(weights, ("dp", "tm"), pairs)
+
+    parts = [weights, partner(step, 0), partner(0, 1), partner(step, 1)]
     up, inner, outer, out = run(
         lambda *refs: final_kernel((channels, half, hidden, params), *refs),
         [up_kernel.shape, inner_kernel.shape, outer_kernel.shape[::-1], out_kernel.shape],
-        [weights, theirs],
+        parts,
         [],
         "final",
         2,

time: 40.9 us -> 40.2 us (0.983)
  waiting for transfers between devices: 12.5 us -> 10.5 us
  starting transfers between devices: 17.1 us -> 18.4 us
    ppermute x3 -> x4, waiting for transfers between devices: 5.51 us -> 3.5 us  [the longest x3 2.32 us: partner(): return lax.ppermute(weights, ('dp', 'tm'), pairs)]
    ppermute x3 -> x4, starting transfers between devices: 2.28 us -> 3.56 us  [the longest x3 3.49 us: partner(): return lax.ppermute(weights, ('dp', 'tm'), pairs)]
  transfers between devices with their start and end apart: 8 -> 9, of which waited for: 6 -> 6; matrix products, arithmetic and copies ran while one was open for 0% -> 0% of each run, Pallas kernels for 6% -> 6%
where the time goes in v6:
time: 40.2 us; the launch traced here: 39.9 us
  starting transfers between devices  18.4 us (46%)
  waiting for transfers between devices  10.5 us (26%)
  Pallas kernels  9.4 us (23%)
  between operations  0.79 us (2%)
  local copies, waits for them, and re-layouts  0.67 us (2%)
    ppermute x3, starting transfers between devices, local(): theirs = lax.ppermute(sent, 'tm', [(i, i ^ step) for i in range(count)])  11.1 us
    pallas_call x6, Pallas kernels, run(): pl.pallas_call(kernel, out_shape=tuple((jax.ShapeDtypeStruct(*(x if isins...  9.4 us
    ppermute x3, waiting for transfers between devices, local(): theirs = lax.ppermute(sent, 'tm', [(i, i ^ step) for i in range(count)])  6.98 us
    ppermute x3, starting transfers between devices, partner(): return lax.ppermute(weights, ('dp', 'tm'), pairs)  3.49 us
    ppermute x1, starting transfers between devices, local(): first = lax.ppermute(own, 'tm', pairs)  3.06 us
    ppermute x3, waiting for transfers between devices, partner(): return lax.ppermute(weights, ('dp', 'tm'), pairs)  2.32 us
    ppermute x1, waiting for transfers between devices, local(): lax.ppermute(weights, 'dp', [(i, i ^ step) for i in range(depth)])  1.18 us
  transfers between devices with their start and end apart: 9, of which 6 were waited for; matrix products, arithmetic and copies ran while one was open for 0% of the time, Pallas kernels for 6%

profile of v6, /device:TPU:0, one launch (start us, length us, event | category | flops | bytes accessed | tf_op | source)
XLA Modules:
  0.0 39.9 jit_solution(16434727321934276781)
XLA Ops:
  0.7 2.2 %own_decode.1 = (f32[24,128]{1,0:T(8,128)S(1)}, f32[64,512]{1,0:T(8,128)S(1)}, bf16[64,384]{1,0:T(8,128)(2,1)S(1)}, bf16[32,384]{1,0:T(8,128)(2,1)S(1)}, bf16[64...) custom-call(f32[1,64,512]{2,1,0:T(8,128)} %refs_0_.2, ...), custom_call_target="tpu_custom_call" | custom-call | tf_op jit(solution)/shard_map/own_decode/pallas_call | solution.py:625
  2.9 3.1 %collective-permute-start = (f32[24,128]{1,0:T(8,128)S(1)}, f32[24,128]{1,0:T(8,128)S(1)}, u32[]{:S(2)}, u32[]{:S(2)}) collective-permute-start(f32[24,128]{1,0:T(8,128)S(1)} %get-tuple-element.41.refs_4_.refs_0_), channel_id=1, source_target_pairs={{0,1},{1,0},{2,3},{3,2},{4,5},{5,4},{6,7},{7,6},{8,9},{9,8},{10,11... | collective-permute-start | bytes 36872 | tf_op jit(solution)/shard_map/ppermute | solution.py:693
  6.0 0.7 %collective-permute-start.1 = (f32[24,128]{1,0:T(8,128)S(1)}, f32[24,128]{1,0:T(8,128)S(1)}, u32[]{:S(2)}, u32[]{:S(2)}) collective-permute-start(f32[24,128]{1,0:T(8,128)S(1)} %get-tuple-element.41.refs_4_.refs_0_), channel_id=1, source_target_pairs={{1,2},{2,1},{3,4},{4,3},{5,6},{6,5},{9,10},{10,9},{11,12},{12,11},... | collective-permute-start | bytes 36872 | tf_op jit(solution)/shard_map/ppermute | solution.py:695
  6.7 0.6 %copy-done.2 = f32[32,16]{0,1:T(8,128)S(1)} copy-done((f32[32,16]{0,1:T(8,128)S(1)}, f32[32,16]{0,1:T(8,128)}, u32[]{:S(2)}) %copy-start.2) | copy-done | bytes 2072
  7.3 1.1 %backward_weights.1 = (bf16[64,384]{1,0:T(8,128)(2,1)S(1)}, bf16[64,192]{1,0:T(8,128)(2,1)S(1)}, bf16[32,192]{1,0:T(8,128)(2,1)S(1)}, bf16[64,24]{1,0:T(8,128)(2...) custom-call(f32[4,32,64]{2,1,0:T(8,128)S(1)} %copy-done, ...), custom_call_target="tpu_custom_call" | custom-call | tf_op jit(solution)/shard_map/backward_weights/pallas_call | solution.py:625
  8.5 4.0 %losses.1 = (f32[137,128]{1,0:T(8,128)S(1)}, f32[137,128]{1,0:T(8,128)S(1)}, f32[192,640]{1,0:T(8,128)S(1)}, f32[64,640]{1,0:T(8,128)S(1)}) custom-call(f32[24,128]{1,0:T(8,128)S(1)} %get-tuple-element.41.refs_4_.refs_0_, f32[24,128]{1,0:T(8,128)S(1)} %collective-permute-done.refs_1_, f32[24,128]{1,0:T(8,128)S(1)} %collective-permute-done.1.refs_2_, ...), custom_call_target="tpu_custom_call" | custom-call | tf_op jit(solution)/shard_map/losses/pallas_call | solution.py:625
  12.4 4.3 %collective-permute-start.2 = (f32[137,128]{1,0:T(8,128)S(1)}, f32[137,128]{1,0:T(8,128)S(1)}, u32[]{:S(2)}, u32[]{:S(2)}) collective-permute-start(f32[137,128]{1,0:T(8,128)S(1)} %get-tuple-element.70), channel_id=1, source_target_pairs={{0,1},{1,0},{2,3},{3,2},{4,5},{5,4},{6,7},{7,6},{8,9},{9,8},{10,11... | collective-permute-start | bytes 210440 | tf_op jit(solution)/shard_map/ppermute | solution.py:725
  16.8 2.3 %collective-permute-done.2 = f32[137,128]{1,0:T(8,128)S(1)} collective-permute-done((f32[137,128]{1,0:T(8,128)S(1)}, f32[137,128]{1,0:T(8,128)S(1)}, u32[]{:S(2)}, u32[]{:S(2)}) %collective-permute-start.2) | collective-permute-done | bytes 70176 | tf_op jit(solution)/shard_map/ppermute | solution.py:725
  19.1 0.1 select_select_fusion.1
  19.2 3.3 %collective-permute-start.3 = (f32[137,128]{1,0:T(8,128)S(1)}, f32[137,128]{1,0:T(8,128)S(1)}, u32[]{:S(2)}, u32[]{:S(2)}) collective-permute-start(f32[137,128]{1,0:T(8,128)S(1)} %select_select_fusion.1), channel_id=1, source_target_pairs={{0,2},{1,3},{2,0},{3,1},{4,6},{5,7},{6,4},{7,5},{8,10},{9,11},{10,... | collective-permute-start | bytes 210440 | tf_op jit(solution)/shard_map/ppermute | solution.py:725
  22.5 2.3 %collective-permute-done.3 = f32[137,128]{1,0:T(8,128)S(1)} collective-permute-done((f32[137,128]{1,0:T(8,128)S(1)}, f32[137,128]{1,0:T(8,128)S(1)}, u32[]{:S(2)}, u32[]{:S(2)}) %collective-permute-start.3) | collective-permute-done | bytes 70176 | tf_op jit(solution)/shard_map/ppermute | solution.py:725
  24.9 0.1 select_select_fusion.refs_0_
  25.0 3.4 %collective-permute-start.4 = (f32[137,128]{1,0:T(8,128)S(1)}, f32[137,128]{1,0:T(8,128)S(1)}, u32[]{:S(2)}, u32[]{:S(2)}) collective-permute-start(f32[137,128]{1,0:T(8,128)S(1)} %select_select_fusion.refs_0_), channel_id=1, source_target_pairs={{0,4},{1,5},{2,6},{3,7},{4,0},{5,1},{6,2},{7,3},{8,12},{9,13},{10,... | collective-permute-start | bytes 210440 | tf_op jit(solution)/shard_map/ppermute | solution.py:725
  28.4 2.3 %collective-permute-done.4.refs_1_ = f32[137,128]{1,0:T(8,128)S(1)} collective-permute-done((f32[137,128]{1,0:T(8,128)S(1)}, f32[137,128]{1,0:T(8,128)S(1)}, u32[]{:S(2)}, u32[]{:S(2)}) %collective-permute-start.4) | collective-permute-done | bytes 70176 | tf_op jit(solution)/shard_map/ppermute | solution.py:725
  30.7 0.1 combine.1
  30.8 0.1 collective-permute-start.5
  30.9 1.2 %collective-permute-done.5 = f32[48,128]{1,0:T(8,128)S(1)} collective-permute-done((f32[48,128]{1,0:T(8,128)S(1)}, f32[48,128]{1,0:T(8,128)S(1)}, u32[]{:S(2)}, u32[]{:S(2)}) %collective-permute-start.5) | collective-permute-done | bytes 24608 | tf_op jit(solution)/shard_map/ppermute | solution.py:756
  32.1 1.5 %collective-permute-start.6 = (f32[48,128]{1,0:T(8,128)S(1)}, f32[48,128]{1,0:T(8,128)S(1)}, u32[]{:S(2)}, u32[]{:S(2)}) collective-permute-start(f32[48,128]{1,0:T(8,128)S(1)} %add.17.refs_0_), channel_id=1, source_target_pairs={{0,16},{1,17},{2,18},{3,19},{4,20},{5,21},{6,22},{7,23},{8,24},{9,... | collective-permute-start | bytes 73736 | tf_op jit(solution)/shard_map/ppermute | solution.py:762
  33.6 0.7 %collective-permute-start.7 = (f32[48,128]{1,0:T(8,128)S(1)}, f32[48,128]{1,0:T(8,128)S(1)}, u32[]{:S(2)}, u32[]{:S(2)}) collective-permute-start(f32[48,128]{1,0:T(8,128)S(1)} %add.17.refs_0_), channel_id=1, source_target_pairs={{0,1},{1,0},{2,3},{3,2},{4,5},{5,4},{6,7},{7,6},{8,9},{9,8},{10,11... | collective-permute-start | bytes 73736 | tf_op jit(solution)/shard_map/ppermute | solution.py:762
  34.3 1.3 %collective-permute-start.8 = (f32[48,128]{1,0:T(8,128)S(1)}, f32[48,128]{1,0:T(8,128)S(1)}, u32[]{:S(2)}, u32[]{:S(2)}) collective-permute-start(f32[48,128]{1,0:T(8,128)S(1)} %add.17.refs_0_), channel_id=1, source_target_pairs={{0,17},{1,16},{2,19},{3,18},{4,21},{5,20},{6,23},{7,22},{8,25},{9,... | collective-permute-start | bytes 73736 | tf_op jit(solution)/shard_map/ppermute | solution.py:762
  35.6 1.1 %latent.1 = f32[1,64,512]{2,1,0:T(8,128)} custom-call(f32[192,640]{1,0:T(8,128)S(1)} %get-tuple-element.67.refs_0_, f32[64,640]{1,0:T(8,128)S(1)} %get-tuple-element.68.refs_1_, bf16[64,384]{1,0:T(8,128)(2,1)S(1)} %get-tuple-element.59.refs_20_.refs_2_, f32[16,128]{1,0:T(8,128)S(1)} %get-tuple-element.71.refs_3_), custom_call_target="tpu_custom_call" | custom-call | tf_op jit(solution)/shard_map/latent/pallas_call | solution.py:625
  36.7 0.7 %collective-permute-done.7.refs_2_ = f32[48,128]{1,0:T(8,128)S(1)} collective-permute-done((f32[48,128]{1,0:T(8,128)S(1)}, f32[48,128]{1,0:T(8,128)S(1)}, u32[]{:S(2)}, u32[]{:S(2)}) %collective-permute-start.7) | collective-permute-done | bytes 24608 | tf_op jit(solution)/shard_map/ppermute | solution.py:762
  37.4 1.6 %collective-permute-done.8.refs_3_ = f32[48,128]{1,0:T(8,128)S(1)} collective-permute-done((f32[48,128]{1,0:T(8,128)S(1)}, f32[48,128]{1,0:T(8,128)S(1)}, u32[]{:S(2)}, u32[]{:S(2)}) %collective-permute-start.8) | collective-permute-done | bytes 24608 | tf_op jit(solution)/shard_map/ppermute | solution.py:762
  39.0 0.9 %final.1 = (f32[4,32,64]{2,1,0:T(8,128)}, f32[3,16,32]{2,1,0:T(8,128)}, f32[16,32]{1,0:T(8,128)}, f32[7,32]{1,0:T(8,128)}) custom-call(f32[48,128]{1,0:T(8,128)S(1)} %add.17.refs_0_, f32[48,128]{1,0:T(8,128)S(1)} %collective-permute-done.6.refs_1_, f32[48,128]{1,0:T(8,128)S(1)} %collective-permute-done.7.refs_2_, f32[48,128]{1,0:T(8,128)S(1)} %collective-permute-done.8.refs_3_), custom_call_target="tpu_custom_call" | custom-call | tf_op jit(solution)/shard_map/final/pallas_call | solution.py:625
  (14 shorter events, 0.1 us)
Async XLA Ops:
  0.6 6.0 %copy-start = (f32[4,32,64]{2,1,0:T(8,128)S(1)}, f32[4,32,64]{2,1,0:T(8,128)}, u32[]{:S(2)}) copy-start(f32[4,32,64]{2,1,0:T(8,128)} %refs_0_.3) | copy-start | bytes 98308
  0.6 6.0 %copy-start.3 = (f32[7,32]{1,0:T(8,128)S(1)}, f32[7,32]{1,0:T(8,128)}, u32[]{:S(2)}) copy-start(f32[7,32]{1,0:T(8,128)} %refs_3_.3) | copy-start | bytes 2692
  2.9 3.8 %copy-start.1 = (f32[3,16,32]{2,1,0:T(8,128)S(1)}, f32[3,16,32]{2,1,0:T(8,128)}, u32[]{:S(2)}) copy-start(f32[3,16,32]{2,1,0:T(8,128)} %refs_1_.3) | copy-start | bytes 18436
  2.9 5.6 %collective-permute-start = (f32[24,128]{1,0:T(8,128)S(1)}, f32[24,128]{1,0:T(8,128)S(1)}, u32[]{:S(2)}, u32[]{:S(2)}) collective-permute-start(f32[24,128]{1,0:T(8,128)S(1)} %get-tuple-element.41.refs_4_.refs_0_), channel_id=1, source_target_pairs={{0,1},{1,0},{2,3},{3,2},{4,5},{5,4},{6,7},{7,6},{8,9},{9,8},{10,11... | collective-permute-start | bytes 36872 | tf_op jit(solution)/shard_map/ppermute | solution.py:693
  6.0 2.5 %collective-permute-start.1 = (f32[24,128]{1,0:T(8,128)S(1)}, f32[24,128]{1,0:T(8,128)S(1)}, u32[]{:S(2)}, u32[]{:S(2)}) collective-permute-start(f32[24,128]{1,0:T(8,128)S(1)} %get-tuple-element.41.refs_4_.refs_0_), channel_id=1, source_target_pairs={{1,2},{2,1},{3,4},{4,3},{5,6},{6,5},{9,10},{10,9},{11,12},{12,11},... | collective-permute-start | bytes 36872 | tf_op jit(solution)/shard_map/ppermute | solution.py:695
  6.6 0.7 %copy-start.2 = (f32[32,16]{0,1:T(8,128)S(1)}, f32[32,16]{0,1:T(8,128)}, u32[]{:S(2)}) copy-start(f32[32,16]{0,1:T(8,128)} %param.14) | copy-start | bytes 6148
  12.4 6.7 %collective-permute-start.2 = (f32[137,128]{1,0:T(8,128)S(1)}, f32[137,128]{1,0:T(8,128)S(1)}, u32[]{:S(2)}, u32[]{:S(2)}) collective-permute-start(f32[137,128]{1,0:T(8,128)S(1)} %get-tuple-element.70), channel_id=1, source_target_pairs={{0,1},{1,0},{2,3},{3,2},{4,5},{5,4},{6,7},{7,6},{8,9},{9,8},{10,11... | collective-permute-start | bytes 210440 | tf_op jit(solution)/shard_map/ppermute | solution.py:725
  19.2 5.7 %collective-permute-start.3 = (f32[137,128]{1,0:T(8,128)S(1)}, f32[137,128]{1,0:T(8,128)S(1)}, u32[]{:S(2)}, u32[]{:S(2)}) collective-permute-start(f32[137,128]{1,0:T(8,128)S(1)} %select_select_fusion.1), channel_id=1, source_target_pairs={{0,2},{1,3},{2,0},{3,1},{4,6},{5,7},{6,4},{7,5},{8,10},{9,11},{10,... | collective-permute-start | bytes 210440 | tf_op jit(solution)/shard_map/ppermute | solution.py:725
  25.0 5.8 %collective-permute-start.4 = (f32[137,128]{1,0:T(8,128)S(1)}, f32[137,128]{1,0:T(8,128)S(1)}, u32[]{:S(2)}, u32[]{:S(2)}) collective-permute-start(f32[137,128]{1,0:T(8,128)S(1)} %select_select_fusion.refs_0_), channel_id=1, source_target_pairs={{0,4},{1,5},{2,6},{3,7},{4,0},{5,1},{6,2},{7,3},{8,12},{9,13},{10,... | collective-permute-start | bytes 210440 | tf_op jit(solution)/shard_map/ppermute | solution.py:725
  30.8 1.3 %collective-permute-start.5 = (f32[48,128]{1,0:T(8,128)S(1)}, f32[48,128]{1,0:T(8,128)S(1)}, u32[]{:S(2)}, u32[]{:S(2)}) collective-permute-start(f32[48,128]{1,0:T(8,128)S(1)} %get-tuple-element.72), channel_id=1, source_target_pairs={{0,8},{8,0},{16,24},{24,16},{1,9},{9,1},{17,25},{25,17},{2,10},{10... | collective-permute-start | bytes 73736 | tf_op jit(solution)/shard_map/ppermute | solution.py:756
  32.1 4.6 %collective-permute-start.6 = (f32[48,128]{1,0:T(8,128)S(1)}, f32[48,128]{1,0:T(8,128)S(1)}, u32[]{:S(2)}, u32[]{:S(2)}) collective-permute-start(f32[48,128]{1,0:T(8,128)S(1)} %add.17.refs_0_), channel_id=1, source_target_pairs={{0,16},{1,17},{2,18},{3,19},{4,20},{5,21},{6,22},{7,23},{8,24},{9,... | collective-permute-start | bytes 73736 | tf_op jit(solution)/shard_map/ppermute | solution.py:762
  33.6 3.8 %collective-permute-start.7 = (f32[48,128]{1,0:T(8,128)S(1)}, f32[48,128]{1,0:T(8,128)S(1)}, u32[]{:S(2)}, u32[]{:S(2)}) collective-permute-start(f32[48,128]{1,0:T(8,128)S(1)} %add.17.refs_0_), channel_id=1, source_target_pairs={{0,1},{1,0},{2,3},{3,2},{4,5},{5,4},{6,7},{7,6},{8,9},{9,8},{10,11... | collective-permute-start | bytes 73736 | tf_op jit(solution)/shard_map/ppermute | solution.py:762
  34.3 4.7 %collective-permute-start.8 = (f32[48,128]{1,0:T(8,128)S(1)}, f32[48,128]{1,0:T(8,128)S(1)}, u32[]{:S(2)}, u32[]{:S(2)}) collective-permute-start(f32[48,128]{1,0:T(8,128)S(1)} %add.17.refs_0_), channel_id=1, source_target_pairs={{0,17},{1,16},{2,19},{3,18},{4,21},{5,20},{6,23},{7,22},{8,25},{9,... | collective-permute-start | bytes 73736 | tf_op jit(solution)/shard_map/ppermute | solution.py:762

commit v7 on v6

--- a/solution.py
+++ b/solution.py
@@ -720,17 +720,31 @@
     index = lax.axis_index("tm")
     line = lax.broadcasted_iota(jnp.int32, payload.shape, 0)
     lane = lax.broadcasted_iota(jnp.int32, payload.shape, 1)
-    step = 1
+
+    def exchange(x, mask):
+        return lax.ppermute(x, "tm", [(i, i ^ mask) for i in range(count)])
+
+    def merge(mine, theirs, passed, step):
+        low = index % step
+        swap = ((low == 0) & (lane >= LANES // 2)) | ((low == step - 1) & (lane < LANES // 2))
+        return jnp.where(line < rows + 8, mine + theirs, jnp.where(swap, theirs, passed))
+
+    if count < 8:
+        payload = merge(payload, exchange(sent, 1), payload, 1)
+        step = 2
+    else:
+        near, across, far = exchange(sent, 1), exchange(payload, 2), exchange(sent, 3)
+        low = index % 2
+        swap = ((low == 0) & (lane >= LANES // 2)) | ((low == 1) & (lane < LANES // 2))
+        payload = jnp.where(
+            line < rows + 8, (payload + near) + (across + far), jnp.where(swap, far, near)
+        )
+        step = 4
     while True:
-        theirs = lax.ppermute(sent, "tm", [(i, i ^ step) for i in range(count)])
+        theirs = exchange(payload, step)
         if 2 * step == count:
             break
-        low = index % step
-        swap = ((low == 0) & (lane >= LANES // 2)) | ((low == step - 1) & (lane < LANES // 2))
-        payload = jnp.where(
-            line < rows + 8, payload + theirs, jnp.where(swap, theirs, payload)
-        )
-        sent = payload
+        payload = merge(payload, theirs, payload, step)
         step *= 2
 
     weights, aux = run(

time: 40.2 us -> 39.3 us (0.978)
  starting transfers between devices: 18.4 us -> 17.7 us
    ppermute x3 -> x4, starting transfers between devices: 11.1 us -> 10.4 us  [exchange(): return lax.ppermute(x, 'tm', [(i, i ^ mask) for i in range(count)])]
    ppermute x3, waiting for transfers between devices: 2.32 us -> 1.88 us  [partner(): return lax.ppermute(weights, ('dp', 'tm'), pairs)]
    ppermute x3 -> x4, waiting for transfers between devices: 6.98 us -> 7.3 us  [exchange(): return lax.ppermute(x, 'tm', [(i, i ^ mask) for i in range(count)])]
  transfers between devices with their start and end apart: 9 -> 10, of which waited for: 6 -> 5; matrix products, arithmetic and copies ran while one was open for 0% -> 0% of each run, Pallas kernels for 6% -> 6%
where the time goes in v7:
time: 39.3 us; the launch traced here: 39 us
  starting transfers between devices  17.7 us (45%)
  waiting for transfers between devices  10.4 us (26%)
  Pallas kernels  9.4 us (24%)
  between operations  0.79 us (2%)
  local copies, waits for them, and re-layouts  0.67 us (2%)
    ppermute x4, starting transfers between devices, exchange(): return lax.ppermute(x, 'tm', [(i, i ^ mask) for i in range(count)])  10.4 us
    pallas_call x6, Pallas kernels, run(): pl.pallas_call(kernel, out_shape=tuple((jax.ShapeDtypeStruct(*(x if isins...  9.4 us
    ppermute x4, waiting for transfers between devices, exchange(): return lax.ppermute(x, 'tm', [(i, i ^ mask) for i in range(count)])  7.3 us
    ppermute x3, starting transfers between devices, partner(): return lax.ppermute(weights, ('dp', 'tm'), pairs)  3.49 us
    ppermute x1, starting transfers between devices, local(): first = lax.ppermute(own, 'tm', pairs)  3.06 us
    ppermute x3, waiting for transfers between devices, partner(): return lax.ppermute(weights, ('dp', 'tm'), pairs)  1.88 us
    ppermute x1, waiting for transfers between devices, local(): lax.ppermute(weights, 'dp', [(i, i ^ step) for i in range(depth)])  1.18 us
  transfers between devices with their start and end apart: 10, of which 5 were waited for; matrix products, arithmetic and copies ran while one was open for 0% of the time, Pallas kernels for 6%

profile of v7, /device:TPU:0, one launch (start us, length us, event | category | flops | bytes accessed | tf_op | source)
XLA Modules:
  0.0 39.0 jit_solution(10674246096697055802)
XLA Ops:
  0.7 2.2 %own_decode.1 = (f32[24,128]{1,0:T(8,128)S(1)}, f32[64,512]{1,0:T(8,128)S(1)}, bf16[64,384]{1,0:T(8,128)(2,1)S(1)}, bf16[32,384]{1,0:T(8,128)(2,1)S(1)}, bf16[64...) custom-call(f32[1,64,512]{2,1,0:T(8,128)} %refs_0_.2, ...), custom_call_target="tpu_custom_call" | custom-call | tf_op jit(solution)/shard_map/own_decode/pallas_call | solution.py:625
  2.9 0.0 copy-start.1
  2.9 3.1 %collective-permute-start = (f32[24,128]{1,0:T(8,128)S(1)}, f32[24,128]{1,0:T(8,128)S(1)}, u32[]{:S(2)}, u32[]{:S(2)}) collective-permute-start(f32[24,128]{1,0:T(8,128)S(1)} %get-tuple-element.41.refs_4_.refs_0_), channel_id=1, source_target_pairs={{0,1},{1,0},{2,3},{3,2},{4,5},{5,4},{6,7},{7,6},{8,9},{9,8},{10,11... | collective-permute-start | bytes 36872 | tf_op jit(solution)/shard_map/ppermute | solution.py:693
  6.0 0.7 %collective-permute-start.1 = (f32[24,128]{1,0:T(8,128)S(1)}, f32[24,128]{1,0:T(8,128)S(1)}, u32[]{:S(2)}, u32[]{:S(2)}) collective-permute-start(f32[24,128]{1,0:T(8,128)S(1)} %get-tuple-element.41.refs_4_.refs_0_), channel_id=1, source_target_pairs={{1,2},{2,1},{3,4},{4,3},{5,6},{6,5},{9,10},{10,9},{11,12},{12,11},... | collective-permute-start | bytes 36872 | tf_op jit(solution)/shard_map/ppermute | solution.py:695
  6.6 0.0 copy-start.2
  6.7 0.6 %copy-done.2 = f32[32,16]{0,1:T(8,128)S(1)} copy-done((f32[32,16]{0,1:T(8,128)S(1)}, f32[32,16]{0,1:T(8,128)}, u32[]{:S(2)}) %copy-start.2) | copy-done | bytes 2072
  7.3 1.1 %backward_weights.1 = (bf16[64,384]{1,0:T(8,128)(2,1)S(1)}, bf16[64,192]{1,0:T(8,128)(2,1)S(1)}, bf16[32,192]{1,0:T(8,128)(2,1)S(1)}, bf16[64,24]{1,0:T(8,128)(2...) custom-call(f32[4,32,64]{2,1,0:T(8,128)S(1)} %copy-done, ...), custom_call_target="tpu_custom_call" | custom-call | tf_op jit(solution)/shard_map/backward_weights/pallas_call | solution.py:625
  8.5 4.0 %losses.1 = (f32[137,128]{1,0:T(8,128)S(1)}, f32[137,128]{1,0:T(8,128)S(1)}, f32[192,640]{1,0:T(8,128)S(1)}, f32[64,640]{1,0:T(8,128)S(1)}) custom-call(f32[24,128]{1,0:T(8,128)S(1)} %get-tuple-element.41.refs_4_.refs_0_, f32[24,128]{1,0:T(8,128)S(1)} %collective-permute-done.refs_1_, f32[24,128]{1,0:T(8,128)S(1)} %collective-permute-done.1.refs_2_, ...), custom_call_target="tpu_custom_call" | custom-call | tf_op jit(solution)/shard_map/losses/pallas_call | solution.py:625
  12.4 4.3 %collective-permute-start.2 = (f32[137,128]{1,0:T(8,128)S(1)}, f32[137,128]{1,0:T(8,128)S(1)}, u32[]{:S(2)}, u32[]{:S(2)}) collective-permute-start(f32[137,128]{1,0:T(8,128)S(1)} %get-tuple-element.70), channel_id=1, source_target_pairs={{0,1},{1,0},{2,3},{3,2},{4,5},{5,4},{6,7},{7,6},{8,9},{9,8},{10,11... | collective-permute-start | bytes 210440 | tf_op jit(solution)/shard_map/ppermute | solution.py:725
  16.8 2.7 %collective-permute-start.4 = (f32[137,128]{1,0:T(8,128)S(1)}, f32[137,128]{1,0:T(8,128)S(1)}, u32[]{:S(2)}, u32[]{:S(2)}) collective-permute-start(f32[137,128]{1,0:T(8,128)S(1)} %get-tuple-element.70), channel_id=1, source_target_pairs={{0,3},{1,2},{2,1},{3,0},{4,7},{5,6},{6,5},{7,4},{8,11},{9,10},{10,... | collective-permute-start | bytes 210440 | tf_op jit(solution)/shard_map/ppermute | solution.py:725
  19.5 4.3 %collective-permute-done.3 = f32[137,128]{1,0:T(8,128)S(1)} collective-permute-done((f32[137,128]{1,0:T(8,128)S(1)}, f32[137,128]{1,0:T(8,128)S(1)}, u32[]{:S(2)}, u32[]{:S(2)}) %collective-permute-start.3) | collective-permute-done | bytes 70176 | tf_op jit(solution)/shard_map/ppermute | solution.py:725
  23.8 0.1 select_select_fusion.refs_0_
  23.9 3.4 %collective-permute-start.5 = (f32[137,128]{1,0:T(8,128)S(1)}, f32[137,128]{1,0:T(8,128)S(1)}, u32[]{:S(2)}, u32[]{:S(2)}) collective-permute-start(f32[137,128]{1,0:T(8,128)S(1)} %select_select_fusion.refs_0_), channel_id=1, source_target_pairs={{0,4},{1,5},{2,6},{3,7},{4,0},{5,1},{6,2},{7,3},{8,12},{9,13},{10,... | collective-permute-start | bytes 210440 | tf_op jit(solution)/shard_map/ppermute | solution.py:725
  27.3 3.0 %collective-permute-done.5.refs_1_ = f32[137,128]{1,0:T(8,128)S(1)} collective-permute-done((f32[137,128]{1,0:T(8,128)S(1)}, f32[137,128]{1,0:T(8,128)S(1)}, u32[]{:S(2)}, u32[]{:S(2)}) %collective-permute-start.5) | collective-permute-done | bytes 70176 | tf_op jit(solution)/shard_map/ppermute | solution.py:725
  30.3 0.1 combine.1
  30.4 0.1 collective-permute-start.6
  30.5 1.2 %collective-permute-done.6 = f32[48,128]{1,0:T(8,128)S(1)} collective-permute-done((f32[48,128]{1,0:T(8,128)S(1)}, f32[48,128]{1,0:T(8,128)S(1)}, u32[]{:S(2)}, u32[]{:S(2)}) %collective-permute-start.6) | collective-permute-done | bytes 24608 | tf_op jit(solution)/shard_map/ppermute | solution.py:770
  31.7 1.5 %collective-permute-start.7 = (f32[48,128]{1,0:T(8,128)S(1)}, f32[48,128]{1,0:T(8,128)S(1)}, u32[]{:S(2)}, u32[]{:S(2)}) collective-permute-start(f32[48,128]{1,0:T(8,128)S(1)} %add.20.refs_0_), channel_id=1, source_target_pairs={{0,16},{1,17},{2,18},{3,19},{4,20},{5,21},{6,22},{7,23},{8,24},{9,... | collective-permute-start | bytes 73736 | tf_op jit(solution)/shard_map/ppermute | solution.py:776
  33.1 0.3 collective-permute-start.8
  33.4 1.7 %collective-permute-start.9 = (f32[48,128]{1,0:T(8,128)S(1)}, f32[48,128]{1,0:T(8,128)S(1)}, u32[]{:S(2)}, u32[]{:S(2)}) collective-permute-start(f32[48,128]{1,0:T(8,128)S(1)} %add.20.refs_0_), channel_id=1, source_target_pairs={{0,17},{1,16},{2,19},{3,18},{4,21},{5,20},{6,23},{7,22},{8,25},{9,... | collective-permute-start | bytes 73736 | tf_op jit(solution)/shard_map/ppermute | solution.py:776
  35.1 1.1 %latent.1 = f32[1,64,512]{2,1,0:T(8,128)} custom-call(f32[192,640]{1,0:T(8,128)S(1)} %get-tuple-element.67.refs_0_, f32[64,640]{1,0:T(8,128)S(1)} %get-tuple-element.68.refs_1_, bf16[64,384]{1,0:T(8,128)(2,1)S(1)} %get-tuple-element.59.refs_20_.refs_2_, f32[16,128]{1,0:T(8,128)S(1)} %get-tuple-element.71.refs_3_), custom_call_target="tpu_custom_call" | custom-call | tf_op jit(solution)/shard_map/latent/pallas_call | solution.py:625
  36.3 0.8 %collective-permute-done.8.refs_2_ = f32[48,128]{1,0:T(8,128)S(1)} collective-permute-done((f32[48,128]{1,0:T(8,128)S(1)}, f32[48,128]{1,0:T(8,128)S(1)}, u32[]{:S(2)}, u32[]{:S(2)}) %collective-permute-start.8) | collective-permute-done | bytes 24608 | tf_op jit(solution)/shard_map/ppermute | solution.py:776
  37.1 1.1 %collective-permute-done.9.refs_3_ = f32[48,128]{1,0:T(8,128)S(1)} collective-permute-done((f32[48,128]{1,0:T(8,128)S(1)}, f32[48,128]{1,0:T(8,128)S(1)}, u32[]{:S(2)}, u32[]{:S(2)}) %collective-permute-start.9) | collective-permute-done | bytes 24608 | tf_op jit(solution)/shard_map/ppermute | solution.py:776
  38.2 0.9 %final.1 = (f32[4,32,64]{2,1,0:T(8,128)}, f32[3,16,32]{2,1,0:T(8,128)}, f32[16,32]{1,0:T(8,128)}, f32[7,32]{1,0:T(8,128)}) custom-call(f32[48,128]{1,0:T(8,128)S(1)} %add.20.refs_0_, f32[48,128]{1,0:T(8,128)S(1)} %collective-permute-done.7.refs_1_, f32[48,128]{1,0:T(8,128)S(1)} %collective-permute-done.8.refs_2_, f32[48,128]{1,0:T(8,128)S(1)} %collective-permute-done.9.refs_3_), custom_call_target="tpu_custom_call" | custom-call | tf_op jit(solution)/shard_map/final/pallas_call | solution.py:625
  (14 shorter events, 0.0 us)
Async XLA Ops:
  0.6 6.0 %copy-start = (f32[4,32,64]{2,1,0:T(8,128)S(1)}, f32[4,32,64]{2,1,0:T(8,128)}, u32[]{:S(2)}) copy-start(f32[4,32,64]{2,1,0:T(8,128)} %refs_0_.3) | copy-start | bytes 98308
  0.6 6.0 %copy-start.3 = (f32[7,32]{1,0:T(8,128)S(1)}, f32[7,32]{1,0:T(8,128)}, u32[]{:S(2)}) copy-start(f32[7,32]{1,0:T(8,128)} %refs_3_.3) | copy-start | bytes 2692
  2.9 3.8 %copy-start.1 = (f32[3,16,32]{2,1,0:T(8,128)S(1)}, f32[3,16,32]{2,1,0:T(8,128)}, u32[]{:S(2)}) copy-start(f32[3,16,32]{2,1,0:T(8,128)} %refs_1_.3) | copy-start | bytes 18436
  2.9 5.6 %collective-permute-start = (f32[24,128]{1,0:T(8,128)S(1)}, f32[24,128]{1,0:T(8,128)S(1)}, u32[]{:S(2)}, u32[]{:S(2)}) collective-permute-start(f32[24,128]{1,0:T(8,128)S(1)} %get-tuple-element.41.refs_4_.refs_0_), channel_id=1, source_target_pairs={{0,1},{1,0},{2,3},{3,2},{4,5},{5,4},{6,7},{7,6},{8,9},{9,8},{10,11... | collective-permute-start | bytes 36872 | tf_op jit(solution)/shard_map/ppermute | solution.py:693
  6.0 2.5 %collective-permute-start.1 = (f32[24,128]{1,0:T(8,128)S(1)}, f32[24,128]{1,0:T(8,128)S(1)}, u32[]{:S(2)}, u32[]{:S(2)}) collective-permute-start(f32[24,128]{1,0:T(8,128)S(1)} %get-tuple-element.41.refs_4_.refs_0_), channel_id=1, source_target_pairs={{1,2},{2,1},{3,4},{4,3},{5,6},{6,5},{9,10},{10,9},{11,12},{12,11},... | collective-permute-start | bytes 36872 | tf_op jit(solution)/shard_map/ppermute | solution.py:695
  6.6 0.7 %copy-start.2 = (f32[32,16]{0,1:T(8,128)S(1)}, f32[32,16]{0,1:T(8,128)}, u32[]{:S(2)}) copy-start(f32[32,16]{0,1:T(8,128)} %param.14) | copy-start | bytes 6148
  12.4 7.1 %collective-permute-start.2 = (f32[137,128]{1,0:T(8,128)S(1)}, f32[137,128]{1,0:T(8,128)S(1)}, u32[]{:S(2)}, u32[]{:S(2)}) collective-permute-start(f32[137,128]{1,0:T(8,128)S(1)} %get-tuple-element.70), channel_id=1, source_target_pairs={{0,1},{1,0},{2,3},{3,2},{4,5},{5,4},{6,7},{7,6},{8,9},{9,8},{10,11... | collective-permute-start | bytes 210440 | tf_op jit(solution)/shard_map/ppermute | solution.py:725
  16.8 7.1 %collective-permute-start.4 = (f32[137,128]{1,0:T(8,128)S(1)}, f32[137,128]{1,0:T(8,128)S(1)}, u32[]{:S(2)}, u32[]{:S(2)}) collective-permute-start(f32[137,128]{1,0:T(8,128)S(1)} %get-tuple-element.70), channel_id=1, source_target_pairs={{0,3},{1,2},{2,1},{3,0},{4,7},{5,6},{6,5},{7,4},{8,11},{9,10},{10,... | collective-permute-start | bytes 210440 | tf_op jit(solution)/shard_map/ppermute | solution.py:725
  19.5 4.4 %collective-permute-start.3 = (f32[137,128]{1,0:T(8,128)S(1)}, f32[137,128]{1,0:T(8,128)S(1)}, u32[]{:S(2)}, u32[]{:S(2)}) collective-permute-start(f32[137,128]{1,0:T(8,128)S(1)} %get-tuple-element.69), channel_id=1, source_target_pairs={{0,2},{1,3},{2,0},{3,1},{4,6},{5,7},{6,4},{7,5},{8,10},{9,11},{10,... | collective-permute-start | bytes 210440 | tf_op jit(solution)/shard_map/ppermute | solution.py:725
  23.9 6.3 %collective-permute-start.5 = (f32[137,128]{1,0:T(8,128)S(1)}, f32[137,128]{1,0:T(8,128)S(1)}, u32[]{:S(2)}, u32[]{:S(2)}) collective-permute-start(f32[137,128]{1,0:T(8,128)S(1)} %select_select_fusion.refs_0_), channel_id=1, source_target_pairs={{0,4},{1,5},{2,6},{3,7},{4,0},{5,1},{6,2},{7,3},{8,12},{9,13},{10,... | collective-permute-start | bytes 210440 | tf_op jit(solution)/shard_map/ppermute | solution.py:725
  30.4 1.3 %collective-permute-start.6 = (f32[48,128]{1,0:T(8,128)S(1)}, f32[48,128]{1,0:T(8,128)S(1)}, u32[]{:S(2)}, u32[]{:S(2)}) collective-permute-start(f32[48,128]{1,0:T(8,128)S(1)} %get-tuple-element.72), channel_id=1, source_target_pairs={{0,8},{8,0},{16,24},{24,16},{1,9},{9,1},{17,25},{25,17},{2,10},{10... | collective-permute-start | bytes 73736 | tf_op jit(solution)/shard_map/ppermute | solution.py:770
  31.7 4.6 %collective-permute-start.7 = (f32[48,128]{1,0:T(8,128)S(1)}, f32[48,128]{1,0:T(8,128)S(1)}, u32[]{:S(2)}, u32[]{:S(2)}) collective-permute-start(f32[48,128]{1,0:T(8,128)S(1)} %add.20.refs_0_), channel_id=1, source_target_pairs={{0,16},{1,17},{2,18},{3,19},{4,20},{5,21},{6,22},{7,23},{8,24},{9,... | collective-permute-start | bytes 73736 | tf_op jit(solution)/shard_map/ppermute | solution.py:776
  33.1 3.9 %collective-permute-start.8 = (f32[48,128]{1,0:T(8,128)S(1)}, f32[48,128]{1,0:T(8,128)S(1)}, u32[]{:S(2)}, u32[]{:S(2)}) collective-permute-start(f32[48,128]{1,0:T(8,128)S(1)} %add.20.refs_0_), channel_id=1, source_target_pairs={{0,1},{1,0},{2,3},{3,2},{4,5},{5,4},{6,7},{7,6},{8,9},{9,8},{10,11... | collective-permute-start | bytes 73736 | tf_op jit(solution)/shard_map/ppermute | solution.py:776
  33.4 4.7 %collective-permute-start.9 = (f32[48,128]{1,0:T(8,128)S(1)}, f32[48,128]{1,0:T(8,128)S(1)}, u32[]{:S(2)}, u32[]{:S(2)}) collective-permute-start(f32[48,128]{1,0:T(8,128)S(1)} %add.20.refs_0_), channel_id=1, source_target_pairs={{0,17},{1,16},{2,19},{3,18},{4,21},{5,20},{6,23},{7,22},{8,25},{9,... | collective-permute-start | bytes 73736 | tf_op jit(solution)/shard_map/ppermute | solution.py:776
